TPU v7x, 256 devices: a whole 4x4x8 slice. The times are simulated.
256 devices in a mesh: sub: 64 (over z, y, core), grp: 4 (over x).
Axes of the slice: x: 4, y: 4, z: 8, core: 2. Of those that a mesh axis runs over, the one named last changes fastest.
Arguments:
- residual: float32 [16, 64, 4, 512], P(None, 'sub', 'grp'), may hold values from -6 to 6
- bounds: float32 [2], replicated, may hold values from 0.2 to 14, as said below
- local_inverse: bfloat16 [64, 4, 1024, 1024], P('sub', 'grp'), may hold values from -1 to 2
- corner_basis: bfloat16 [64, 4, 24, 1024], P('sub', 'grp'), may hold values from -1 to 1
- corner_map: int32 [64, 4, 24], P('sub', 'grp'), may hold values from 0 to 255
- coarse_inverse: float32 [256, 256], P(('sub', 'grp')), may hold values from -1 to 2, as said below
Outputs:
- basis: float32 [5, 16, 64, 4, 512], P(None, None, 'sub', 'grp')
- gram: float32 [80, 80], replicated
Inputs may be any that keep to these rules, and one draw needn't show every extreme that they name: bounds[0] lies in 0.2 to 0.4 and bounds[1] in 10 to 14. `coarse_inverse`: symmetric.
All inputs are finite; a program needn't handle non-finite values.
Results may differ from a plain program's by a relative error of at most 0.0022.
Values may be sent and summed in bfloat16 or wider, within the bound.
No kernel may reach another device: no remote copies, remote signals or barrier semaphores. Data moves between devices by JAX's collectives and lax.ppermute only.
A program may use at most 64 MiB of HBM per device.

v0:
```python
import functools

import jax
import jax.numpy as jnp
from jax import lax
from jax.experimental import pallas as pl
from jax.experimental.pallas import tpu as pltpu
from jax.sharding import Mesh
from jax.sharding import PartitionSpec as P


BLOCKS = 5
RHS = 16
FACE = 256
WIDTH = 4 * FACE
NCO = 256
SLOT = 32
SLOTS = 5 * SLOT
SUB = ("z", "y", "core")
PLANE = ("y", "x")
HIGH = lax.Precision.HIGHEST
F32, BF16 = jnp.float32, jnp.bfloat16
SEG = [slice(i * FACE, (i + 1) * FACE) for i in range(4)]


NN = (((1,), (0,)), ((), ()))
NT = (((1,), (1,)), ((), ()))


def hdot(a, b, dims=NN):
    return lax.dot_general(a, b, dims, precision=HIGH, preferred_element_type=F32)


def bdot(a, b, dims=NN):
    return lax.dot_general(a, b, dims, preferred_element_type=F32)


def dot2(a, exact, dims=NN):
    rows = a.shape[0]
    top = a.astype(BF16)
    low = (a - top.astype(F32)).astype(BF16)
    got = bdot(jnp.concatenate([top, low], axis=0), exact, dims)
    return got[:rows] + got[rows:]


def call(kernel, outs, args, spaces=None, scratch=(), limit=12, out_space=None, aliases=None):
    vmem = pl.BlockSpec(memory_space=pltpu.VMEM)
    out_spec = pl.BlockSpec(memory_space=out_space) if out_space is not None else vmem
    specs = [vmem if s is None else pl.BlockSpec(memory_space=s) for s in (spaces or [None] * len(args))]
    if spaces:
        args = [
            pltpu.with_memory_space_constraint(a, pltpu.HBM) if s is pltpu.HBM else a for a, s in zip(args, spaces)
        ]
    run = pl.pallas_call(
        kernel,
        out_shape=[jax.ShapeDtypeStruct(s, d) for s, d in outs],
        in_specs=specs,
        out_specs=[out_spec] * len(outs),
        scratch_shapes=list(scratch),
        input_output_aliases=aliases or {},
        compiler_params=pltpu.CompilerParams(vmem_limit_bytes=limit << 20),
    )
    return run(*args)


def along(x, axis, by):
    count = lax.axis_size(axis)
    return lax.ppermute(x, axis, [(i, (i + by) % count) for i in range(count)])


def exchange(x, axis):
    return lax.all_to_all(x, axis, split_axis=0, concat_axis=0, tiled=True)


def swapped(v):
    return along(v, "core", 1)


def in_pairs(v, axis, first):
    count = lax.axis_size(axis)
    pairs = []
    for i in range(first, first + count, 2):
        a, b = i % count, (i + 1) % count
        pairs += [(a, b), (b, a)]
    return lax.ppermute(v, axis, pairs)


def neighbours(sends):
    return [in_pairs(sends[0], SUB, 1), in_pairs(sends[1], "x", 1), in_pairs(sends[2], "x", 0), swapped(sends[3])]


def label_of(n):
    return ((n // 4) % 2) * 128 + ((n // 8) % 4 * 4 + n % 4) * 8 + n // 32


def pack_kernel(
    block_hbm, corners_hbm, ids_hbm,
    s0, s1, s2, s3, labels, block, corners, wide_block, given, packs, sems,
):
    copies = [
        pltpu.make_async_copy(src, dst, sems.at[i])
        for i, (src, dst) in enumerate(
            ((block_hbm, wide_block), (corners_hbm, corners), (ids_hbm, given))
        )
    ]
    for copy in copies:
        copy.start()
    for copy in copies:
        copy.wait()
    count = corners.shape[0]
    labels[...] = jnp.full((1, 256), -1, jnp.int32)
    labels[:, :count] = label_of(given[...])
    text = labels[...].astype(F32).astype(BF16)
    x = wide_block[...].reshape(RHS, 2 * FACE)
    block[...] = x
    top = x.astype(BF16)
    rest = (x - top.astype(F32)).astype(BF16)
    for i, s in enumerate(SEG):
        if i % 2 == 0:
            packs[i, :RHS] = top[:, SEG[i // 2]]
            packs[i, RHS : 2 * RHS] = rest[:, SEG[i // 2]]
        else:
            packs[i, : 2 * RHS] = jnp.zeros((2 * RHS, FACE), BF16)
        packs[i, 2 * RHS : 2 * RHS + count] = corners[:, s]
        packs[i, 2 * RHS + count :] = jnp.broadcast_to(text, (8, FACE))
    put_sends([packs[i] for i in range(4)], (s0, s1, s2, s3))


def terms_of(load, u, wide, spread_t):
    both = dot2(dot2(jnp.concatenate([load * 0.5, u], axis=0), wide, NT), spread_t, NT)
    return both[:RHS], both[RHS:]


def lifted(z, wide, spread_t):
    return dot2(dot2(z, spread_t), wide)


def either(axis, even_branch, odd_branch):
    even = lax.axis_index(axis) % 2 == 0
    pl.when(even)(even_branch)
    pl.when(jnp.logical_not(even))(odd_branch)


def on_core(zero_branch, other_branch):
    either("core", zero_branch, other_branch)


def put_pair(axis, up, low, first, second):
    def even():
        first[...] = up
        second[...] = low

    def odd():
        first[...] = low
        second[...] = up

    either(axis, even, odd)


def put_sends(faces, outs):
    put_pair("core", faces[0], faces[1], outs[3], outs[0])
    put_pair("x", faces[2], faces[3], outs[2], outs[1])


def put_image(u, out, sends):
    out[...] = u
    put_sends([u[:, s] for s in SEG], sends)


def arrived(refs):
    values = [r[...] for r in refs]
    if values[0].dtype != F32:
        values = [v.astype(F32) for v in values]
    zero, even = lax.axis_index("core") == 0, lax.axis_index("x") % 2 == 0
    return [
        jnp.where(zero, values[3], values[0]),
        jnp.where(zero, values[0], values[3]),
        jnp.where(even, values[2], values[1]),
        jnp.where(even, values[1], values[2]),
    ]


def split_by_core(first, second, keep, send):
    def zero():
        keep[...] = first
        send[...] = second

    def one():
        keep[...] = second
        send[...] = first

    on_core(zero, one)


def high_low(x):
    top = x.astype(BF16).astype(F32)
    return top, x - top


def start_kernel(
    block, r0, r1, r2, r3, corners, labels, inverse, load_out, wide_out, spread_out, image, s0, s1, s2, s3,
):
    count = corners.shape[0]
    k = 2 * RHS
    next_sub, prev_sub, next_grp, prev_grp = arrived((r0, r1, r2, r3))
    load_out[:, SEG[0]] = block[:, :FACE]
    load_out[:, SEG[1]] = -(prev_sub[:RHS] + prev_sub[RHS:k])
    load_out[:, SEG[2]] = block[:, FACE:]
    load_out[:, SEG[3]] = -(prev_grp[:RHS] + prev_grp[RHS:k])
    put_image(bdot(load_out[...].astype(BF16), inverse[...]), image, (s0, s1, s2, s3))
    wide_out[...] = jnp.zeros((SLOTS, WIDTH), BF16)
    wide_out[:count] = corners[...]
    others = (next_sub, prev_sub, next_grp, prev_grp)
    for i, other in enumerate(others):
        wide_out[SLOT * (i + 1) : SLOT * (i + 1) + count, SEG[i]] = (-other[k : k + count]).astype(BF16)
    lane = lax.broadcasted_iota(jnp.int32, (8, 256), 1)
    ids = jnp.where(lane < SLOT, jnp.broadcast_to(labels[...], (8, 256)).astype(F32), -1.0)
    for i, other in enumerate(others):
        moved = pltpu.roll(other[k + count :], SLOT * (i + 1), 1)
        mine = jnp.logical_and(lane >= SLOT * (i + 1), lane < SLOT * (i + 2))
        ids = jnp.where(mine, moved, ids)
    number = lax.broadcasted_iota(jnp.int32, (NCO, 256), 0).astype(F32)
    spread_out[...] = (number == ids[:1]).astype(F32).astype(BF16)


def row_kernel(bounds, row_hbm, coef, own_row, row, sem):
    copy = pltpu.make_async_copy(row_hbm, row, sem)
    copy.start()
    low, high = bounds[0], bounds[1]
    centre = jnp.full((1, WIDTH), (low + high) * 0.5, F32)
    inv = 1.0 / jnp.full((1, WIDTH), (high - low) * 0.5, F32)
    coef[...] = jnp.concatenate([centre, inv, 2.0 * inv, jnp.zeros((5, WIDTH), F32)], axis=0)
    n = lax.broadcasted_iota(jnp.int32, (NCO, NCO), 0)
    m = lax.broadcasted_iota(jnp.int32, (NCO, NCO), 1)
    order = (label_of(n) == m).astype(F32).astype(BF16)
    copy.wait()
    own_row[...] = dot2(jnp.broadcast_to(row[...], (RHS, NCO)), order)[:8]


def fetch_kernel(inverse_hbm, out, sem):
    copy = pltpu.make_async_copy(inverse_hbm, out, sem)
    copy.start()
    copy.wait()


def moment_kernel(load0, image, wide_in, spread, inverse, keep, send):
    wide, spread_t = wide_in[...], spread[:, :SLOTS]
    pairs0 = bdot(wide, wide, NT) * 0.5
    pairs1 = dot2(bdot(wide, inverse[...]), wide, NT)
    half = dot2(jnp.concatenate([pairs0, pairs1], axis=0), spread_t, NT)
    half = jnp.concatenate([half[:SLOTS], half[SLOTS:]], axis=1)
    top = half.astype(BF16)
    low = (half - top.astype(F32)).astype(BF16)
    both = bdot(spread_t, jnp.concatenate([top, low], axis=1))
    both = both[:, : 2 * NCO] + both[:, 2 * NCO :]
    w, g = terms_of(load0[...], image[...], wide, spread_t)

    def put(first, second):
        first[:NCO] = both[:, :NCO]
        first[NCO:] = w
        second[:NCO] = both[:, NCO:]
        second[NCO:] = g

    on_core(lambda: put(keep, send), lambda: put(send, keep))


def jumped(image, near):
    return [image[:, s] - n for s, n in zip(SEG, arrived(near), strict=True)]


def join_kernel(coef, load0, n0, n1, n2, n3, image, wide_in, spread, inverse, base1, g2):
    centre, inv, _ = terms_in(coef, WIDTH)
    jump = jnp.concatenate(jumped(image, (n0, n1, n2, n3)), axis=1)
    base1[...] = (jump - centre * load0[...]) * inv
    u = dot2(jump, inverse[...])
    g2[...] = dot2(dot2(u, wide_in[...], NT), spread[:, :SLOTS], NT)


def plane0_kernel(keep, got, g2, out):
    pieces = [high_low(keep[NCO:] + got[NCO:]), high_low(g2[...])]
    zero = jnp.zeros((4, NCO), F32)
    for p in range(16):
        rows = slice(16 * p, 16 * p + 16)
        small = [piece[part][p : p + 1] for part in range(2) for piece in pieces]
        out[p] = jnp.concatenate([keep[rows] + got[rows], *small, zero], axis=0).astype(BF16)


def summed(got):
    total = got[0].astype(F32)
    for p in range(1, got.shape[0]):
        total = total + got[p].astype(F32)
    return total


def depth0_kernel(got, own_row, out):
    total = summed(got)
    g = total[16:18] + total[18:20]
    rows = [total[:16], *high_low(g), *high_low(own_row[:1]), jnp.zeros((2, NCO), F32)]
    value = jnp.concatenate(rows, axis=0).astype(BF16)
    for q in range(8):
        out[q] = value


def spread0_kernel(got, out):
    every = [got[q].astype(F32) for q in range(8)]
    total = functools.reduce(jnp.add, every)
    g = total[16:18] + total[18:20]
    rows = [total[:16], *high_low(g), jnp.zeros((4, NCO), F32)]
    rows += [r[20:21] for r in every] + [r[21:22] for r in every]
    value = jnp.concatenate(rows, axis=0).astype(BF16)
    for p in range(16):
        out[p] = value


def collect0_kernel(got, out):
    g = []
    for p in range(16):
        out[16 * p : 16 * p + 16] = got[p, :16]
        g.append(got[p, 16:24].astype(F32))
        out[320 + 8 * p : 328 + 8 * p] = got[p, 24:32]
        out[448 + 8 * p : 456 + 8 * p] = got[p, 32:40]
    out[256:320] = jnp.concatenate([r[i : i + 1] for i in range(4) for r in g], axis=0).astype(BF16)


def terms_in(coef, width):
    return coef[0:1, :width], coef[1:2, :width], coef[2:3, :width]


def block1_kernel(
    own, got, base1, coef, spread, wide_in, inverse, coarse, w0, z0, load1, image1, s0, s1, s2, s3,
):
    _, inv, _ = terms_in(coef, WIDTH)

    def put(first, second):
        for half, part in ((slice(0, 128), first), (slice(128, 256), second)):
            coarse[half] = part[320:448].astype(F32) + part[448:576].astype(F32)
        w0[...] = first[256:272].astype(F32) + first[288:304].astype(F32)

    on_core(lambda: put(own, got), lambda: put(got, own))
    z = hdot(w0[...], coarse[...])
    z0[...] = z
    load1[...] = base1[...] + inv * lifted(z, wide_in[...], spread[:, :SLOTS])
    put_image(bdot(load1[...].astype(BF16), inverse[...]), image1, (s0, s1, s2, s3))


def solve_kernel(coef, own, got, z0, w0, coarse, spread, wide_in, w1, w2, lift1, lift2, m0, m1, g1, g2):
    centre, inv, alpha = terms_in(coef, NCO)

    def put(first, second):
        m0[...] = first[:NCO]
        m1[...] = second[:NCO]
        g1[...] = second[256:272].astype(F32) + second[288:304].astype(F32)
        parts = [part[i : i + RHS].astype(F32) for part in (first, second) for i in (272, 304)]
        g2[...] = functools.reduce(jnp.add, parts)

    on_core(lambda: put(own, got), lambda: put(got, own))
    z, w = z0[...], w0[...]
    after = (g1[...] + dot2(z, m0[...]) - centre * w) * inv
    w1[...] = after
    z1 = hdot(after, coarse[...])
    image = (g2[...] + dot2(z, m1[...]) - centre * g1[...]) * inv
    last = alpha * (image + dot2(z1, m0[...]) - centre * after) - w
    w2[...] = last
    z2 = hdot(last, coarse[...])
    lift = lifted(jnp.concatenate([z1, z2], axis=0), wide_in[...], spread[:, :SLOTS])
    lift1[...] = lift[:RHS]
    lift2[...] = lift[RHS:]


def next_kernel(
    coef, lift, n0, n1, n2, n3, image, before, now, inverse, load, image_out, s0, s1, s2, s3,
):
    centre, _, alpha = terms_in(coef, FACE)
    for s, jump in zip(SEG, jumped(image, (n0, n1, n2, n3)), strict=True):
        load[:, s] = alpha * (jump + lift[:, s] - centre * now[:, s]) - before[:, s]
    put_image(bdot(load[...].astype(BF16), inverse[...]), image_out, (s0, s1, s2, s3))


def last_kernel(
    coef, lift, n0, n1, n2, n3, image, before, now, inverse, load, image_out, low_sub, low_grp,
):
    centre, _, alpha = terms_in(coef, FACE)
    for s, jump in zip(SEG, jumped(image, (n0, n1, n2, n3)), strict=True):
        load[:, s] = alpha * (jump + lift[:, s] - centre * now[:, s]) - before[:, s]
    u = bdot(load[...].astype(BF16), inverse[...])
    image_out[...] = u
    low_sub[...] = u[:, SEG[1]]
    low_grp[...] = u[:, SEG[3]]


def terms_kernel(coef, block, load1, load2, load3, image, spread, wide_in, stack, partial4, keep, send):
    centre, _, alpha = terms_in(coef, FACE)
    w, g = terms_of(load3[...], image[...], wide_in[...], spread[:, :SLOTS])
    left, right = slice(0, FACE), slice(FACE, 2 * FACE)
    stack[:RHS] = block[...]
    for level, load in ((1, load1), (2, load2), (3, load3)):
        stack[level * RHS : (level + 1) * RHS, left] = load[:, SEG[0]]
        stack[level * RHS : (level + 1) * RHS, right] = load[:, SEG[2]]
    for half, s in ((left, SEG[0]), (right, SEG[2])):
        partial4[:, half] = alpha * (image[:, s] - centre * load3[:, s]) - load2[:, s]
    known = jnp.concatenate([stack[...], jnp.zeros((64, 2 * FACE), F32)], axis=0)
    terms = hdot(stack[...], known, NT)
    t = [terms[i * RHS : (i + 1) * RHS] for i in range(BLOCKS - 1)]
    lane = lax.broadcasted_iota(jnp.int32, (RHS, 128), 1)
    first = jnp.where(lane < 64, t[0], pltpu.roll(t[1], 48, 1))
    second = jnp.where(lane < 32, pltpu.roll(t[2], 96, 1), pltpu.roll(t[3], 112, 1))
    split_by_core(
        jnp.concatenate([w, jnp.zeros((RHS, NCO), F32)], axis=0),
        jnp.concatenate([g, jnp.concatenate([first, second], axis=1)], axis=0),
        keep,
        send,
    )


def coded(total):
    zero = lax.axis_index("core") == 0
    return jnp.where(zero, jnp.concatenate(high_low(total[:RHS]), axis=0), total)


def decoded(total):
    zero = lax.axis_index("core") == 0
    whole = jnp.concatenate([total[:RHS] + total[RHS:], jnp.zeros((RHS, NCO), F32)], axis=0)
    return jnp.where(zero, whole, total)


def gram_kernel(coef, stack, partial4, n0, n2, keep, got, known4, out):
    _, _, alpha = terms_in(coef, FACE)
    known4[:, :FACE] = partial4[:, :FACE] - alpha * n0[...]
    known4[:, FACE:] = partial4[:, FACE:] - alpha * n2[...]
    q = known4[...]
    row = hdot(q, jnp.concatenate([stack[...], q, jnp.zeros((48, 2 * FACE), F32)], axis=0), NT)
    row = jnp.concatenate([row[:8], row[8:]], axis=1)
    value = jnp.concatenate([coded(keep[...] + got[...]), row], axis=0).astype(BF16)
    for p in range(16):
        out[p] = value


def depth1_kernel(got, out):
    total = summed(got)
    value = jnp.concatenate([coded(decoded(total[: 2 * RHS])), total[2 * RHS :]], axis=0).astype(BF16)
    for q in range(8):
        out[q] = value


def sum_kernel(got, out):
    total = summed(got)
    out[: 2 * RHS] = decoded(total[: 2 * RHS])
    out[2 * RHS :] = total[2 * RHS :]


def store_kernel(stack, basis_hbm, basis, sem):
    for level in range(BLOCKS - 1):
        basis[level] = stack[level * RHS : (level + 1) * RHS].reshape(RHS, 1, 1, 2 * FACE)
    copy = pltpu.make_async_copy(basis, basis_hbm.at[: BLOCKS - 1], sem)
    copy.start()
    copy.wait()


def final_kernel(
    coef, own, got, coarse, matrix, w0, w1, w2, known4, spread, wide_in, stored,
    basis_hbm, gram_hbm, block4, gram, square, sems,
):
    centre, _, alpha = terms_in(coef, NCO)
    zero = lax.axis_index("core") == 0
    w3 = jnp.where(zero, own[:RHS], got[:RHS])
    second = jnp.where(zero, got[: 2 * RHS], own[: 2 * RHS])
    g3, packed = second[:RHS], second[RHS:]
    row = own[2 * RHS :] + got[2 * RHS :]
    row = jnp.concatenate([row[:, :128], row[:, 128:]], axis=0)
    z3 = hdot(w3, coarse[...])
    lift = lifted(z3, wide_in[...], spread[:, :SLOTS])
    value = jnp.concatenate(
        [known4[:, :FACE] + alpha * lift[:, SEG[0]], known4[:, FACE:] + alpha * lift[:, SEG[2]]], axis=1
    )
    block4[...] = value.reshape(RHS, 1, 1, 2 * FACE)
    late = pltpu.make_async_copy(block4, basis_hbm.at[BLOCKS - 1], sems.at[0])
    late.start()
    wk = alpha * (g3 - centre * w3) - w2[...]
    z_row = jnp.concatenate([jnp.zeros((64, NCO), F32), z3, jnp.zeros((48, NCO), F32)], axis=0)
    rows = jnp.concatenate([w0[...], w1[...], w2[...], w3, wk, dot2(z3, matrix[...])], axis=0)
    cross = hdot(rows, z_row, NT)
    alpha = alpha[:, :128]
    h0, h1 = packed[:, :128], packed[:, 128:]
    parts = [h0, pltpu.roll(h0, 80, 1), pltpu.roll(h1, 32, 1), pltpu.roll(h1, 16, 1)]
    lane = lax.broadcasted_iota(jnp.int32, (RHS, 128), 1)
    for i in range(BLOCKS - 1):
        rows = slice(i * RHS, (i + 1) * RHS)
        square[rows] = jnp.where(lane < 64, parts[i], 0.0) + alpha * cross[rows]
    last = slice(4 * RHS, 5 * RHS)
    own4 = alpha * cross[last]
    square[last] = alpha * alpha * cross[5 * RHS :]
    square[5 * RHS :] = jnp.zeros((48, 128), F32)
    column = jnp.concatenate([jnp.zeros((64, 128), F32), row, jnp.zeros((48, 128), F32)], axis=0)
    sided = jnp.concatenate([jnp.zeros((64, 128), F32), own4, jnp.zeros((48, 128), F32)], axis=0)
    up = square[...]
    r = lax.broadcasted_iota(jnp.int32, (128, 128), 0) // RHS
    c = lax.broadcasted_iota(jnp.int32, (128, 128), 1) // RHS
    whole = jnp.where(r <= c, up, up.T) + column + sided + sided.T
    whole = whole + jnp.where(jnp.logical_and(r < 4, c == 4), column.T, 0.0)
    gram[...] = (whole * (1.0 / (2 * FACE * 64)))[: BLOCKS * RHS, : BLOCKS * RHS]
    result = pltpu.make_async_copy(gram, gram_hbm, sems.at[1])
    result.start()
    late.wait()
    result.wait()


def body(residual, bounds, local_inverse, corner_basis, corner_map, coarse_inverse):
    inverse = local_inverse.reshape(WIDTH, WIDTH)
    corners = corner_basis.reshape(-1, WIDTH)
    count = corners.shape[0]
    face = ((RHS, FACE), F32)
    load = ((RHS, WIDTH), F32)
    small = ((RHS, NCO), F32)
    half = ((RHS, 2 * FACE), F32)
    square = ((NCO, NCO), F32)
    blocks = ((BLOCKS, RHS, 1, 1, 2 * FACE), F32)
    smem, hbm = pltpu.SMEM, pltpu.HBM

    *packs, labels, block, corners = call(
        pack_kernel,
        [((64, FACE), BF16)] * 4 + [((1, 256), jnp.int32), half, ((count, WIDTH), BF16)],
        [residual, corners, corner_map.reshape(1, count)],
        [hbm] * 3,
        [pltpu.VMEM((RHS, 1, 1, 2 * FACE), F32), pltpu.VMEM((1, count), jnp.int32), pltpu.VMEM((4, 64, FACE), BF16),
         pltpu.SemaphoreType.DMA((3,))],
    )
    near = neighbours(packs)
    (inverse,) = call(fetch_kernel, [((WIDTH, WIDTH), BF16)], [inverse], [hbm], [pltpu.SemaphoreType.DMA(())])
    coef, own_row = call(
        row_kernel,
        [((8, WIDTH), F32), ((8, NCO), F32)],
        [bounds, coarse_inverse],
        [smem, hbm],
        [pltpu.VMEM((1, NCO), F32), pltpu.SemaphoreType.DMA(())],
    )
    load0, wide, spread, image0, *sends = call(
        start_kernel,
        [load, ((SLOTS, WIDTH), BF16), ((NCO, 256), BF16), load, face, face, face, face],
        [block, *near, corners, labels, inverse],
    )
    near0 = neighbours(sends)
    keep, send = call(
        moment_kernel,
        [((272, NCO), F32), ((272, NCO), F32)],
        [load0, image0, wide, spread, inverse],
    )
    got = swapped(send)
    base1, g2 = call(join_kernel, [load, small], [coef, load0, *near0, image0, wide, spread, inverse])
    (v,) = call(plane0_kernel, [((16, 24, NCO), BF16)], [keep, got, g2])
    (v,) = call(depth0_kernel, [((8, 24, NCO), BF16)], [exchange(v, PLANE), own_row])
    (v,) = call(spread0_kernel, [((16, 40, NCO), BF16)], [exchange(v, "z")])
    (own,) = call(collect0_kernel, [((576, NCO), BF16)], [exchange(v, PLANE)])

    got = swapped(own)
    coarse, w0, z0, load1, image1, *sends = call(
        block1_kernel,
        [square, small, small, load, load, face, face, face, face],
        [own, got, base1, coef, spread, wide, inverse],
    )
    near1 = neighbours(sends)
    w1, w2, lift1, lift2, m0 = call(
        solve_kernel,
        [small, small, load, load, ((NCO, NCO), BF16)],
        [coef, own, got, z0, w0, coarse, spread, wide],
        scratch=[pltpu.VMEM((NCO, NCO), BF16), pltpu.VMEM((RHS, NCO), F32), pltpu.VMEM((RHS, NCO), F32)],
    )
    load2, image2, *sends = call(
        next_kernel,
        [load, load, face, face, face, face],
        [coef, lift1, *near1, image1, load0, load1, inverse],
    )
    near2 = neighbours(sends)
    load3, image3, low_sub, low_grp = call(
        last_kernel,
        [load, load, face, face],
        [coef, lift2, *near2, image2, load1, load2, inverse],
    )
    n0 = along(low_sub, SUB, -1)
    n2 = along(low_grp, "x", -1)
    stack, partial4, keep, send = call(
        terms_kernel,
        [((4 * RHS, 2 * FACE), F32), half, ((32, NCO), F32), ((32, NCO), F32)],
        [coef, block, load1, load2, load3, image3, spread, wide],
    )
    got = swapped(send)
    known4, v = call(
        gram_kernel,
        [half, ((16, 40, NCO), BF16)],
        [coef, stack, partial4, n0, n2, keep, got],
    )
    (stored,) = call(
        store_kernel,
        [blocks],
        [stack],
        scratch=[pltpu.VMEM((BLOCKS - 1, RHS, 1, 1, 2 * FACE), F32), pltpu.SemaphoreType.DMA(())],
        out_space=hbm,
    )
    (v,) = call(depth1_kernel, [((8, 40, NCO), BF16)], [exchange(v, PLANE)])
    (own,) = call(sum_kernel, [((40, NCO), F32)], [exchange(v, "z")])
    basis, gram = call(
        final_kernel,
        [blocks, ((BLOCKS * RHS, BLOCKS * RHS), F32)],
        [coef, own, swapped(own), coarse, m0, w0, w1, w2, known4, spread, wide, stored],
        [None] * 11 + [hbm],
        [pltpu.VMEM((RHS, 1, 1, 2 * FACE), F32), pltpu.VMEM((BLOCKS * RHS, BLOCKS * RHS), F32),
         pltpu.VMEM((128, 128), F32), pltpu.SemaphoreType.DMA((2,))],
        out_space=hbm,
        aliases={11: 0},
    )
    return basis, gram


def solution(mesh):
    split = Mesh(mesh.devices.reshape(8, 4, 2, mesh.shape["grp"]), ("z", "y", "core", "x"))
    in_specs = (
        P(None, SUB, "x", None),
        P(),
        P(SUB, "x", None, None),
        P(SUB, "x", None, None),
        P(SUB, "x", None),
        P(("z", "y", "core", "x"), None),
    )
    out_specs = (P(None, None, SUB, "x", None), P())
    return jax.shard_map(body, mesh=split, in_specs=in_specs, out_specs=out_specs, check_vma=False)
```

profile of v0, /device:TPU:1, one launch (start us, length us, event | category | flops | bytes accessed | tf_op | source)
XLA Modules:
  0.0 115.5 jit_solution(13876801108181170787)
XLA Ops:
  1.6 2.8 %collective-permute-start = (bf16[64,256]{1,0:T(8,128)(2,1)S(1)}, bf16[64,256]{1,0:T(8,128)(2,1)S(1)}, u32[]{:S(2)}, u32[]{:S(2)}) collective-permute-start(bf16[64,256]{1,0:T(8,128)(2,1)S(1)} %get-tuple-element.55), channel_id=1, source_target_pairs={{4,8},{8,4},{12,16},{16,12},{20,24},{24,20},{28,32},{32,28},{36,40... | collective-permute-start | bytes 98312 | tf_op jit(solution)/shard_map/ppermute | solution.py:85
  4.4 2.5 %collective-permute-start.1 = (bf16[64,256]{1,0:T(8,128)(2,1)S(1)}, bf16[64,256]{1,0:T(8,128)(2,1)S(1)}, u32[]{:S(2)}, u32[]{:S(2)}) collective-permute-start(bf16[64,256]{1,0:T(8,128)(2,1)S(1)} %get-tuple-element.56), channel_id=1, source_target_pairs={{1,2},{2,1},{3,0},{0,3},{5,6},{6,5},{7,4},{4,7},{9,10},{10,9},{11,... | collective-permute-start | bytes 98312 | tf_op jit(solution)/shard_map/ppermute | solution.py:85
  6.9 7.1 %collective-permute-start.3 = (bf16[64,256]{1,0:T(8,128)(2,1)S(1)}, bf16[64,256]{1,0:T(8,128)(2,1)S(1)}, u32[]{:S(2)}, u32[]{:S(2)}) collective-permute-start(bf16[64,256]{1,0:T(8,128)(2,1)S(1)} %get-tuple-element.58), channel_id=1, source_target_pairs={{0,4},{4,0},{1,5},{5,1},{2,6},{6,2},{3,7},{7,3},{8,12},{12,8},{9,1... | collective-permute-start | bytes 98312 | tf_op jit(solution)/shard_map/ppermute | solution.py:68
  13.9 1.6 %shard_map.79.inverse = bf16[1024,1024]{1,0:T(8,128)(2,1)S(1)} custom-call(bf16[1024,1024]{1,0:T(8,128)(2,1)} %bitcast.3), custom_call_target="tpu_custom_call" | custom-call | tf_op jit(solution)/shard_map/pallas_call | solution.py:63
  16.1 1.6 %shard_map.81 = (f32[272,256]{1,0:T(8,128)S(1)}, f32[272,256]{1,0:T(8,128)S(1)}) custom-call(f32[16,1024]{1,0:T(8,128)S(1)} %get-tuple-element.61.load0.before, f32[16,1024]{1,0:T(8,128)S(1)} %get-tuple-element.62.image, bf16[160,1024]{1,0:T(8,128)(2,1)S(1)} %get-tuple-element.63.wide_in, bf16[256,256]{1,0:T(8,128)(2,1)S(1)} %get-tuple-element.64.spread, ...), custom_call_target="tpu_custom_call" | custom-call | tf_op jit(solution)/shard_map/pallas_call | solution.py:63
  17.7 2.0 %collective-permute-start.4 = (f32[272,256]{1,0:T(8,128)S(1)}, f32[272,256]{1,0:T(8,128)S(1)}, u32[]{:S(2)}, u32[]{:S(2)}) collective-permute-start(f32[272,256]{1,0:T(8,128)S(1)} %get-tuple-element.66), channel_id=1, source_target_pairs={{0,4},{4,0},{1,5},{5,1},{2,6},{6,2},{3,7},{7,3},{8,12},{12,8},{9,1... | collective-permute-start | bytes 835592 | tf_op jit(solution)/shard_map/ppermute | solution.py:68
  20.6 2.3 %collective-permute-start.8 = (f32[16,256]{1,0:T(8,128)S(1)}, f32[16,256]{1,0:T(8,128)S(1)}, u32[]{:S(2)}, u32[]{:S(2)}) collective-permute-start(f32[16,256]{1,0:T(8,128)S(1)} %get-tuple-element.70), channel_id=1, source_target_pairs={{0,4},{4,0},{1,5},{5,1},{2,6},{6,2},{3,7},{7,3},{8,12},{12,8},{9,1... | collective-permute-start | bytes 49160 | tf_op jit(solution)/shard_map/ppermute | solution.py:68
  22.9 1.4 %shard_map.77 = (f32[8,1024]{1,0:T(8,128)S(1)}, f32[8,256]{1,0:T(8,128)S(1)}) custom-call(f32[2]{0:T(128)S(1)} %copy-done, f32[1,256]{1,0:T(1,128)} %row_hbm.1), custom_call_target="tpu_custom_call" | custom-call | tf_op jit(solution)/shard_map/pallas_call | solution.py:63
  25.1 11.3 %all_to_all.25.got = bf16[16,24,256]{2,1,0:T(8,128)(2,1)S(1)} all-to-all(bf16[16,24,256]{2,1,0:T(8,128)(2,1)S(1)} %shard_map.83), channel_id=1, replica_groups=mesh['z'=8,'y'=4,'core'=2,'x'=4] {'y','x'}, dimensions={0} | all-to-all | bytes 393216 | tf_op jit(solution)/shard_map/all_to_all | solution.py:72
  36.4 11.4 %all_to_all.26.got = bf16[8,24,256]{2,1,0:T(8,128)(2,1)S(1)} all-to-all(bf16[8,24,256]{2,1,0:T(8,128)(2,1)S(1)} %shard_map.84), channel_id=1, replica_groups=mesh['z'=8,'y'=4,'core'=2,'x'=4] {'z'}, dimensions={0} | all-to-all | bytes 196608 | tf_op jit(solution)/shard_map/all_to_all | solution.py:72
  47.9 10.9 %all_to_all.27.got = bf16[16,40,256]{2,1,0:T(8,128)(2,1)S(1)} all-to-all(bf16[16,40,256]{2,1,0:T(8,128)(2,1)S(1)} %shard_map.85), channel_id=1, replica_groups=mesh['z'=8,'y'=4,'core'=2,'x'=4] {'y','x'}, dimensions={0} | all-to-all | bytes 655360 | tf_op jit(solution)/shard_map/all_to_all | solution.py:72
  58.8 4.5 %collective-permute-start.9 = (bf16[576,256]{1,0:T(8,128)(2,1)S(1)}, bf16[576,256]{1,0:T(8,128)(2,1)S(1)}, u32[]{:S(2)}, u32[]{:S(2)}) collective-permute-start(bf16[576,256]{1,0:T(8,128)(2,1)S(1)} %shard_map.86.own), channel_id=1, source_target_pairs={{0,4},{4,0},{1,5},{5,1},{2,6},{6,2},{3,7},{7,3},{8,12},{12,8},{9,1... | collective-permute-start | bytes 884744 | tf_op jit(solution)/shard_map/ppermute | solution.py:68
  63.3 1.2 %collective-permute-done.9.got = bf16[576,256]{1,0:T(8,128)(2,1)S(1)} collective-permute-done((bf16[576,256]{1,0:T(8,128)(2,1)S(1)}, bf16[576,256]{1,0:T(8,128)(2,1)S(1)}, u32[]{:S(2)}, u32[]{:S(2)}) %collective-permute-start.9) | collective-permute-done | bytes 294944 | tf_op jit(solution)/shard_map/ppermute | solution.py:68
  67.5 1.4 %shard_map.88 = (f32[16,256]{1,0:T(8,128)S(1)}, f32[16,256]{1,0:T(8,128)S(1)}, f32[16,1024]{1,0:T(8,128)S(1)}, f32[16,1024]{1,0:T(8,128)S(1)}, bf16[256,256]{1,0:T(8,128)(2,1)S(1)}) custom-call(f32[8,1024]{1,0:T(8,128)S(1)} %get-tuple-element.53.coef, bf16[576,256]{1,0:T(8,128)(2,1)S(1)} %shard_map.86.own, bf16[576,256]{1,0:T(8,128)(2,1)S(1)} %collective-permute-done.9.got, ...), custom_call_target="tpu_custom_call" | custom-call | tf_op jit(solution)/shard_map/pallas_call | solution.py:63
  69.8 2.8 %collective-permute-start.14 = (f32[16,256]{1,0:T(8,128)S(1)}, f32[16,256]{1,0:T(8,128)S(1)}, u32[]{:S(2)}, u32[]{:S(2)}) collective-permute-start(f32[16,256]{1,0:T(8,128)S(1)} %get-tuple-element.86), channel_id=1, source_target_pairs={{4,8},{8,4},{12,16},{16,12},{20,24},{24,20},{28,32},{32,28},{36,40... | collective-permute-start | bytes 49160 | tf_op jit(solution)/shard_map/ppermute | solution.py:85
  72.6 1.7 %collective-permute-start.15 = (f32[16,256]{1,0:T(8,128)S(1)}, f32[16,256]{1,0:T(8,128)S(1)}, u32[]{:S(2)}, u32[]{:S(2)}) collective-permute-start(f32[16,256]{1,0:T(8,128)S(1)} %get-tuple-element.87), channel_id=1, source_target_pairs={{1,2},{2,1},{3,0},{0,3},{5,6},{6,5},{7,4},{4,7},{9,10},{10,9},{11,... | collective-permute-start | bytes 49160 | tf_op jit(solution)/shard_map/ppermute | solution.py:85
  74.3 2.5 %collective-permute-start.17 = (f32[16,256]{1,0:T(8,128)S(1)}, f32[16,256]{1,0:T(8,128)S(1)}, u32[]{:S(2)}, u32[]{:S(2)}) collective-permute-start(f32[16,256]{1,0:T(8,128)S(1)} %get-tuple-element.89), channel_id=1, source_target_pairs={{0,4},{4,0},{1,5},{5,1},{2,6},{6,2},{3,7},{7,3},{8,12},{12,8},{9,1... | collective-permute-start | bytes 49160 | tf_op jit(solution)/shard_map/ppermute | solution.py:68
  78.5 3.0 %collective-permute-start.20 = (f32[32,256]{1,0:T(8,128)S(1)}, f32[32,256]{1,0:T(8,128)S(1)}, u32[]{:S(2)}, u32[]{:S(2)}) collective-permute-start(f32[32,256]{1,0:T(8,128)S(1)} %get-tuple-element.98), channel_id=1, source_target_pairs={{0,4},{4,0},{1,5},{5,1},{2,6},{6,2},{3,7},{7,3},{8,12},{12,8},{9,1... | collective-permute-start | bytes 98312 | tf_op jit(solution)/shard_map/ppermute | solution.py:68
  81.6 1.2 %collective-permute-start.19 = (f32[16,256]{1,0:T(8,128)S(1)}, f32[16,256]{1,0:T(8,128)S(1)}, u32[]{:S(2)}, u32[]{:S(2)}) collective-permute-start(f32[16,256]{1,0:T(8,128)S(1)} %get-tuple-element.96), channel_id=1, source_target_pairs={{0,3},{1,0},{2,1},{3,2},{4,7},{5,4},{6,5},{7,6},{8,11},{9,8},{10,9... | collective-permute-start | bytes 49160 | tf_op jit(solution)/shard_map/ppermute | solution.py:68
  82.8 1.9 %collective-permute-done.18.n0 = f32[16,256]{1,0:T(8,128)S(1)} collective-permute-done((f32[16,256]{1,0:T(8,128)S(1)}, f32[16,256]{1,0:T(8,128)S(1)}, u32[]{:S(2)}, u32[]{:S(2)}) %collective-permute-start.18) | collective-permute-done | bytes 16416 | tf_op jit(solution)/shard_map/ppermute | solution.py:68
  84.9 11.2 %all_to_all.28.got = bf16[16,40,256]{2,1,0:T(8,128)(2,1)S(1)} all-to-all(bf16[16,40,256]{2,1,0:T(8,128)(2,1)S(1)} %get-tuple-element.99), channel_id=1, replica_groups=mesh['z'=8,'y'=4,'core'=2,'x'=4] {'y','x'}, dimensions={0} | all-to-all | bytes 655360 | tf_op jit(solution)/shard_map/all_to_all | solution.py:72
  96.2 14.5 %all_to_all.29.got = bf16[8,40,256]{2,1,0:T(8,128)(2,1)S(1)} all-to-all(bf16[8,40,256]{2,1,0:T(8,128)(2,1)S(1)} %shard_map.93), channel_id=1, replica_groups=mesh['z'=8,'y'=4,'core'=2,'x'=4] {'z'}, dimensions={0} | all-to-all | bytes 327680 | tf_op jit(solution)/shard_map/all_to_all | solution.py:72
  110.7 2.2 %collective-permute-start.21 = (f32[40,256]{1,0:T(8,128)S(1)}, f32[40,256]{1,0:T(8,128)S(1)}, u32[]{:S(2)}, u32[]{:S(2)}) collective-permute-start(f32[40,256]{1,0:T(8,128)S(1)} %shard_map.94.own), channel_id=1, source_target_pairs={{0,4},{4,0},{1,5},{5,1},{2,6},{6,2},{3,7},{7,3},{8,12},{12,8},{9,1... | collective-permute-start | bytes 122888 | tf_op jit(solution)/shard_map/ppermute | solution.py:68
  113.7 1.6 %shard_map.96 = (f32[5,16,1,1,512]{4,3,2,1,0:T(1,128)}, f32[80,80]{1,0:T(8,128)}) custom-call(f32[8,1024]{1,0:T(8,128)S(1)} %get-tuple-element.53.coef, f32[40,256]{1,0:T(8,128)S(1)} %shard_map.94.own, f32[40,256]{1,0:T(8,128)S(1)} %collective-permute-done.21.got, f32[256,256]{1,0:T(8,128)S(1)} %get-tuple-element.77.coarse, ...), custom_call_target="tpu_custom_call", output_to_operand_aliasing={{0}: (11, {})} | custom-call | tf_op jit(solution)/shard_map/pallas_call | solution.py:63
  (47 shorter events, 10.2 us)
Async XLA Ops:
  1.6 13.9 %collective-permute-start = (bf16[64,256]{1,0:T(8,128)(2,1)S(1)}, bf16[64,256]{1,0:T(8,128)(2,1)S(1)}, u32[]{:S(2)}, u32[]{:S(2)}) collective-permute-start(bf16[64,256]{1,0:T(8,128)(2,1)S(1)} %get-tuple-element.55), channel_id=1, source_target_pairs={{4,8},{8,4},{12,16},{16,12},{20,24},{24,20},{28,32},{32,28},{36,40... | collective-permute-start | bytes 98312 | tf_op jit(solution)/shard_map/ppermute | solution.py:85
  4.4 11.2 %collective-permute-start.1 = (bf16[64,256]{1,0:T(8,128)(2,1)S(1)}, bf16[64,256]{1,0:T(8,128)(2,1)S(1)}, u32[]{:S(2)}, u32[]{:S(2)}) collective-permute-start(bf16[64,256]{1,0:T(8,128)(2,1)S(1)} %get-tuple-element.56), channel_id=1, source_target_pairs={{1,2},{2,1},{3,0},{0,3},{5,6},{6,5},{7,4},{4,7},{9,10},{10,9},{11,... | collective-permute-start | bytes 98312 | tf_op jit(solution)/shard_map/ppermute | solution.py:85
  6.9 8.7 %collective-permute-start.2 = (bf16[64,256]{1,0:T(8,128)(2,1)S(1)}, bf16[64,256]{1,0:T(8,128)(2,1)S(1)}, u32[]{:S(2)}, u32[]{:S(2)}) collective-permute-start(bf16[64,256]{1,0:T(8,128)(2,1)S(1)} %get-tuple-element.57), channel_id=1, source_target_pairs={{0,1},{1,0},{2,3},{3,2},{4,5},{5,4},{6,7},{7,6},{8,9},{9,8},{10,11... | collective-permute-start | bytes 98312 | tf_op jit(solution)/shard_map/ppermute | solution.py:85
  6.9 8.7 %collective-permute-start.3 = (bf16[64,256]{1,0:T(8,128)(2,1)S(1)}, bf16[64,256]{1,0:T(8,128)(2,1)S(1)}, u32[]{:S(2)}, u32[]{:S(2)}) collective-permute-start(bf16[64,256]{1,0:T(8,128)(2,1)S(1)} %get-tuple-element.58), channel_id=1, source_target_pairs={{0,4},{4,0},{1,5},{5,1},{2,6},{6,2},{3,7},{7,3},{8,12},{12,8},{9,1... | collective-permute-start | bytes 98312 | tf_op jit(solution)/shard_map/ppermute | solution.py:68
  15.6 7.3 %copy-start = (f32[2]{0:T(128)S(1)}, f32[2]{0:T(128)}, u32[]{:S(2)}) copy-start(f32[2]{0:T(128)} %bounds.1) | copy-start | bytes 28
  17.7 7.3 %collective-permute-start.4 = (f32[272,256]{1,0:T(8,128)S(1)}, f32[272,256]{1,0:T(8,128)S(1)}, u32[]{:S(2)}, u32[]{:S(2)}) collective-permute-start(f32[272,256]{1,0:T(8,128)S(1)} %get-tuple-element.66), channel_id=1, source_target_pairs={{0,4},{4,0},{1,5},{5,1},{2,6},{6,2},{3,7},{7,3},{8,12},{12,8},{9,1... | collective-permute-start | bytes 835592 | tf_op jit(solution)/shard_map/ppermute | solution.py:68
  19.7 4.6 %collective-permute-start.5 = (f32[16,256]{1,0:T(8,128)S(1)}, f32[16,256]{1,0:T(8,128)S(1)}, u32[]{:S(2)}, u32[]{:S(2)}) collective-permute-start(f32[16,256]{1,0:T(8,128)S(1)} %get-tuple-element.67), channel_id=1, source_target_pairs={{4,8},{8,4},{12,16},{16,12},{20,24},{24,20},{28,32},{32,28},{36,40... | collective-permute-start | bytes 49160 | tf_op jit(solution)/shard_map/ppermute | solution.py:85
  19.7 4.6 %collective-permute-start.6 = (f32[16,256]{1,0:T(8,128)S(1)}, f32[16,256]{1,0:T(8,128)S(1)}, u32[]{:S(2)}, u32[]{:S(2)}) collective-permute-start(f32[16,256]{1,0:T(8,128)S(1)} %get-tuple-element.68), channel_id=1, source_target_pairs={{1,2},{2,1},{3,0},{0,3},{5,6},{6,5},{7,4},{4,7},{9,10},{10,9},{11,... | collective-permute-start | bytes 49160 | tf_op jit(solution)/shard_map/ppermute | solution.py:85
  20.6 3.7 %collective-permute-start.7 = (f32[16,256]{1,0:T(8,128)S(1)}, f32[16,256]{1,0:T(8,128)S(1)}, u32[]{:S(2)}, u32[]{:S(2)}) collective-permute-start(f32[16,256]{1,0:T(8,128)S(1)} %get-tuple-element.69), channel_id=1, source_target_pairs={{0,1},{1,0},{2,3},{3,2},{4,5},{5,4},{6,7},{7,6},{8,9},{9,8},{10,11... | collective-permute-start | bytes 49160 | tf_op jit(solution)/shard_map/ppermute | solution.py:85
  20.6 3.7 %collective-permute-start.8 = (f32[16,256]{1,0:T(8,128)S(1)}, f32[16,256]{1,0:T(8,128)S(1)}, u32[]{:S(2)}, u32[]{:S(2)}) collective-permute-start(f32[16,256]{1,0:T(8,128)S(1)} %get-tuple-element.70), channel_id=1, source_target_pairs={{0,4},{4,0},{1,5},{5,1},{2,6},{6,2},{3,7},{7,3},{8,12},{12,8},{9,1... | collective-permute-start | bytes 49160 | tf_op jit(solution)/shard_map/ppermute | solution.py:68
  58.8 5.7 %collective-permute-start.9 = (bf16[576,256]{1,0:T(8,128)(2,1)S(1)}, bf16[576,256]{1,0:T(8,128)(2,1)S(1)}, u32[]{:S(2)}, u32[]{:S(2)}) collective-permute-start(bf16[576,256]{1,0:T(8,128)(2,1)S(1)} %shard_map.86.own), channel_id=1, source_target_pairs={{0,4},{4,0},{1,5},{5,1},{2,6},{6,2},{3,7},{7,3},{8,12},{12,8},{9,1... | collective-permute-start | bytes 884744 | tf_op jit(solution)/shard_map/ppermute | solution.py:68
  65.5 3.4 %collective-permute-start.10 = (f32[16,256]{1,0:T(8,128)S(1)}, f32[16,256]{1,0:T(8,128)S(1)}, u32[]{:S(2)}, u32[]{:S(2)}) collective-permute-start(f32[16,256]{1,0:T(8,128)S(1)} %get-tuple-element.79), channel_id=1, source_target_pairs={{4,8},{8,4},{12,16},{16,12},{20,24},{24,20},{28,32},{32,28},{36,40... | collective-permute-start | bytes 49160 | tf_op jit(solution)/shard_map/ppermute | solution.py:85
  65.5 3.9 %collective-permute-start.11 = (f32[16,256]{1,0:T(8,128)S(1)}, f32[16,256]{1,0:T(8,128)S(1)}, u32[]{:S(2)}, u32[]{:S(2)}) collective-permute-start(f32[16,256]{1,0:T(8,128)S(1)} %get-tuple-element.80), channel_id=1, source_target_pairs={{1,2},{2,1},{3,0},{0,3},{5,6},{6,5},{7,4},{4,7},{9,10},{10,9},{11,... | collective-permute-start | bytes 49160 | tf_op jit(solution)/shard_map/ppermute | solution.py:85
  66.3 3.1 %collective-permute-start.12 = (f32[16,256]{1,0:T(8,128)S(1)}, f32[16,256]{1,0:T(8,128)S(1)}, u32[]{:S(2)}, u32[]{:S(2)}) collective-permute-start(f32[16,256]{1,0:T(8,128)S(1)} %get-tuple-element.81), channel_id=1, source_target_pairs={{0,1},{1,0},{2,3},{3,2},{4,5},{5,4},{6,7},{7,6},{8,9},{9,8},{10,11... | collective-permute-start | bytes 49160 | tf_op jit(solution)/shard_map/ppermute | solution.py:85
  66.3 3.1 %collective-permute-start.13 = (f32[16,256]{1,0:T(8,128)S(1)}, f32[16,256]{1,0:T(8,128)S(1)}, u32[]{:S(2)}, u32[]{:S(2)}) collective-permute-start(f32[16,256]{1,0:T(8,128)S(1)} %get-tuple-element.82), channel_id=1, source_target_pairs={{0,4},{4,0},{1,5},{5,1},{2,6},{6,2},{3,7},{7,3},{8,12},{12,8},{9,1... | collective-permute-start | bytes 49160 | tf_op jit(solution)/shard_map/ppermute | solution.py:68
  69.8 7.1 %collective-permute-start.14 = (f32[16,256]{1,0:T(8,128)S(1)}, f32[16,256]{1,0:T(8,128)S(1)}, u32[]{:S(2)}, u32[]{:S(2)}) collective-permute-start(f32[16,256]{1,0:T(8,128)S(1)} %get-tuple-element.86), channel_id=1, source_target_pairs={{4,8},{8,4},{12,16},{16,12},{20,24},{24,20},{28,32},{32,28},{36,40... | collective-permute-start | bytes 49160 | tf_op jit(solution)/shard_map/ppermute | solution.py:85
  72.6 4.3 %collective-permute-start.15 = (f32[16,256]{1,0:T(8,128)S(1)}, f32[16,256]{1,0:T(8,128)S(1)}, u32[]{:S(2)}, u32[]{:S(2)}) collective-permute-start(f32[16,256]{1,0:T(8,128)S(1)} %get-tuple-element.87), channel_id=1, source_target_pairs={{1,2},{2,1},{3,0},{0,3},{5,6},{6,5},{7,4},{4,7},{9,10},{10,9},{11,... | collective-permute-start | bytes 49160 | tf_op jit(solution)/shard_map/ppermute | solution.py:85
  74.3 2.9 %collective-permute-start.16 = (f32[16,256]{1,0:T(8,128)S(1)}, f32[16,256]{1,0:T(8,128)S(1)}, u32[]{:S(2)}, u32[]{:S(2)}) collective-permute-start(f32[16,256]{1,0:T(8,128)S(1)} %get-tuple-element.88), channel_id=1, source_target_pairs={{0,1},{1,0},{2,3},{3,2},{4,5},{5,4},{6,7},{7,6},{8,9},{9,8},{10,11... | collective-permute-start | bytes 49160 | tf_op jit(solution)/shard_map/ppermute | solution.py:85
  74.3 3.4 %collective-permute-start.17 = (f32[16,256]{1,0:T(8,128)S(1)}, f32[16,256]{1,0:T(8,128)S(1)}, u32[]{:S(2)}, u32[]{:S(2)}) collective-permute-start(f32[16,256]{1,0:T(8,128)S(1)} %get-tuple-element.89), channel_id=1, source_target_pairs={{0,4},{4,0},{1,5},{5,1},{2,6},{6,2},{3,7},{7,3},{8,12},{12,8},{9,1... | collective-permute-start | bytes 49160 | tf_op jit(solution)/shard_map/ppermute | solution.py:68
  78.5 6.2 %collective-permute-start.20 = (f32[32,256]{1,0:T(8,128)S(1)}, f32[32,256]{1,0:T(8,128)S(1)}, u32[]{:S(2)}, u32[]{:S(2)}) collective-permute-start(f32[32,256]{1,0:T(8,128)S(1)} %get-tuple-element.98), channel_id=1, source_target_pairs={{0,4},{4,0},{1,5},{5,1},{2,6},{6,2},{3,7},{7,3},{8,12},{12,8},{9,1... | collective-permute-start | bytes 98312 | tf_op jit(solution)/shard_map/ppermute | solution.py:68
  81.5 3.2 %collective-permute-start.18 = (f32[16,256]{1,0:T(8,128)S(1)}, f32[16,256]{1,0:T(8,128)S(1)}, u32[]{:S(2)}, u32[]{:S(2)}) collective-permute-start(f32[16,256]{1,0:T(8,128)S(1)} %get-tuple-element.95), channel_id=1, source_target_pairs={{0,252},{4,0},{8,4},{12,8},{16,12},{20,16},{24,20},{28,24},{32,28}... | collective-permute-start | bytes 49160 | tf_op jit(solution)/shard_map/ppermute | solution.py:68
  81.6 3.1 %collective-permute-start.19 = (f32[16,256]{1,0:T(8,128)S(1)}, f32[16,256]{1,0:T(8,128)S(1)}, u32[]{:S(2)}, u32[]{:S(2)}) collective-permute-start(f32[16,256]{1,0:T(8,128)S(1)} %get-tuple-element.96), channel_id=1, source_target_pairs={{0,3},{1,0},{2,1},{3,2},{4,7},{5,4},{6,5},{7,6},{8,11},{9,8},{10,9... | collective-permute-start | bytes 49160 | tf_op jit(solution)/shard_map/ppermute | solution.py:68
  110.7 3.0 %collective-permute-start.21 = (f32[40,256]{1,0:T(8,128)S(1)}, f32[40,256]{1,0:T(8,128)S(1)}, u32[]{:S(2)}, u32[]{:S(2)}) collective-permute-start(f32[40,256]{1,0:T(8,128)S(1)} %shard_map.94.own), channel_id=1, source_target_pairs={{0,4},{4,0},{1,5},{5,1},{2,6},{6,2},{3,7},{7,3},{8,12},{12,8},{9,1... | collective-permute-start | bytes 122888 | tf_op jit(solution)/shard_map/ppermute | solution.py:68
where the time goes:
time: 116 us; the launch traced here: 115 us
  blocking collectives  59.2 us (51%)
  starting transfers between devices  37.5 us (32%)
  Pallas kernels  13.1 us (11%)
  waiting for transfers between devices  4.64 us (4%)
    all_to_all x5, blocking collectives, exchange(): return lax.all_to_all(x, axis, split_axis=0, concat_axis=0, tiled=True)  59.2 us
    ppermute x10, starting transfers between devices, along(): return lax.ppermute(x, axis, [(i, (i + by) % count) for i in range(count)])  25.9 us
    pallas_call x20, Pallas kernels, call(): return run(*args)  13.1 us
    ppermute x12, starting transfers between devices, in_pairs(): return lax.ppermute(v, axis, pairs)  11.6 us
    ppermute x10, waiting for transfers between devices, along(): return lax.ppermute(x, axis, [(i, (i + by) % count) for i in range(count)])  3.76 us
  transfers between devices with their start and end apart: 22, of which 6 were waited for; matrix products, arithmetic and copies ran while one was open for 0% of the time, Pallas kernels for 5%

commit v1 on v0

--- a/solution.py
+++ b/solution.py
@@ -223,8 +223,10 @@
     spread_out[...] = (number == ids[:1]).astype(F32).astype(BF16)
 
 
-def row_kernel(bounds, row_hbm, coef, own_row, row, sem):
-    copy = pltpu.make_async_copy(row_hbm, row, sem)
+def fetch_kernel(bounds, inverse_hbm, row_hbm, out, coef, own_row, row, sems):
+    fetch = pltpu.make_async_copy(inverse_hbm, out, sems.at[0])
+    fetch.start()
+    copy = pltpu.make_async_copy(row_hbm, row, sems.at[1])
     copy.start()
     low, high = bounds[0], bounds[1]
     centre = jnp.full((1, WIDTH), (low + high) * 0.5, F32)
@@ -235,12 +237,7 @@
     order = (label_of(n) == m).astype(F32).astype(BF16)
     copy.wait()
     own_row[...] = dot2(jnp.broadcast_to(row[...], (RHS, NCO)), order)[:8]
-
-
-def fetch_kernel(inverse_hbm, out, sem):
-    copy = pltpu.make_async_copy(inverse_hbm, out, sem)
-    copy.start()
-    copy.wait()
+    fetch.wait()
 
 
 def moment_kernel(load0, image, wide_in, spread, inverse, keep, send):
@@ -487,16 +484,15 @@
         rows = slice(i * RHS, (i + 1) * RHS)
         square[rows] = jnp.where(lane < 64, parts[i], 0.0) + alpha * cross[rows]
     last = slice(4 * RHS, 5 * RHS)
-    own4 = alpha * cross[last]
-    square[last] = alpha * alpha * cross[5 * RHS :]
+    square[last] = alpha * alpha * cross[5 * RHS :] + jnp.where(lane < 64, 0.0, row)
     square[5 * RHS :] = jnp.zeros((48, 128), F32)
-    column = jnp.concatenate([jnp.zeros((64, 128), F32), row, jnp.zeros((48, 128), F32)], axis=0)
-    sided = jnp.concatenate([jnp.zeros((64, 128), F32), own4, jnp.zeros((48, 128), F32)], axis=0)
+    own4 = jnp.where(lane < 64, row, alpha * cross[last])
+    column = jnp.concatenate([jnp.zeros((64, 128), F32), own4, jnp.zeros((48, 128), F32)], axis=0)
     up = square[...]
     r = lax.broadcasted_iota(jnp.int32, (128, 128), 0) // RHS
     c = lax.broadcasted_iota(jnp.int32, (128, 128), 1) // RHS
-    whole = jnp.where(r <= c, up, up.T) + column + sided + sided.T
-    whole = whole + jnp.where(jnp.logical_and(r < 4, c == 4), column.T, 0.0)
+    sided = jnp.where(r < c, up, 0.0) + column
+    whole = jnp.where(r == c, up, 0.0) + sided + sided.T
     gram[...] = (whole * (1.0 / (2 * FACE * 64)))[: BLOCKS * RHS, : BLOCKS * RHS]
     result = pltpu.make_async_copy(gram, gram_hbm, sems.at[1])
     result.start()
@@ -525,13 +521,12 @@
          pltpu.SemaphoreType.DMA((3,))],
     )
     near = neighbours(packs)
-    (inverse,) = call(fetch_kernel, [((WIDTH, WIDTH), BF16)], [inverse], [hbm], [pltpu.SemaphoreType.DMA(())])
-    coef, own_row = call(
-        row_kernel,
-        [((8, WIDTH), F32), ((8, NCO), F32)],
-        [bounds, coarse_inverse],
-        [smem, hbm],
-        [pltpu.VMEM((1, NCO), F32), pltpu.SemaphoreType.DMA(())],
+    inverse, coef, own_row = call(
+        fetch_kernel,
+        [((WIDTH, WIDTH), BF16), ((8, WIDTH), F32), ((8, NCO), F32)],
+        [bounds, inverse, coarse_inverse],
+        [smem, hbm, hbm],
+        [pltpu.VMEM((1, NCO), F32), pltpu.SemaphoreType.DMA((2,))],
     )
     load0, wide, spread, image0, *sends = call(
         start_kernel,

time: 116 us -> 116 us (level)
  starting transfers between devices: 37.5 us -> 35.9 us
  blocking collectives: 59.2 us -> 60.4 us
    ppermute x10, starting transfers between devices: 25.9 us -> 24.1 us  [along(): return lax.ppermute(x, axis, [(i, (i + by) % count) for i in range(count)])]
    pallas_call x20 -> x19, Pallas kernels: 13.1 us -> 12.1 us  [call(): return run(*args)]
  transfers between devices with their start and end apart: 22 -> 22, of which waited for: 6 -> 9; matrix products, arithmetic and copies ran while one was open for 0% -> 0% of each run, Pallas kernels for 5% -> 4%
where the time goes in v1:
time: 116 us
  blocking collectives  60.4 us (52%)
  starting transfers between devices  35.9 us (31%)
  Pallas kernels  12.1 us (10%)
  waiting for transfers between devices  5.73 us (5%)
    all_to_all x5, blocking collectives, exchange(): return lax.all_to_all(x, axis, split_axis=0, concat_axis=0, tiled=True)  60.4 us
    ppermute x10, starting transfers between devices, along(): return lax.ppermute(x, axis, [(i, (i + by) % count) for i in range(count)])  24.1 us
    pallas_call x19, Pallas kernels, call(): return run(*args)  12.1 us
    ppermute x12, starting transfers between devices, in_pairs(): return lax.ppermute(v, axis, pairs)  11.8 us
    ppermute x10, waiting for transfers between devices, along(): return lax.ppermute(x, axis, [(i, (i + by) % count) for i in range(count)])  4 us
  transfers between devices with their start and end apart: 22, of which 9 were waited for; matrix products, arithmetic and copies ran while one was open for 0% of the time, Pallas kernels for 4%

profile of v1, /device:TPU:1, one launch (start us, length us, event | category | flops | bytes accessed | tf_op | source)
XLA Modules:
  0.0 115.8 jit_solution(16345739771873190087)
XLA Ops:
  0.6 1.0 shard_map.78
  1.6 2.8 %collective-permute-start = (bf16[64,256]{1,0:T(8,128)(2,1)S(1)}, bf16[64,256]{1,0:T(8,128)(2,1)S(1)}, u32[]{:S(2)}, u32[]{:S(2)}) collective-permute-start(bf16[64,256]{1,0:T(8,128)(2,1)S(1)} %get-tuple-element.56), channel_id=1, source_target_pairs={{4,8},{8,4},{12,16},{16,12},{20,24},{24,20},{28,32},{32,28},{36,40... | collective-permute-start | bytes 98312 | tf_op jit(solution)/shard_map/ppermute | solution.py:85
  4.4 2.5 %collective-permute-start.1 = (bf16[64,256]{1,0:T(8,128)(2,1)S(1)}, bf16[64,256]{1,0:T(8,128)(2,1)S(1)}, u32[]{:S(2)}, u32[]{:S(2)}) collective-permute-start(bf16[64,256]{1,0:T(8,128)(2,1)S(1)} %get-tuple-element.57), channel_id=1, source_target_pairs={{1,2},{2,1},{3,0},{0,3},{5,6},{6,5},{7,4},{4,7},{9,10},{10,9},{11,... | collective-permute-start | bytes 98312 | tf_op jit(solution)/shard_map/ppermute | solution.py:85
  6.9 7.1 %collective-permute-start.3 = (bf16[64,256]{1,0:T(8,128)(2,1)S(1)}, bf16[64,256]{1,0:T(8,128)(2,1)S(1)}, u32[]{:S(2)}, u32[]{:S(2)}) collective-permute-start(bf16[64,256]{1,0:T(8,128)(2,1)S(1)} %get-tuple-element.59), channel_id=1, source_target_pairs={{0,4},{4,0},{1,5},{5,1},{2,6},{6,2},{3,7},{7,3},{8,12},{12,8},{9,1... | collective-permute-start | bytes 98312 | tf_op jit(solution)/shard_map/ppermute | solution.py:68
  14.6 2.1 %shard_map.77 = (bf16[1024,1024]{1,0:T(8,128)(2,1)S(1)}, f32[8,1024]{1,0:T(8,128)S(1)}, f32[8,256]{1,0:T(8,128)S(1)}) custom-call(f32[2]{0:T(128)S(1)} %copy-done, bf16[1024,1024]{1,0:T(8,128)(2,1)} %bitcast.3, f32[1,256]{1,0:T(1,128)} %row_hbm.1), custom_call_target="tpu_custom_call" | custom-call | tf_op jit(solution)/shard_map/pallas_call | solution.py:63
  17.3 1.6 %shard_map.80 = (f32[272,256]{1,0:T(8,128)S(1)}, f32[272,256]{1,0:T(8,128)S(1)}) custom-call(f32[16,1024]{1,0:T(8,128)S(1)} %get-tuple-element.63.load0.before, f32[16,1024]{1,0:T(8,128)S(1)} %get-tuple-element.64.image, bf16[160,1024]{1,0:T(8,128)(2,1)S(1)} %get-tuple-element.65.wide_in, bf16[256,256]{1,0:T(8,128)(2,1)S(1)} %get-tuple-element.66.spread, ...), custom_call_target="tpu_custom_call" | custom-call | tf_op jit(solution)/shard_map/pallas_call | solution.py:63
  20.8 2.1 %collective-permute-start.8 = (f32[16,256]{1,0:T(8,128)S(1)}, f32[16,256]{1,0:T(8,128)S(1)}, u32[]{:S(2)}, u32[]{:S(2)}) collective-permute-start(f32[16,256]{1,0:T(8,128)S(1)} %get-tuple-element.72), channel_id=1, source_target_pairs={{0,4},{4,0},{1,5},{5,1},{2,6},{6,2},{3,7},{7,3},{8,12},{12,8},{9,1... | collective-permute-start | bytes 49160 | tf_op jit(solution)/shard_map/ppermute | solution.py:68
  24.5 11.2 %all_to_all.25.got = bf16[16,24,256]{2,1,0:T(8,128)(2,1)S(1)} all-to-all(bf16[16,24,256]{2,1,0:T(8,128)(2,1)S(1)} %shard_map.82), channel_id=1, replica_groups=mesh['z'=8,'y'=4,'core'=2,'x'=4] {'y','x'}, dimensions={0} | all-to-all | bytes 393216 | tf_op jit(solution)/shard_map/all_to_all | solution.py:72
  35.7 13.0 %all_to_all.26.got = bf16[8,24,256]{2,1,0:T(8,128)(2,1)S(1)} all-to-all(bf16[8,24,256]{2,1,0:T(8,128)(2,1)S(1)} %shard_map.83), channel_id=1, replica_groups=mesh['z'=8,'y'=4,'core'=2,'x'=4] {'z'}, dimensions={0} | all-to-all | bytes 196608 | tf_op jit(solution)/shard_map/all_to_all | solution.py:72
  48.8 10.6 %all_to_all.27.got = bf16[16,40,256]{2,1,0:T(8,128)(2,1)S(1)} all-to-all(bf16[16,40,256]{2,1,0:T(8,128)(2,1)S(1)} %shard_map.84), channel_id=1, replica_groups=mesh['z'=8,'y'=4,'core'=2,'x'=4] {'y','x'}, dimensions={0} | all-to-all | bytes 655360 | tf_op jit(solution)/shard_map/all_to_all | solution.py:72
  59.5 4.0 %collective-permute-start.9 = (bf16[576,256]{1,0:T(8,128)(2,1)S(1)}, bf16[576,256]{1,0:T(8,128)(2,1)S(1)}, u32[]{:S(2)}, u32[]{:S(2)}) collective-permute-start(bf16[576,256]{1,0:T(8,128)(2,1)S(1)} %shard_map.85.own), channel_id=1, source_target_pairs={{0,4},{4,0},{1,5},{5,1},{2,6},{6,2},{3,7},{7,3},{8,12},{12,8},{9,1... | collective-permute-start | bytes 884744 | tf_op jit(solution)/shard_map/ppermute | solution.py:68
  63.4 1.2 %collective-permute-done.9.got = bf16[576,256]{1,0:T(8,128)(2,1)S(1)} collective-permute-done((bf16[576,256]{1,0:T(8,128)(2,1)S(1)}, bf16[576,256]{1,0:T(8,128)(2,1)S(1)}, u32[]{:S(2)}, u32[]{:S(2)}) %collective-permute-start.9) | collective-permute-done | bytes 294944 | tf_op jit(solution)/shard_map/ppermute | solution.py:68
  66.5 1.1 collective-permute-start.13
  67.5 1.2 %shard_map.87 = (f32[16,256]{1,0:T(8,128)S(1)}, f32[16,256]{1,0:T(8,128)S(1)}, f32[16,1024]{1,0:T(8,128)S(1)}, f32[16,1024]{1,0:T(8,128)S(1)}, bf16[256,256]{1,0:T(8,128)(2,1)S(1)}) custom-call(f32[8,1024]{1,0:T(8,128)S(1)} %get-tuple-element.54.coef, bf16[576,256]{1,0:T(8,128)(2,1)S(1)} %shard_map.85.own, bf16[576,256]{1,0:T(8,128)(2,1)S(1)} %collective-permute-done.9.got, ...), custom_call_target="tpu_custom_call" | custom-call | tf_op jit(solution)/shard_map/pallas_call | solution.py:63
  70.0 2.9 %collective-permute-start.14 = (f32[16,256]{1,0:T(8,128)S(1)}, f32[16,256]{1,0:T(8,128)S(1)}, u32[]{:S(2)}, u32[]{:S(2)}) collective-permute-start(f32[16,256]{1,0:T(8,128)S(1)} %get-tuple-element.88), channel_id=1, source_target_pairs={{4,8},{8,4},{12,16},{16,12},{20,24},{24,20},{28,32},{32,28},{36,40... | collective-permute-start | bytes 49160 | tf_op jit(solution)/shard_map/ppermute | solution.py:85
  72.9 1.7 %collective-permute-start.15 = (f32[16,256]{1,0:T(8,128)S(1)}, f32[16,256]{1,0:T(8,128)S(1)}, u32[]{:S(2)}, u32[]{:S(2)}) collective-permute-start(f32[16,256]{1,0:T(8,128)S(1)} %get-tuple-element.89), channel_id=1, source_target_pairs={{1,2},{2,1},{3,0},{0,3},{5,6},{6,5},{7,4},{4,7},{9,10},{10,9},{11,... | collective-permute-start | bytes 49160 | tf_op jit(solution)/shard_map/ppermute | solution.py:85
  74.6 2.5 %collective-permute-start.17 = (f32[16,256]{1,0:T(8,128)S(1)}, f32[16,256]{1,0:T(8,128)S(1)}, u32[]{:S(2)}, u32[]{:S(2)}) collective-permute-start(f32[16,256]{1,0:T(8,128)S(1)} %get-tuple-element.91), channel_id=1, source_target_pairs={{0,4},{4,0},{1,5},{5,1},{2,6},{6,2},{3,7},{7,3},{8,12},{12,8},{9,1... | collective-permute-start | bytes 49160 | tf_op jit(solution)/shard_map/ppermute | solution.py:68
  78.8 3.0 %collective-permute-start.20 = (f32[32,256]{1,0:T(8,128)S(1)}, f32[32,256]{1,0:T(8,128)S(1)}, u32[]{:S(2)}, u32[]{:S(2)}) collective-permute-start(f32[32,256]{1,0:T(8,128)S(1)} %get-tuple-element.100), channel_id=1, source_target_pairs={{0,4},{4,0},{1,5},{5,1},{2,6},{6,2},{3,7},{7,3},{8,12},{12,8},{9,1... | collective-permute-start | bytes 98312 | tf_op jit(solution)/shard_map/ppermute | solution.py:68
  81.9 1.2 %collective-permute-start.19 = (f32[16,256]{1,0:T(8,128)S(1)}, f32[16,256]{1,0:T(8,128)S(1)}, u32[]{:S(2)}, u32[]{:S(2)}) collective-permute-start(f32[16,256]{1,0:T(8,128)S(1)} %get-tuple-element.98), channel_id=1, source_target_pairs={{0,3},{1,0},{2,1},{3,2},{4,7},{5,4},{6,5},{7,6},{8,11},{9,8},{10,9... | collective-permute-start | bytes 49160 | tf_op jit(solution)/shard_map/ppermute | solution.py:68
  83.1 1.9 %collective-permute-done.18.n0 = f32[16,256]{1,0:T(8,128)S(1)} collective-permute-done((f32[16,256]{1,0:T(8,128)S(1)}, f32[16,256]{1,0:T(8,128)S(1)}, u32[]{:S(2)}, u32[]{:S(2)}) %collective-permute-start.18) | collective-permute-done | bytes 16416 | tf_op jit(solution)/shard_map/ppermute | solution.py:68
  85.2 11.2 %all_to_all.28.got = bf16[16,40,256]{2,1,0:T(8,128)(2,1)S(1)} all-to-all(bf16[16,40,256]{2,1,0:T(8,128)(2,1)S(1)} %get-tuple-element.101), channel_id=1, replica_groups=mesh['z'=8,'y'=4,'core'=2,'x'=4] {'y','x'}, dimensions={0} | all-to-all | bytes 655360 | tf_op jit(solution)/shard_map/all_to_all | solution.py:72
  96.5 14.4 %all_to_all.29.got = bf16[8,40,256]{2,1,0:T(8,128)(2,1)S(1)} all-to-all(bf16[8,40,256]{2,1,0:T(8,128)(2,1)S(1)} %shard_map.92), channel_id=1, replica_groups=mesh['z'=8,'y'=4,'core'=2,'x'=4] {'z'}, dimensions={0} | all-to-all | bytes 327680 | tf_op jit(solution)/shard_map/all_to_all | solution.py:72
  110.9 2.3 %collective-permute-start.21 = (f32[40,256]{1,0:T(8,128)S(1)}, f32[40,256]{1,0:T(8,128)S(1)}, u32[]{:S(2)}, u32[]{:S(2)}) collective-permute-start(f32[40,256]{1,0:T(8,128)S(1)} %shard_map.93.own), channel_id=1, source_target_pairs={{0,4},{4,0},{1,5},{5,1},{2,6},{6,2},{3,7},{7,3},{8,12},{12,8},{9,1... | collective-permute-start | bytes 122888 | tf_op jit(solution)/shard_map/ppermute | solution.py:68
  114.0 1.6 %shard_map.95 = (f32[5,16,1,1,512]{4,3,2,1,0:T(1,128)}, f32[80,80]{1,0:T(8,128)}) custom-call(f32[8,1024]{1,0:T(8,128)S(1)} %get-tuple-element.54.coef, f32[40,256]{1,0:T(8,128)S(1)} %shard_map.93.own, f32[40,256]{1,0:T(8,128)S(1)} %collective-permute-done.21.got, f32[256,256]{1,0:T(8,128)S(1)} %get-tuple-element.79.coarse, ...), custom_call_target="tpu_custom_call", output_to_operand_aliasing={{0}: (11, {})} | custom-call | tf_op jit(solution)/shard_map/pallas_call | solution.py:63
  (46 shorter events, 10.8 us)
Async XLA Ops:
  1.6 15.1 %collective-permute-start = (bf16[64,256]{1,0:T(8,128)(2,1)S(1)}, bf16[64,256]{1,0:T(8,128)(2,1)S(1)}, u32[]{:S(2)}, u32[]{:S(2)}) collective-permute-start(bf16[64,256]{1,0:T(8,128)(2,1)S(1)} %get-tuple-element.56), channel_id=1, source_target_pairs={{4,8},{8,4},{12,16},{16,12},{20,24},{24,20},{28,32},{32,28},{36,40... | collective-permute-start | bytes 98312 | tf_op jit(solution)/shard_map/ppermute | solution.py:85
  4.4 12.4 %collective-permute-start.1 = (bf16[64,256]{1,0:T(8,128)(2,1)S(1)}, bf16[64,256]{1,0:T(8,128)(2,1)S(1)}, u32[]{:S(2)}, u32[]{:S(2)}) collective-permute-start(bf16[64,256]{1,0:T(8,128)(2,1)S(1)} %get-tuple-element.57), channel_id=1, source_target_pairs={{1,2},{2,1},{3,0},{0,3},{5,6},{6,5},{7,4},{4,7},{9,10},{10,9},{11,... | collective-permute-start | bytes 98312 | tf_op jit(solution)/shard_map/ppermute | solution.py:85
  6.9 9.9 %collective-permute-start.2 = (bf16[64,256]{1,0:T(8,128)(2,1)S(1)}, bf16[64,256]{1,0:T(8,128)(2,1)S(1)}, u32[]{:S(2)}, u32[]{:S(2)}) collective-permute-start(bf16[64,256]{1,0:T(8,128)(2,1)S(1)} %get-tuple-element.58), channel_id=1, source_target_pairs={{0,1},{1,0},{2,3},{3,2},{4,5},{5,4},{6,7},{7,6},{8,9},{9,8},{10,11... | collective-permute-start | bytes 98312 | tf_op jit(solution)/shard_map/ppermute | solution.py:85
  6.9 9.9 %collective-permute-start.3 = (bf16[64,256]{1,0:T(8,128)(2,1)S(1)}, bf16[64,256]{1,0:T(8,128)(2,1)S(1)}, u32[]{:S(2)}, u32[]{:S(2)}) collective-permute-start(bf16[64,256]{1,0:T(8,128)(2,1)S(1)} %get-tuple-element.59), channel_id=1, source_target_pairs={{0,4},{4,0},{1,5},{5,1},{2,6},{6,2},{3,7},{7,3},{8,12},{12,8},{9,1... | collective-permute-start | bytes 98312 | tf_op jit(solution)/shard_map/ppermute | solution.py:68
  13.9 0.7 copy-start
  18.9 5.6 %collective-permute-start.4 = (f32[272,256]{1,0:T(8,128)S(1)}, f32[272,256]{1,0:T(8,128)S(1)}, u32[]{:S(2)}, u32[]{:S(2)}) collective-permute-start(f32[272,256]{1,0:T(8,128)S(1)} %get-tuple-element.68), channel_id=1, source_target_pairs={{0,4},{4,0},{1,5},{5,1},{2,6},{6,2},{3,7},{7,3},{8,12},{12,8},{9,1... | collective-permute-start | bytes 835592 | tf_op jit(solution)/shard_map/ppermute | solution.py:68
  19.7 3.2 %collective-permute-start.5 = (f32[16,256]{1,0:T(8,128)S(1)}, f32[16,256]{1,0:T(8,128)S(1)}, u32[]{:S(2)}, u32[]{:S(2)}) collective-permute-start(f32[16,256]{1,0:T(8,128)S(1)} %get-tuple-element.69), channel_id=1, source_target_pairs={{4,8},{8,4},{12,16},{16,12},{20,24},{24,20},{28,32},{32,28},{36,40... | collective-permute-start | bytes 49160 | tf_op jit(solution)/shard_map/ppermute | solution.py:85
  19.7 3.8 %collective-permute-start.6 = (f32[16,256]{1,0:T(8,128)S(1)}, f32[16,256]{1,0:T(8,128)S(1)}, u32[]{:S(2)}, u32[]{:S(2)}) collective-permute-start(f32[16,256]{1,0:T(8,128)S(1)} %get-tuple-element.70), channel_id=1, source_target_pairs={{1,2},{2,1},{3,0},{0,3},{5,6},{6,5},{7,4},{4,7},{9,10},{10,9},{11,... | collective-permute-start | bytes 49160 | tf_op jit(solution)/shard_map/ppermute | solution.py:85
  20.6 2.9 %collective-permute-start.7 = (f32[16,256]{1,0:T(8,128)S(1)}, f32[16,256]{1,0:T(8,128)S(1)}, u32[]{:S(2)}, u32[]{:S(2)}) collective-permute-start(f32[16,256]{1,0:T(8,128)S(1)} %get-tuple-element.71), channel_id=1, source_target_pairs={{0,1},{1,0},{2,3},{3,2},{4,5},{5,4},{6,7},{7,6},{8,9},{9,8},{10,11... | collective-permute-start | bytes 49160 | tf_op jit(solution)/shard_map/ppermute | solution.py:85
  20.8 2.9 %collective-permute-start.8 = (f32[16,256]{1,0:T(8,128)S(1)}, f32[16,256]{1,0:T(8,128)S(1)}, u32[]{:S(2)}, u32[]{:S(2)}) collective-permute-start(f32[16,256]{1,0:T(8,128)S(1)} %get-tuple-element.72), channel_id=1, source_target_pairs={{0,4},{4,0},{1,5},{5,1},{2,6},{6,2},{3,7},{7,3},{8,12},{12,8},{9,1... | collective-permute-start | bytes 49160 | tf_op jit(solution)/shard_map/ppermute | solution.py:68
  59.5 5.2 %collective-permute-start.9 = (bf16[576,256]{1,0:T(8,128)(2,1)S(1)}, bf16[576,256]{1,0:T(8,128)(2,1)S(1)}, u32[]{:S(2)}, u32[]{:S(2)}) collective-permute-start(bf16[576,256]{1,0:T(8,128)(2,1)S(1)} %shard_map.85.own), channel_id=1, source_target_pairs={{0,4},{4,0},{1,5},{5,1},{2,6},{6,2},{3,7},{7,3},{8,12},{12,8},{9,1... | collective-permute-start | bytes 884744 | tf_op jit(solution)/shard_map/ppermute | solution.py:68
  65.6 3.2 %collective-permute-start.10 = (f32[16,256]{1,0:T(8,128)S(1)}, f32[16,256]{1,0:T(8,128)S(1)}, u32[]{:S(2)}, u32[]{:S(2)}) collective-permute-start(f32[16,256]{1,0:T(8,128)S(1)} %get-tuple-element.81), channel_id=1, source_target_pairs={{4,8},{8,4},{12,16},{16,12},{20,24},{24,20},{28,32},{32,28},{36,40... | collective-permute-start | bytes 49160 | tf_op jit(solution)/shard_map/ppermute | solution.py:85
  65.6 3.9 %collective-permute-start.11 = (f32[16,256]{1,0:T(8,128)S(1)}, f32[16,256]{1,0:T(8,128)S(1)}, u32[]{:S(2)}, u32[]{:S(2)}) collective-permute-start(f32[16,256]{1,0:T(8,128)S(1)} %get-tuple-element.82), channel_id=1, source_target_pairs={{1,2},{2,1},{3,0},{0,3},{5,6},{6,5},{7,4},{4,7},{9,10},{10,9},{11,... | collective-permute-start | bytes 49160 | tf_op jit(solution)/shard_map/ppermute | solution.py:85
  66.4 3.1 %collective-permute-start.12 = (f32[16,256]{1,0:T(8,128)S(1)}, f32[16,256]{1,0:T(8,128)S(1)}, u32[]{:S(2)}, u32[]{:S(2)}) collective-permute-start(f32[16,256]{1,0:T(8,128)S(1)} %get-tuple-element.83), channel_id=1, source_target_pairs={{0,1},{1,0},{2,3},{3,2},{4,5},{5,4},{6,7},{7,6},{8,9},{9,8},{10,11... | collective-permute-start | bytes 49160 | tf_op jit(solution)/shard_map/ppermute | solution.py:85
  66.5 3.1 %collective-permute-start.13 = (f32[16,256]{1,0:T(8,128)S(1)}, f32[16,256]{1,0:T(8,128)S(1)}, u32[]{:S(2)}, u32[]{:S(2)}) collective-permute-start(f32[16,256]{1,0:T(8,128)S(1)} %get-tuple-element.84), channel_id=1, source_target_pairs={{0,4},{4,0},{1,5},{5,1},{2,6},{6,2},{3,7},{7,3},{8,12},{12,8},{9,1... | collective-permute-start | bytes 49160 | tf_op jit(solution)/shard_map/ppermute | solution.py:68
  70.0 7.2 %collective-permute-start.14 = (f32[16,256]{1,0:T(8,128)S(1)}, f32[16,256]{1,0:T(8,128)S(1)}, u32[]{:S(2)}, u32[]{:S(2)}) collective-permute-start(f32[16,256]{1,0:T(8,128)S(1)} %get-tuple-element.88), channel_id=1, source_target_pairs={{4,8},{8,4},{12,16},{16,12},{20,24},{24,20},{28,32},{32,28},{36,40... | collective-permute-start | bytes 49160 | tf_op jit(solution)/shard_map/ppermute | solution.py:85
  72.9 4.3 %collective-permute-start.15 = (f32[16,256]{1,0:T(8,128)S(1)}, f32[16,256]{1,0:T(8,128)S(1)}, u32[]{:S(2)}, u32[]{:S(2)}) collective-permute-start(f32[16,256]{1,0:T(8,128)S(1)} %get-tuple-element.89), channel_id=1, source_target_pairs={{1,2},{2,1},{3,0},{0,3},{5,6},{6,5},{7,4},{4,7},{9,10},{10,9},{11,... | collective-permute-start | bytes 49160 | tf_op jit(solution)/shard_map/ppermute | solution.py:85
  74.6 2.9 %collective-permute-start.16 = (f32[16,256]{1,0:T(8,128)S(1)}, f32[16,256]{1,0:T(8,128)S(1)}, u32[]{:S(2)}, u32[]{:S(2)}) collective-permute-start(f32[16,256]{1,0:T(8,128)S(1)} %get-tuple-element.90), channel_id=1, source_target_pairs={{0,1},{1,0},{2,3},{3,2},{4,5},{5,4},{6,7},{7,6},{8,9},{9,8},{10,11... | collective-permute-start | bytes 49160 | tf_op jit(solution)/shard_map/ppermute | solution.py:85
  74.6 3.4 %collective-permute-start.17 = (f32[16,256]{1,0:T(8,128)S(1)}, f32[16,256]{1,0:T(8,128)S(1)}, u32[]{:S(2)}, u32[]{:S(2)}) collective-permute-start(f32[16,256]{1,0:T(8,128)S(1)} %get-tuple-element.91), channel_id=1, source_target_pairs={{0,4},{4,0},{1,5},{5,1},{2,6},{6,2},{3,7},{7,3},{8,12},{12,8},{9,1... | collective-permute-start | bytes 49160 | tf_op jit(solution)/shard_map/ppermute | solution.py:68
  78.8 6.2 %collective-permute-start.20 = (f32[32,256]{1,0:T(8,128)S(1)}, f32[32,256]{1,0:T(8,128)S(1)}, u32[]{:S(2)}, u32[]{:S(2)}) collective-permute-start(f32[32,256]{1,0:T(8,128)S(1)} %get-tuple-element.100), channel_id=1, source_target_pairs={{0,4},{4,0},{1,5},{5,1},{2,6},{6,2},{3,7},{7,3},{8,12},{12,8},{9,1... | collective-permute-start | bytes 98312 | tf_op jit(solution)/shard_map/ppermute | solution.py:68
  81.8 3.2 %collective-permute-start.18 = (f32[16,256]{1,0:T(8,128)S(1)}, f32[16,256]{1,0:T(8,128)S(1)}, u32[]{:S(2)}, u32[]{:S(2)}) collective-permute-start(f32[16,256]{1,0:T(8,128)S(1)} %get-tuple-element.97), channel_id=1, source_target_pairs={{0,252},{4,0},{8,4},{12,8},{16,12},{20,16},{24,20},{28,24},{32,28}... | collective-permute-start | bytes 49160 | tf_op jit(solution)/shard_map/ppermute | solution.py:68
  81.9 3.1 %collective-permute-start.19 = (f32[16,256]{1,0:T(8,128)S(1)}, f32[16,256]{1,0:T(8,128)S(1)}, u32[]{:S(2)}, u32[]{:S(2)}) collective-permute-start(f32[16,256]{1,0:T(8,128)S(1)} %get-tuple-element.98), channel_id=1, source_target_pairs={{0,3},{1,0},{2,1},{3,2},{4,7},{5,4},{6,5},{7,6},{8,11},{9,8},{10,9... | collective-permute-start | bytes 49160 | tf_op jit(solution)/shard_map/ppermute | solution.py:68
  110.9 3.2 %collective-permute-start.21 = (f32[40,256]{1,0:T(8,128)S(1)}, f32[40,256]{1,0:T(8,128)S(1)}, u32[]{:S(2)}, u32[]{:S(2)}) collective-permute-start(f32[40,256]{1,0:T(8,128)S(1)} %shard_map.93.own), channel_id=1, source_target_pairs={{0,4},{4,0},{1,5},{5,1},{2,6},{6,2},{3,7},{7,3},{8,12},{12,8},{9,1... | collective-permute-start | bytes 122888 | tf_op jit(solution)/shard_map/ppermute | solution.py:68

commit v2 on v1

--- a/solution.py
+++ b/solution.py
@@ -35,6 +35,16 @@
     return lax.dot_general(a, b, dims, preferred_element_type=F32)
 
 
+def halves_of(a):
+    top = a.astype(BF16)
+    return top, (a - top.astype(F32)).astype(BF16)
+
+
+def dot_halves(a, table):
+    rows = table.shape[0] // 2
+    return dot2(a, table[:rows]) + bdot(a.astype(BF16), table[rows:])
+
+
 def dot2(a, exact, dims=NN):
     rows = a.shape[0]
     top = a.astype(BF16)
@@ -43,9 +53,10 @@
     return got[:rows] + got[rows:]
 
 
-def call(kernel, outs, args, spaces=None, scratch=(), limit=12, out_space=None, aliases=None):
+def call(kernel, outs, args, spaces=None, scratch=(), limit=20, out_space=None, aliases=None):
     vmem = pl.BlockSpec(memory_space=pltpu.VMEM)
-    out_spec = pl.BlockSpec(memory_space=out_space) if out_space is not None else vmem
+    out_spaces = out_space if isinstance(out_space, list) else [out_space] * len(outs)
+    out_specs = [vmem if s is None else pl.BlockSpec(memory_space=s) for s in out_spaces]
     specs = [vmem if s is None else pl.BlockSpec(memory_space=s) for s in (spaces or [None] * len(args))]
     if spaces:
         args = [
@@ -53,9 +64,12 @@
         ]
     run = pl.pallas_call(
         kernel,
-        out_shape=[jax.ShapeDtypeStruct(s, d) for s, d in outs],
+        out_shape=[
+            pltpu.HBM(s, d) if space is pltpu.HBM else jax.ShapeDtypeStruct(s, d)
+            for (s, d), space in zip(outs, out_spaces)
+        ],
         in_specs=specs,
-        out_specs=[out_spec] * len(outs),
+        out_specs=out_specs,
         scratch_shapes=list(scratch),
         input_output_aliases=aliases or {},
         compiler_params=pltpu.CompilerParams(vmem_limit_bytes=limit << 20),
@@ -207,7 +221,7 @@
     load_out[:, SEG[1]] = -(prev_sub[:RHS] + prev_sub[RHS:k])
     load_out[:, SEG[2]] = block[:, FACE:]
     load_out[:, SEG[3]] = -(prev_grp[:RHS] + prev_grp[RHS:k])
-    put_image(bdot(load_out[...].astype(BF16), inverse[...]), image, (s0, s1, s2, s3))
+    put_image(dot2(load_out[...], inverse[...]), image, (s0, s1, s2, s3))
     wide_out[...] = jnp.zeros((SLOTS, WIDTH), BF16)
     wide_out[:count] = corners[...]
     others = (next_sub, prev_sub, next_grp, prev_grp)
@@ -240,10 +254,15 @@
     fetch.wait()
 
 
-def moment_kernel(load0, image, wide_in, spread, inverse, keep, send):
+def moment_kernel(load0, image, wide_in, spread, inverse, keep, send, lifted_image):
     wide, spread_t = wide_in[...], spread[:, :SLOTS]
     pairs0 = bdot(wide, wide, NT) * 0.5
-    pairs1 = dot2(bdot(wide, inverse[...]), wide, NT)
+    wide_image = bdot(wide, inverse[...])
+    top, low = halves_of(wide_image)
+    top, low = halves_of(bdot(spread_t, top) + bdot(spread_t, low))
+    lifted_image[:NCO] = top
+    lifted_image[NCO:] = low
+    pairs1 = dot2(wide_image, wide, NT)
     half = dot2(jnp.concatenate([pairs0, pairs1], axis=0), spread_t, NT)
     half = jnp.concatenate([half[:SLOTS], half[SLOTS:]], axis=1)
     top = half.astype(BF16)
@@ -265,12 +284,65 @@
     return [image[:, s] - n for s, n in zip(SEG, arrived(near), strict=True)]
 
 
-def join_kernel(coef, load0, n0, n1, n2, n3, image, wide_in, spread, inverse, base1, g2):
+def put_chain(u, lifts, sends):
+    top = u.astype(BF16)
+    low = (u - top.astype(F32)).astype(BF16)
+    put_sends([jnp.concatenate([top[:, s], low[:, s], lifts[:, s]], axis=0) for s in SEG], sends)
+
+
+def chain_jumps(u, own_lift, near):
+    far = arrived(near)
+    jump = jnp.concatenate([u[:, s] - (n[:RHS] + n[RHS : 2 * RHS]) for s, n in zip(SEG, far, strict=True)], axis=1)
+    lift = [own_lift(s) - n[2 * RHS :] for s, n in zip(SEG, far, strict=True)]
+    return jump, jnp.concatenate(lift, axis=1)
+
+
+def join_kernel(
+    coef, load0, n0, n1, n2, n3, image, wide_in, spread, inverse, lifted_image, base1, jump0, g2, image_x, s0, s1, s2, s3
+):
     centre, inv, _ = terms_in(coef, WIDTH)
     jump = jnp.concatenate(jumped(image, (n0, n1, n2, n3)), axis=1)
+    jump0[...] = jump
     base1[...] = (jump - centre * load0[...]) * inv
     u = dot2(jump, inverse[...])
+    image_x[...] = u
     g2[...] = dot2(dot2(u, wide_in[...], NT), spread[:, :SLOTS], NT)
+    put_chain(u, lifted_image[:NCO], (s0, s1, s2, s3))
+
+
+def chain1_kernel(
+    n0, n1, n2, n3, image_x, lifted_image, inverse_hbm,
+    jump1, lift1_hbm, image_x2, lifted2, s0, s1, s2, s3, inverse, lift1, sems,
+):
+    fetch = pltpu.make_async_copy(inverse_hbm, inverse, sems.at[0])
+    fetch.start()
+
+    def own_lift(s):
+        return lifted_image[:NCO, s].astype(F32) + lifted_image[NCO:, s].astype(F32)
+
+    jump, lift = chain_jumps(image_x[...], own_lift, (n0, n1, n2, n3))
+    jump1[...] = jump
+    top, low = halves_of(lift)
+    lift1[:NCO] = top
+    lift1[NCO:] = low
+    store = pltpu.make_async_copy(lift1, lift1_hbm, sems.at[1])
+    store.start()
+    fetch.wait()
+    u = dot2(jump, inverse[...])
+    image_x2[...] = u
+    both = bdot(lift1[...], inverse[...])
+    lifts = (both[:NCO] + both[NCO:]).astype(BF16)
+    lifted2[...] = lifts
+    put_chain(u, lifts, (s0, s1, s2, s3))
+    store.wait()
+
+
+def chain2_kernel(n0, n1, n2, n3, image_x2, lifted2, jump2, lift2):
+    jump, lift = chain_jumps(image_x2[...], lambda s: lifted2[:, s].astype(F32), (n0, n1, n2, n3))
+    jump2[...] = jump
+    top, low = halves_of(lift)
+    lift2[:NCO] = top
+    lift2[NCO:] = low
 
 
 def plane0_kernel(keep, got, g2, out):
@@ -323,35 +395,29 @@
     return coef[0:1, :width], coef[1:2, :width], coef[2:3, :width]
 
 
-def block1_kernel(
-    own, got, base1, coef, spread, wide_in, inverse, coarse, w0, z0, load1, image1, s0, s1, s2, s3,
+def march_kernel(
+    coef, own, got, load0, base1, jump0, jump1, jump2, chain2, spread, wide_in, chain1_hbm, inverse_hbm,
+    coarse, m0, w0, w1, w2, load1, load2, load3, image3, low_sub, low_grp, m1, g1, g2, chain1, inverse, sems,
 ):
-    _, inv, _ = terms_in(coef, WIDTH)
+    table = pltpu.make_async_copy(chain1_hbm, chain1, sems.at[0])
+    table.start()
+    fetch = pltpu.make_async_copy(inverse_hbm, inverse, sems.at[1])
+    fetch.start()
 
     def put(first, second):
         for half, part in ((slice(0, 128), first), (slice(128, 256), second)):
             coarse[half] = part[320:448].astype(F32) + part[448:576].astype(F32)
-        w0[...] = first[256:272].astype(F32) + first[288:304].astype(F32)
-
-    on_core(lambda: put(own, got), lambda: put(got, own))
-    z = hdot(w0[...], coarse[...])
-    z0[...] = z
-    load1[...] = base1[...] + inv * lifted(z, wide_in[...], spread[:, :SLOTS])
-    put_image(bdot(load1[...].astype(BF16), inverse[...]), image1, (s0, s1, s2, s3))
-
-
-def solve_kernel(coef, own, got, z0, w0, coarse, spread, wide_in, w1, w2, lift1, lift2, m0, m1, g1, g2):
-    centre, inv, alpha = terms_in(coef, NCO)
-
-    def put(first, second):
         m0[...] = first[:NCO]
         m1[...] = second[:NCO]
+        w0[...] = first[256:272].astype(F32) + first[288:304].astype(F32)
         g1[...] = second[256:272].astype(F32) + second[288:304].astype(F32)
         parts = [part[i : i + RHS].astype(F32) for part in (first, second) for i in (272, 304)]
         g2[...] = functools.reduce(jnp.add, parts)
 
     on_core(lambda: put(own, got), lambda: put(got, own))
-    z, w = z0[...], w0[...]
+    centre, inv, alpha = terms_in(coef, NCO)
+    w = w0[...]
+    z = hdot(w, coarse[...])
     after = (g1[...] + dot2(z, m0[...]) - centre * w) * inv
     w1[...] = after
     z1 = hdot(after, coarse[...])
@@ -359,28 +425,24 @@
     last = alpha * (image + dot2(z1, m0[...]) - centre * after) - w
     w2[...] = last
     z2 = hdot(last, coarse[...])
-    lift = lifted(jnp.concatenate([z1, z2], axis=0), wide_in[...], spread[:, :SLOTS])
-    lift1[...] = lift[:RHS]
-    lift2[...] = lift[RHS:]
-
-
-def next_kernel(
-    coef, lift, n0, n1, n2, n3, image, before, now, inverse, load, image_out, s0, s1, s2, s3,
-):
-    centre, _, alpha = terms_in(coef, FACE)
-    for s, jump in zip(SEG, jumped(image, (n0, n1, n2, n3)), strict=True):
-        load[:, s] = alpha * (jump + lift[:, s] - centre * now[:, s]) - before[:, s]
-    put_image(bdot(load[...].astype(BF16), inverse[...]), image_out, (s0, s1, s2, s3))
-
-
-def last_kernel(
-    coef, lift, n0, n1, n2, n3, image, before, now, inverse, load, image_out, low_sub, low_grp,
-):
-    centre, _, alpha = terms_in(coef, FACE)
-    for s, jump in zip(SEG, jumped(image, (n0, n1, n2, n3)), strict=True):
-        load[:, s] = alpha * (jump + lift[:, s] - centre * now[:, s]) - before[:, s]
-    u = bdot(load[...].astype(BF16), inverse[...])
-    image_out[...] = u
+    both = jnp.concatenate([z, z1, z2], axis=0)
+    lift = lifted(both, wide_in[...], spread[:, :SLOTS])
+    far = dot_halves(z, chain2[...])
+    table.wait()
+    near = dot_halves(both[: 2 * RHS], chain1[...])
+    centre, inv, alpha = terms_in(coef, WIDTH)
+    x1 = base1[...] + inv * lift[:RHS]
+    load1[...] = x1
+    j1 = inv * (jump1[...] + near[:RHS] - centre * jump0[...])
+    x2 = alpha * (j1 + lift[RHS : 2 * RHS] - centre * x1) - load0[...]
+    load2[...] = x2
+    jj1 = inv * (jump2[...] + far - centre * jump1[...])
+    j2 = alpha * (jj1 + near[RHS:] - centre * j1) - jump0[...]
+    x3 = alpha * (j2 + lift[2 * RHS :] - centre * x2) - x1
+    load3[...] = x3
+    fetch.wait()
+    u = bdot(x3.astype(BF16), inverse[...])
+    image3[...] = u
     low_sub[...] = u[:, SEG[1]]
     low_grp[...] = u[:, SEG[3]]
 
@@ -534,41 +596,43 @@
         [block, *near, corners, labels, inverse],
     )
     near0 = neighbours(sends)
-    keep, send = call(
+    keep, send, lifted_image = call(
         moment_kernel,
-        [((272, NCO), F32), ((272, NCO), F32)],
+        [((272, NCO), F32), ((272, NCO), F32), ((2 * NCO, WIDTH), BF16)],
         [load0, image0, wide, spread, inverse],
     )
     got = swapped(send)
-    base1, g2 = call(join_kernel, [load, small], [coef, load0, *near0, image0, wide, spread, inverse])
+    chain = ((2 * RHS + NCO, FACE), BF16)
+    table = ((2 * NCO, WIDTH), BF16)
+    base1, jump0, g2, image_x, *sends = call(
+        join_kernel,
+        [load, load, small, load, chain, chain, chain, chain],
+        [coef, load0, *near0, image0, wide, spread, inverse, lifted_image],
+    )
     (v,) = call(plane0_kernel, [((16, 24, NCO), BF16)], [keep, got, g2])
+    near1 = neighbours(sends)
     (v,) = call(depth0_kernel, [((8, 24, NCO), BF16)], [exchange(v, PLANE), own_row])
+    jump1, chain1, image_x2, lifted2, *sends = call(
+        chain1_kernel,
+        [load, table, load, ((NCO, WIDTH), BF16), chain, chain, chain, chain],
+        [*near1, image_x, lifted_image, local_inverse.reshape(WIDTH, WIDTH)],
+        [None] * 6 + [hbm],
+        [pltpu.VMEM((WIDTH, WIDTH), BF16), pltpu.VMEM((2 * NCO, WIDTH), BF16), pltpu.SemaphoreType.DMA((2,))],
+        out_space=[None, hbm] + [None] * 6,
+    )
+    near2 = neighbours(sends)
     (v,) = call(spread0_kernel, [((16, 40, NCO), BF16)], [exchange(v, "z")])
     (own,) = call(collect0_kernel, [((576, NCO), BF16)], [exchange(v, PLANE)])
-
-    got = swapped(own)
-    coarse, w0, z0, load1, image1, *sends = call(
-        block1_kernel,
-        [square, small, small, load, load, face, face, face, face],
-        [own, got, base1, coef, spread, wide, inverse],
-    )
-    near1 = neighbours(sends)
-    w1, w2, lift1, lift2, m0 = call(
-        solve_kernel,
-        [small, small, load, load, ((NCO, NCO), BF16)],
-        [coef, own, got, z0, w0, coarse, spread, wide],
-        scratch=[pltpu.VMEM((NCO, NCO), BF16), pltpu.VMEM((RHS, NCO), F32), pltpu.VMEM((RHS, NCO), F32)],
-    )
-    load2, image2, *sends = call(
-        next_kernel,
-        [load, load, face, face, face, face],
-        [coef, lift1, *near1, image1, load0, load1, inverse],
-    )
-    near2 = neighbours(sends)
-    load3, image3, low_sub, low_grp = call(
-        last_kernel,
-        [load, load, face, face],
-        [coef, lift2, *near2, image2, load1, load2, inverse],
+    jump2, chain2 = call(chain2_kernel, [load, table], [*near2, image_x2, lifted2])
+
+    coarse, m0, w0, w1, w2, load1, load2, load3, image3, low_sub, low_grp = call(
+        march_kernel,
+        [square, ((NCO, NCO), BF16), small, small, small, load, load, load, load, face, face],
+        [coef, own, swapped(own), load0, base1, jump0, jump1, jump2, chain2, spread, wide, chain1,
+         local_inverse.reshape(WIDTH, WIDTH)],
+        [None] * 11 + [hbm, hbm],
+        [pltpu.VMEM((NCO, NCO), BF16), pltpu.VMEM((RHS, NCO), F32), pltpu.VMEM((RHS, NCO), F32),
+         pltpu.VMEM((2 * NCO, WIDTH), BF16), pltpu.VMEM((WIDTH, WIDTH), BF16), pltpu.SemaphoreType.DMA((2,))],
     )
     n0 = along(low_sub, SUB, -1)
     n2 = along(low_grp, "x", -1)

time: 116 us -> 118 us (1.017)
  blocking collectives: 60.4 us -> 51.6 us
  Pallas kernels: 12.1 us -> 16.9 us
  starting transfers between devices: 35.9 us -> 40.2 us
  waiting for transfers between devices: 5.73 us -> 7.26 us
    all_to_all x5 -> x4, blocking collectives: 60.4 us -> 51.6 us  [exchange(): return lax.all_to_all(x, axis, split_axis=0, concat_axis=0, tiled=True)]
    pallas_call x19 -> x18, Pallas kernels: 12.1 us -> 16.9 us  [call(): return run(*args)]
    all_to_all x0 -> x1, starting transfers between devices: none -> 3.54 us  [exchange(): return lax.all_to_all(x, axis, split_axis=0, concat_axis=0, tiled=True)]
    ppermute x12, starting transfers between devices: 11.8 us -> 13.9 us  [in_pairs(): return lax.ppermute(v, axis, pairs)]
    ppermute x10, waiting for transfers between devices: 4 us -> 2.05 us  [along(): return lax.ppermute(x, axis, [(i, (i + by) % count) for i in range(count)])]
    ppermute x12, waiting for transfers between devices: 1.73 us -> 3.67 us  [in_pairs(): return lax.ppermute(v, axis, pairs)]
    all_to_all x0 -> x1, waiting for transfers between devices: none -> 1.54 us  [exchange(): return lax.all_to_all(x, axis, split_axis=0, concat_axis=0, tiled=True)]
    ppermute x10, starting transfers between devices: 24.1 us -> 22.7 us  [along(): return lax.ppermute(x, axis, [(i, (i + by) % count) for i in range(count)])]
  transfers between devices with their start and end apart: 22 -> 23, of which waited for: 9 -> 7; matrix products, arithmetic and copies ran while one was open for 0% -> 0% of each run, Pallas kernels for 4% -> 6%
where the time goes in v2:
time: 118 us
  blocking collectives  51.6 us (44%)
  starting transfers between devices  40.2 us (34%)
  Pallas kernels  16.9 us (14%)
  waiting for transfers between devices  7.26 us (6%)
    all_to_all x4, blocking collectives, exchange(): return lax.all_to_all(x, axis, split_axis=0, concat_axis=0, tiled=True)  51.6 us
    ppermute x10, starting transfers between devices, along(): return lax.ppermute(x, axis, [(i, (i + by) % count) for i in range(count)])  22.7 us
    pallas_call x18, Pallas kernels, call(): return run(*args)  16.9 us
    ppermute x12, starting transfers between devices, in_pairs(): return lax.ppermute(v, axis, pairs)  13.9 us
    ppermute x12, waiting for transfers between devices, in_pairs(): return lax.ppermute(v, axis, pairs)  3.67 us
    all_to_all x1, starting transfers between devices, exchange(): return lax.all_to_all(x, axis, split_axis=0, concat_axis=0, tiled=True)  3.54 us
  transfers between devices with their start and end apart: 23, of which 7 were waited for; matrix products, arithmetic and copies ran while one was open for 0% of the time, Pallas kernels for 6%

profile of v2, /device:TPU:1, one launch (start us, length us, event | category | flops | bytes accessed | tf_op | source)
XLA Modules:
  0.0 117.5 jit_solution(806931485308760646)
XLA Ops:
  1.6 2.8 %collective-permute-start = (bf16[64,256]{1,0:T(8,128)(2,1)S(1)}, bf16[64,256]{1,0:T(8,128)(2,1)S(1)}, u32[]{:S(2)}, u32[]{:S(2)}) collective-permute-start(bf16[64,256]{1,0:T(8,128)(2,1)S(1)} %get-tuple-element.60), channel_id=1, source_target_pairs={{4,8},{8,4},{12,16},{16,12},{20,24},{24,20},{28,32},{32,28},{36,40... | collective-permute-start | bytes 98312 | tf_op jit(solution)/shard_map/ppermute | solution.py:99
  4.4 2.5 %collective-permute-start.1 = (bf16[64,256]{1,0:T(8,128)(2,1)S(1)}, bf16[64,256]{1,0:T(8,128)(2,1)S(1)}, u32[]{:S(2)}, u32[]{:S(2)}) collective-permute-start(bf16[64,256]{1,0:T(8,128)(2,1)S(1)} %get-tuple-element.61), channel_id=1, source_target_pairs={{1,2},{2,1},{3,0},{0,3},{5,6},{6,5},{7,4},{4,7},{9,10},{10,9},{11,... | collective-permute-start | bytes 98312 | tf_op jit(solution)/shard_map/ppermute | solution.py:99
  6.9 7.1 %collective-permute-start.3 = (bf16[64,256]{1,0:T(8,128)(2,1)S(1)}, bf16[64,256]{1,0:T(8,128)(2,1)S(1)}, u32[]{:S(2)}, u32[]{:S(2)}) collective-permute-start(bf16[64,256]{1,0:T(8,128)(2,1)S(1)} %get-tuple-element.63), channel_id=1, source_target_pairs={{0,4},{4,0},{1,5},{5,1},{2,6},{6,2},{3,7},{7,3},{8,12},{12,8},{9,1... | collective-permute-start | bytes 98312 | tf_op jit(solution)/shard_map/ppermute | solution.py:82
  14.6 2.1 %shard_map.77 = (bf16[1024,1024]{1,0:T(8,128)(2,1)S(1)}, f32[8,1024]{1,0:T(8,128)S(1)}, f32[8,256]{1,0:T(8,128)S(1)}) custom-call(f32[2]{0:T(128)S(1)} %copy-done, bf16[1024,1024]{1,0:T(8,128)(2,1)} %bitcast.3, f32[1,256]{1,0:T(1,128)} %row_hbm.1), custom_call_target="tpu_custom_call" | custom-call | tf_op jit(solution)/shard_map/pallas_call | solution.py:77
  17.4 2.0 %shard_map.80 = (f32[272,256]{1,0:T(8,128)S(1)}, f32[272,256]{1,0:T(8,128)S(1)}, bf16[512,1024]{1,0:T(8,128)(2,1)S(1)}) custom-call(f32[16,1024]{1,0:T(8,128)S(1)} %get-tuple-element.67.load0, f32[16,1024]{1,0:T(8,128)S(1)} %get-tuple-element.68.image, bf16[160,1024]{1,0:T(8,128)(2,1)S(1)} %get-tuple-element.69.wide_in, ...), custom_call_target="tpu_custom_call" | custom-call | tf_op jit(solution)/shard_map/pallas_call | solution.py:77
  21.3 2.1 %collective-permute-start.8 = (f32[16,256]{1,0:T(8,128)S(1)}, f32[16,256]{1,0:T(8,128)S(1)}, u32[]{:S(2)}, u32[]{:S(2)}) collective-permute-start(f32[16,256]{1,0:T(8,128)S(1)} %get-tuple-element.76), channel_id=1, source_target_pairs={{0,4},{4,0},{1,5},{5,1},{2,6},{6,2},{3,7},{7,3},{8,12},{12,8},{9,1... | collective-permute-start | bytes 49160 | tf_op jit(solution)/shard_map/ppermute | solution.py:82
  25.1 11.2 %all_to_all.25.got = bf16[16,24,256]{2,1,0:T(8,128)(2,1)S(1)} all-to-all(bf16[16,24,256]{2,1,0:T(8,128)(2,1)S(1)} %shard_map.82), channel_id=1, replica_groups=mesh['z'=8,'y'=4,'core'=2,'x'=4] {'y','x'}, dimensions={0} | all-to-all | bytes 393216 | tf_op jit(solution)/shard_map/all_to_all | solution.py:86
  36.3 13.0 %all_to_all.26.got = bf16[8,24,256]{2,1,0:T(8,128)(2,1)S(1)} all-to-all(bf16[8,24,256]{2,1,0:T(8,128)(2,1)S(1)} %shard_map.83), channel_id=1, replica_groups=mesh['z'=8,'y'=4,'core'=2,'x'=4] {'z'}, dimensions={0} | all-to-all | bytes 196608 | tf_op jit(solution)/shard_map/all_to_all | solution.py:86
  50.1 3.5 %all-to-all-start.2 = ((bf16[16,40,256]{2,1,0:T(8,128)(2,1)}), bf16[16,40,256]{2,1,0:T(8,128)(2,1)S(1)}, u32[]{:S(2)}, u32[]{:S(2)}) async-start(bf16[16,40,256]{2,1,0:T(8,128)(2,1)} %shard_map.84), calls=%async_computation.2 | async-start | bytes 655360 | tf_op jit(solution)/shard_map/all_to_all | solution.py:86
  53.6 3.9 %collective-permute-start.10 = (bf16[288,256]{1,0:T(8,128)(2,1)S(1)}, bf16[288,256]{1,0:T(8,128)(2,1)S(1)}, u32[]{:S(2)}, u32[]{:S(2)}) collective-permute-start(bf16[288,256]{1,0:T(8,128)(2,1)S(1)} %get-tuple-element.82), channel_id=1, source_target_pairs={{4,8},{8,4},{12,16},{16,12},{20,24},{24,20},{28,32},{32,28},{36,40... | collective-permute-start | bytes 442376 | tf_op jit(solution)/shard_map/ppermute | solution.py:99
  57.5 2.4 %collective-permute-start.11 = (bf16[288,256]{1,0:T(8,128)(2,1)S(1)}, bf16[288,256]{1,0:T(8,128)(2,1)S(1)}, u32[]{:S(2)}, u32[]{:S(2)}) collective-permute-start(bf16[288,256]{1,0:T(8,128)(2,1)S(1)} %get-tuple-element.83), channel_id=1, source_target_pairs={{1,2},{2,1},{3,0},{0,3},{5,6},{6,5},{7,4},{4,7},{9,10},{10,9},{11,... | collective-permute-start | bytes 442376 | tf_op jit(solution)/shard_map/ppermute | solution.py:99
  60.0 1.5 %all-to-all-done.2.got = bf16[16,40,256]{2,1,0:T(8,128)(2,1)S(1)} async-done(((bf16[16,40,256]{2,1,0:T(8,128)(2,1)}), bf16[16,40,256]{2,1,0:T(8,128)(2,1)S(1)}, u32[]{:S(2)}, u32[]{:S(2)}) %all-to-all-start.2) | async-done | bytes 327712 | tf_op jit(solution)/shard_map/all_to_all | solution.py:86
  61.6 5.0 %collective-permute-start.9 = (bf16[576,256]{1,0:T(8,128)(2,1)S(1)}, bf16[576,256]{1,0:T(8,128)(2,1)S(1)}, u32[]{:S(2)}, u32[]{:S(2)}) collective-permute-start(bf16[576,256]{1,0:T(8,128)(2,1)S(1)} %shard_map.85.own), channel_id=1, source_target_pairs={{0,4},{4,0},{1,5},{5,1},{2,6},{6,2},{3,7},{7,3},{8,12},{12,8},{9,1... | collective-permute-start | bytes 884744 | tf_op jit(solution)/shard_map/ppermute | solution.py:82
  66.6 3.6 %shard_map.86 = (f32[16,1024]{1,0:T(8,128)S(1)}, bf16[512,1024]{1,0:T(8,128)(2,1)}, f32[16,1024]{1,0:T(8,128)S(1)}, bf16[256,1024]{1,0:T(8,128)(2,1)S(1)}, bf16[...) custom-call(bf16[288,256]{1,0:T(8,128)(2,1)S(1)} %collective-permute, ...), custom_call_target="tpu_custom_call" | custom-call | tf_op jit(solution)/shard_map/pallas_call | solution.py:77
  71.5 1.7 %collective-permute-start.17 = (bf16[288,256]{1,0:T(8,128)(2,1)S(1)}, bf16[288,256]{1,0:T(8,128)(2,1)S(1)}, u32[]{:S(2)}, u32[]{:S(2)}) collective-permute-start(bf16[288,256]{1,0:T(8,128)(2,1)S(1)} %get-tuple-element.91), channel_id=1, source_target_pairs={{0,4},{4,0},{1,5},{5,1},{2,6},{6,2},{3,7},{7,3},{8,12},{12,8},{9,1... | collective-permute-start | bytes 442376 | tf_op jit(solution)/shard_map/ppermute | solution.py:82
  73.1 1.8 %collective-permute-done.14.n0 = bf16[288,256]{1,0:T(8,128)(2,1)S(1)} collective-permute-done((bf16[288,256]{1,0:T(8,128)(2,1)S(1)}, bf16[288,256]{1,0:T(8,128)(2,1)S(1)}, u32[]{:S(2)}, u32[]{:S(2)}) %collective-permute-start.14) | collective-permute-done | bytes 147488 | tf_op jit(solution)/shard_map/ppermute | solution.py:99
  76.5 2.5 %shard_map.88 = (f32[256,256]{1,0:T(8,128)S(1)}, bf16[256,256]{1,0:T(8,128)(2,1)S(1)}, f32[16,256]{1,0:T(8,128)S(1)}, f32[16,256]{1,0:T(8,128)S(1)}, f32[16,256]...) custom-call(f32[8,1024]{1,0:T(8,128)S(1)} %get-tuple-element.58.coef, ...), custom_call_target="tpu_custom_call" | custom-call | tf_op jit(solution)/shard_map/pallas_call | solution.py:77
  79.4 2.2 %collective-permute-start.20 = (f32[32,256]{1,0:T(8,128)S(1)}, f32[32,256]{1,0:T(8,128)S(1)}, u32[]{:S(2)}, u32[]{:S(2)}) collective-permute-start(f32[32,256]{1,0:T(8,128)S(1)} %get-tuple-element.106), channel_id=1, source_target_pairs={{0,4},{4,0},{1,5},{5,1},{2,6},{6,2},{3,7},{7,3},{8,12},{12,8},{9,1... | collective-permute-start | bytes 98312 | tf_op jit(solution)/shard_map/ppermute | solution.py:82
  81.7 1.5 %collective-permute-start.19 = (f32[16,256]{1,0:T(8,128)S(1)}, f32[16,256]{1,0:T(8,128)S(1)}, u32[]{:S(2)}, u32[]{:S(2)}) collective-permute-start(f32[16,256]{1,0:T(8,128)S(1)} %get-tuple-element.104), channel_id=1, source_target_pairs={{0,3},{1,0},{2,1},{3,2},{4,7},{5,4},{6,5},{7,6},{8,11},{9,8},{10,9... | collective-permute-start | bytes 49160 | tf_op jit(solution)/shard_map/ppermute | solution.py:82
  83.2 1.6 %collective-permute-done.18.n0 = f32[16,256]{1,0:T(8,128)S(1)} collective-permute-done((f32[16,256]{1,0:T(8,128)S(1)}, f32[16,256]{1,0:T(8,128)S(1)}, u32[]{:S(2)}, u32[]{:S(2)}) %collective-permute-start.18) | collective-permute-done | bytes 16416 | tf_op jit(solution)/shard_map/ppermute | solution.py:82
  85.0 15.7 %all_to_all.27.got = bf16[16,40,256]{2,1,0:T(8,128)(2,1)S(1)} all-to-all(bf16[16,40,256]{2,1,0:T(8,128)(2,1)S(1)} %get-tuple-element.107), channel_id=1, replica_groups=mesh['z'=8,'y'=4,'core'=2,'x'=4] {'y','x'}, dimensions={0} | all-to-all | bytes 655360 | tf_op jit(solution)/shard_map/all_to_all | solution.py:86
  100.8 11.7 %all_to_all.28.got = bf16[8,40,256]{2,1,0:T(8,128)(2,1)S(1)} all-to-all(bf16[8,40,256]{2,1,0:T(8,128)(2,1)S(1)} %shard_map.91), channel_id=1, replica_groups=mesh['z'=8,'y'=4,'core'=2,'x'=4] {'z'}, dimensions={0} | all-to-all | bytes 327680 | tf_op jit(solution)/shard_map/all_to_all | solution.py:86
  112.5 2.4 %collective-permute-start.21 = (f32[40,256]{1,0:T(8,128)S(1)}, f32[40,256]{1,0:T(8,128)S(1)}, u32[]{:S(2)}, u32[]{:S(2)}) collective-permute-start(f32[40,256]{1,0:T(8,128)S(1)} %shard_map.92.own), channel_id=1, source_target_pairs={{0,4},{4,0},{1,5},{5,1},{2,6},{6,2},{3,7},{7,3},{8,12},{12,8},{9,1... | collective-permute-start | bytes 122888 | tf_op jit(solution)/shard_map/ppermute | solution.py:82
  115.8 1.6 %shard_map.94 = (f32[5,16,1,1,512]{4,3,2,1,0:T(1,128)}, f32[80,80]{1,0:T(8,128)}) custom-call(f32[8,1024]{1,0:T(8,128)S(1)} %get-tuple-element.58.coef, f32[40,256]{1,0:T(8,128)S(1)} %shard_map.92.own, f32[40,256]{1,0:T(8,128)S(1)} %collective-permute-done.21.got, f32[256,256]{1,0:T(8,128)S(1)} %get-tuple-element.108.coarse, ...), custom_call_target="tpu_custom_call", output_to_operand_aliasing={{0}: (11, {})} | custom-call | tf_op jit(solution)/shard_map/pallas_call | solution.py:77
  (46 shorter events, 11.2 us)
Async XLA Ops:
  1.6 15.1 %collective-permute-start = (bf16[64,256]{1,0:T(8,128)(2,1)S(1)}, bf16[64,256]{1,0:T(8,128)(2,1)S(1)}, u32[]{:S(2)}, u32[]{:S(2)}) collective-permute-start(bf16[64,256]{1,0:T(8,128)(2,1)S(1)} %get-tuple-element.60), channel_id=1, source_target_pairs={{4,8},{8,4},{12,16},{16,12},{20,24},{24,20},{28,32},{32,28},{36,40... | collective-permute-start | bytes 98312 | tf_op jit(solution)/shard_map/ppermute | solution.py:99
  4.4 12.4 %collective-permute-start.1 = (bf16[64,256]{1,0:T(8,128)(2,1)S(1)}, bf16[64,256]{1,0:T(8,128)(2,1)S(1)}, u32[]{:S(2)}, u32[]{:S(2)}) collective-permute-start(bf16[64,256]{1,0:T(8,128)(2,1)S(1)} %get-tuple-element.61), channel_id=1, source_target_pairs={{1,2},{2,1},{3,0},{0,3},{5,6},{6,5},{7,4},{4,7},{9,10},{10,9},{11,... | collective-permute-start | bytes 98312 | tf_op jit(solution)/shard_map/ppermute | solution.py:99
  6.9 9.9 %collective-permute-start.2 = (bf16[64,256]{1,0:T(8,128)(2,1)S(1)}, bf16[64,256]{1,0:T(8,128)(2,1)S(1)}, u32[]{:S(2)}, u32[]{:S(2)}) collective-permute-start(bf16[64,256]{1,0:T(8,128)(2,1)S(1)} %get-tuple-element.62), channel_id=1, source_target_pairs={{0,1},{1,0},{2,3},{3,2},{4,5},{5,4},{6,7},{7,6},{8,9},{9,8},{10,11... | collective-permute-start | bytes 98312 | tf_op jit(solution)/shard_map/ppermute | solution.py:99
  6.9 9.9 %collective-permute-start.3 = (bf16[64,256]{1,0:T(8,128)(2,1)S(1)}, bf16[64,256]{1,0:T(8,128)(2,1)S(1)}, u32[]{:S(2)}, u32[]{:S(2)}) collective-permute-start(bf16[64,256]{1,0:T(8,128)(2,1)S(1)} %get-tuple-element.63), channel_id=1, source_target_pairs={{0,4},{4,0},{1,5},{5,1},{2,6},{6,2},{3,7},{7,3},{8,12},{12,8},{9,1... | collective-permute-start | bytes 98312 | tf_op jit(solution)/shard_map/ppermute | solution.py:82
  13.9 0.7 copy-start
  19.4 5.6 %collective-permute-start.4 = (f32[272,256]{1,0:T(8,128)S(1)}, f32[272,256]{1,0:T(8,128)S(1)}, u32[]{:S(2)}, u32[]{:S(2)}) collective-permute-start(f32[272,256]{1,0:T(8,128)S(1)} %get-tuple-element.72), channel_id=1, source_target_pairs={{0,4},{4,0},{1,5},{5,1},{2,6},{6,2},{3,7},{7,3},{8,12},{12,8},{9,1... | collective-permute-start | bytes 835592 | tf_op jit(solution)/shard_map/ppermute | solution.py:82
  20.2 3.2 %collective-permute-start.5 = (f32[16,256]{1,0:T(8,128)S(1)}, f32[16,256]{1,0:T(8,128)S(1)}, u32[]{:S(2)}, u32[]{:S(2)}) collective-permute-start(f32[16,256]{1,0:T(8,128)S(1)} %get-tuple-element.73), channel_id=1, source_target_pairs={{4,8},{8,4},{12,16},{16,12},{20,24},{24,20},{28,32},{32,28},{36,40... | collective-permute-start | bytes 49160 | tf_op jit(solution)/shard_map/ppermute | solution.py:99
  20.2 3.8 %collective-permute-start.6 = (f32[16,256]{1,0:T(8,128)S(1)}, f32[16,256]{1,0:T(8,128)S(1)}, u32[]{:S(2)}, u32[]{:S(2)}) collective-permute-start(f32[16,256]{1,0:T(8,128)S(1)} %get-tuple-element.74), channel_id=1, source_target_pairs={{1,2},{2,1},{3,0},{0,3},{5,6},{6,5},{7,4},{4,7},{9,10},{10,9},{11,... | collective-permute-start | bytes 49160 | tf_op jit(solution)/shard_map/ppermute | solution.py:99
  21.1 2.9 %collective-permute-start.7 = (f32[16,256]{1,0:T(8,128)S(1)}, f32[16,256]{1,0:T(8,128)S(1)}, u32[]{:S(2)}, u32[]{:S(2)}) collective-permute-start(f32[16,256]{1,0:T(8,128)S(1)} %get-tuple-element.75), channel_id=1, source_target_pairs={{0,1},{1,0},{2,3},{3,2},{4,5},{5,4},{6,7},{7,6},{8,9},{9,8},{10,11... | collective-permute-start | bytes 49160 | tf_op jit(solution)/shard_map/ppermute | solution.py:99
  21.3 2.9 %collective-permute-start.8 = (f32[16,256]{1,0:T(8,128)S(1)}, f32[16,256]{1,0:T(8,128)S(1)}, u32[]{:S(2)}, u32[]{:S(2)}) collective-permute-start(f32[16,256]{1,0:T(8,128)S(1)} %get-tuple-element.76), channel_id=1, source_target_pairs={{0,4},{4,0},{1,5},{5,1},{2,6},{6,2},{3,7},{7,3},{8,12},{12,8},{9,1... | collective-permute-start | bytes 49160 | tf_op jit(solution)/shard_map/ppermute | solution.py:82
  50.1 11.4 %all-to-all-start.2 = ((bf16[16,40,256]{2,1,0:T(8,128)(2,1)}), bf16[16,40,256]{2,1,0:T(8,128)(2,1)S(1)}, u32[]{:S(2)}, u32[]{:S(2)}) async-start(bf16[16,40,256]{2,1,0:T(8,128)(2,1)} %shard_map.84), calls=%async_computation.2 | async-start | bytes 655360 | tf_op jit(solution)/shard_map/all_to_all | solution.py:86
  53.6 12.9 %collective-permute-start.10 = (bf16[288,256]{1,0:T(8,128)(2,1)S(1)}, bf16[288,256]{1,0:T(8,128)(2,1)S(1)}, u32[]{:S(2)}, u32[]{:S(2)}) collective-permute-start(bf16[288,256]{1,0:T(8,128)(2,1)S(1)} %get-tuple-element.82), channel_id=1, source_target_pairs={{4,8},{8,4},{12,16},{16,12},{20,24},{24,20},{28,32},{32,28},{36,40... | collective-permute-start | bytes 442376 | tf_op jit(solution)/shard_map/ppermute | solution.py:99
  57.5 9.0 %collective-permute-start.11 = (bf16[288,256]{1,0:T(8,128)(2,1)S(1)}, bf16[288,256]{1,0:T(8,128)(2,1)S(1)}, u32[]{:S(2)}, u32[]{:S(2)}) collective-permute-start(bf16[288,256]{1,0:T(8,128)(2,1)S(1)} %get-tuple-element.83), channel_id=1, source_target_pairs={{1,2},{2,1},{3,0},{0,3},{5,6},{6,5},{7,4},{4,7},{9,10},{10,9},{11,... | collective-permute-start | bytes 442376 | tf_op jit(solution)/shard_map/ppermute | solution.py:99
  59.9 6.6 %collective-permute-start.12 = (bf16[288,256]{1,0:T(8,128)(2,1)S(1)}, bf16[288,256]{1,0:T(8,128)(2,1)S(1)}, u32[]{:S(2)}, u32[]{:S(2)}) collective-permute-start(bf16[288,256]{1,0:T(8,128)(2,1)S(1)} %get-tuple-element.84), channel_id=1, source_target_pairs={{0,1},{1,0},{2,3},{3,2},{4,5},{5,4},{6,7},{7,6},{8,9},{9,8},{10,11... | collective-permute-start | bytes 442376 | tf_op jit(solution)/shard_map/ppermute | solution.py:99
  59.9 6.6 %collective-permute-start.13 = (bf16[288,256]{1,0:T(8,128)(2,1)S(1)}, bf16[288,256]{1,0:T(8,128)(2,1)S(1)}, u32[]{:S(2)}, u32[]{:S(2)}) collective-permute-start(bf16[288,256]{1,0:T(8,128)(2,1)S(1)} %get-tuple-element.85), channel_id=1, source_target_pairs={{0,4},{4,0},{1,5},{5,1},{2,6},{6,2},{3,7},{7,3},{8,12},{12,8},{9,1... | collective-permute-start | bytes 442376 | tf_op jit(solution)/shard_map/ppermute | solution.py:82
  61.6 14.9 %collective-permute-start.9 = (bf16[576,256]{1,0:T(8,128)(2,1)S(1)}, bf16[576,256]{1,0:T(8,128)(2,1)S(1)}, u32[]{:S(2)}, u32[]{:S(2)}) collective-permute-start(bf16[576,256]{1,0:T(8,128)(2,1)S(1)} %shard_map.85.own), channel_id=1, source_target_pairs={{0,4},{4,0},{1,5},{5,1},{2,6},{6,2},{3,7},{7,3},{8,12},{12,8},{9,1... | collective-permute-start | bytes 884744 | tf_op jit(solution)/shard_map/ppermute | solution.py:82
  70.2 4.7 %collective-permute-start.14 = (bf16[288,256]{1,0:T(8,128)(2,1)S(1)}, bf16[288,256]{1,0:T(8,128)(2,1)S(1)}, u32[]{:S(2)}, u32[]{:S(2)}) collective-permute-start(bf16[288,256]{1,0:T(8,128)(2,1)S(1)} %get-tuple-element.88), channel_id=1, source_target_pairs={{4,8},{8,4},{12,16},{16,12},{20,24},{24,20},{28,32},{32,28},{36,40... | collective-permute-start | bytes 442376 | tf_op jit(solution)/shard_map/ppermute | solution.py:99
  70.6 5.6 %collective-permute-start.15 = (bf16[288,256]{1,0:T(8,128)(2,1)S(1)}, bf16[288,256]{1,0:T(8,128)(2,1)S(1)}, u32[]{:S(2)}, u32[]{:S(2)}) collective-permute-start(bf16[288,256]{1,0:T(8,128)(2,1)S(1)} %get-tuple-element.89), channel_id=1, source_target_pairs={{1,2},{2,1},{3,0},{0,3},{5,6},{6,5},{7,4},{4,7},{9,10},{10,9},{11,... | collective-permute-start | bytes 442376 | tf_op jit(solution)/shard_map/ppermute | solution.py:99
  71.3 4.9 %collective-permute-start.16 = (bf16[288,256]{1,0:T(8,128)(2,1)S(1)}, bf16[288,256]{1,0:T(8,128)(2,1)S(1)}, u32[]{:S(2)}, u32[]{:S(2)}) collective-permute-start(bf16[288,256]{1,0:T(8,128)(2,1)S(1)} %get-tuple-element.90), channel_id=1, source_target_pairs={{0,1},{1,0},{2,3},{3,2},{4,5},{5,4},{6,7},{7,6},{8,9},{9,8},{10,11... | collective-permute-start | bytes 442376 | tf_op jit(solution)/shard_map/ppermute | solution.py:99
  71.5 4.7 %collective-permute-start.17 = (bf16[288,256]{1,0:T(8,128)(2,1)S(1)}, bf16[288,256]{1,0:T(8,128)(2,1)S(1)}, u32[]{:S(2)}, u32[]{:S(2)}) collective-permute-start(bf16[288,256]{1,0:T(8,128)(2,1)S(1)} %get-tuple-element.91), channel_id=1, source_target_pairs={{0,4},{4,0},{1,5},{5,1},{2,6},{6,2},{3,7},{7,3},{8,12},{12,8},{9,1... | collective-permute-start | bytes 442376 | tf_op jit(solution)/shard_map/ppermute | solution.py:82
  79.4 5.3 %collective-permute-start.20 = (f32[32,256]{1,0:T(8,128)S(1)}, f32[32,256]{1,0:T(8,128)S(1)}, u32[]{:S(2)}, u32[]{:S(2)}) collective-permute-start(f32[32,256]{1,0:T(8,128)S(1)} %get-tuple-element.106), channel_id=1, source_target_pairs={{0,4},{4,0},{1,5},{5,1},{2,6},{6,2},{3,7},{7,3},{8,12},{12,8},{9,1... | collective-permute-start | bytes 98312 | tf_op jit(solution)/shard_map/ppermute | solution.py:82
  81.6 3.2 %collective-permute-start.18 = (f32[16,256]{1,0:T(8,128)S(1)}, f32[16,256]{1,0:T(8,128)S(1)}, u32[]{:S(2)}, u32[]{:S(2)}) collective-permute-start(f32[16,256]{1,0:T(8,128)S(1)} %get-tuple-element.103), channel_id=1, source_target_pairs={{0,252},{4,0},{8,4},{12,8},{16,12},{20,16},{24,20},{28,24},{32,28}... | collective-permute-start | bytes 49160 | tf_op jit(solution)/shard_map/ppermute | solution.py:82
  81.7 3.1 %collective-permute-start.19 = (f32[16,256]{1,0:T(8,128)S(1)}, f32[16,256]{1,0:T(8,128)S(1)}, u32[]{:S(2)}, u32[]{:S(2)}) collective-permute-start(f32[16,256]{1,0:T(8,128)S(1)} %get-tuple-element.104), channel_id=1, source_target_pairs={{0,3},{1,0},{2,1},{3,2},{4,7},{5,4},{6,5},{7,6},{8,11},{9,8},{10,9... | collective-permute-start | bytes 49160 | tf_op jit(solution)/shard_map/ppermute | solution.py:82
  112.5 3.2 %collective-permute-start.21 = (f32[40,256]{1,0:T(8,128)S(1)}, f32[40,256]{1,0:T(8,128)S(1)}, u32[]{:S(2)}, u32[]{:S(2)}) collective-permute-start(f32[40,256]{1,0:T(8,128)S(1)} %shard_map.92.own), channel_id=1, source_target_pairs={{0,4},{4,0},{1,5},{5,1},{2,6},{6,2},{3,7},{7,3},{8,12},{12,8},{9,1... | collective-permute-start | bytes 122888 | tf_op jit(solution)/shard_map/ppermute | solution.py:82

commit v3 on v2

--- a/solution.py
+++ b/solution.py
@@ -237,14 +237,17 @@
     spread_out[...] = (number == ids[:1]).astype(F32).astype(BF16)
 
 
-def fetch_kernel(bounds, inverse_hbm, row_hbm, out, coef, own_row, row, sems):
+def fetch_kernel(bounds_hbm, inverse_hbm, row_hbm, out, coef, own_row, bounds, row, sems):
+    limits = pltpu.make_async_copy(bounds_hbm, bounds, sems.at[2])
+    limits.start()
+    copy = pltpu.make_async_copy(row_hbm, row, sems.at[1])
+    copy.start()
     fetch = pltpu.make_async_copy(inverse_hbm, out, sems.at[0])
     fetch.start()
-    copy = pltpu.make_async_copy(row_hbm, row, sems.at[1])
-    copy.start()
-    low, high = bounds[0], bounds[1]
-    centre = jnp.full((1, WIDTH), (low + high) * 0.5, F32)
-    inv = 1.0 / jnp.full((1, WIDTH), (high - low) * 0.5, F32)
+    limits.wait()
+    low, high = bounds[:, 0:1], bounds[:, 1:2]
+    centre = jnp.broadcast_to((low + high) * 0.5, (1, WIDTH))
+    inv = 1.0 / jnp.broadcast_to((high - low) * 0.5, (1, WIDTH))
     coef[...] = jnp.concatenate([centre, inv, 2.0 * inv, jnp.zeros((5, WIDTH), F32)], axis=0)
     n = lax.broadcasted_iota(jnp.int32, (NCO, NCO), 0)
     m = lax.broadcasted_iota(jnp.int32, (NCO, NCO), 1)
@@ -312,7 +315,7 @@
 
 def chain1_kernel(
     n0, n1, n2, n3, image_x, lifted_image, inverse_hbm,
-    jump1, lift1_hbm, image_x2, lifted2, s0, s1, s2, s3, inverse, lift1, sems,
+    jump1, lift1_hbm, image_x2, lifted2, s0, s1, s2, s3, inverse, lift1, sends, sems,
 ):
     fetch = pltpu.make_async_copy(inverse_hbm, inverse, sems.at[0])
     fetch.start()
@@ -330,11 +333,15 @@
     fetch.wait()
     u = dot2(jump, inverse[...])
     image_x2[...] = u
-    both = bdot(lift1[...], inverse[...])
-    lifts = (both[:NCO] + both[NCO:]).astype(BF16)
+    lifts = bdot(top, inverse[...]).astype(BF16)
+    put_chain(u, lifts, [sends.at[i] for i in range(4)])
+    copies = [pltpu.make_async_copy(sends.at[i], s, sems.at[i + 2]) for i, s in enumerate((s0, s1, s2, s3))]
+    for copy in copies:
+        copy.start()
     lifted2[...] = lifts
-    put_chain(u, lifts, (s0, s1, s2, s3))
     store.wait()
+    for copy in copies:
+        copy.wait()
 
 
 def chain2_kernel(n0, n1, n2, n3, image_x2, lifted2, jump2, lift2):
@@ -572,7 +579,7 @@
     half = ((RHS, 2 * FACE), F32)
     square = ((NCO, NCO), F32)
     blocks = ((BLOCKS, RHS, 1, 1, 2 * FACE), F32)
-    smem, hbm = pltpu.SMEM, pltpu.HBM
+    hbm = pltpu.HBM
 
     *packs, labels, block, corners = call(
         pack_kernel,
@@ -586,9 +593,9 @@
     inverse, coef, own_row = call(
         fetch_kernel,
         [((WIDTH, WIDTH), BF16), ((8, WIDTH), F32), ((8, NCO), F32)],
-        [bounds, inverse, coarse_inverse],
-        [smem, hbm, hbm],
-        [pltpu.VMEM((1, NCO), F32), pltpu.SemaphoreType.DMA((2,))],
+        [bounds.reshape(1, 2), inverse, coarse_inverse],
+        [hbm, hbm, hbm],
+        [pltpu.VMEM((1, 2), F32), pltpu.VMEM((1, NCO), F32), pltpu.SemaphoreType.DMA((3,))],
     )
     load0, wide, spread, image0, *sends = call(
         start_kernel,
@@ -617,8 +624,9 @@
         [load, table, load, ((NCO, WIDTH), BF16), chain, chain, chain, chain],
         [*near1, image_x, lifted_image, local_inverse.reshape(WIDTH, WIDTH)],
         [None] * 6 + [hbm],
-        [pltpu.VMEM((WIDTH, WIDTH), BF16), pltpu.VMEM((2 * NCO, WIDTH), BF16), pltpu.SemaphoreType.DMA((2,))],
-        out_space=[None, hbm] + [None] * 6,
+        [pltpu.VMEM((WIDTH, WIDTH), BF16), pltpu.VMEM((2 * NCO, WIDTH), BF16), pltpu.VMEM((4, *chain[0]), BF16),
+         pltpu.SemaphoreType.DMA((6,))],
+        out_space=[None, hbm, None, None] + [hbm] * 4,
     )
     near2 = neighbours(sends)
     (v,) = call(spread0_kernel, [((16, 40, NCO), BF16)], [exchange(v, "z")])

time: 118 us -> 118 us (level)
    ppermute x10, starting transfers between devices: 22.7 us -> 23.9 us  [along(): return lax.ppermute(x, axis, [(i, (i + by) % count) for i in range(count)])]
where the time goes in v3:
time: 118 us
  blocking collectives  51.5 us (44%)
  starting transfers between devices  41.3 us (35%)
  Pallas kernels  16.7 us (14%)
  waiting for transfers between devices  7.44 us (6%)
    all_to_all x4, blocking collectives, exchange(): return lax.all_to_all(x, axis, split_axis=0, concat_axis=0, tiled=True)  51.5 us
    ppermute x10, starting transfers between devices, along(): return lax.ppermute(x, axis, [(i, (i + by) % count) for i in range(count)])  23.9 us
    pallas_call x18, Pallas kernels, call(): return run(*args)  16.7 us
    ppermute x12, starting transfers between devices, in_pairs(): return lax.ppermute(v, axis, pairs)  13.8 us
    ppermute x12, waiting for transfers between devices, in_pairs(): return lax.ppermute(v, axis, pairs)  3.89 us
    all_to_all x1, starting transfers between devices, exchange(): return lax.all_to_all(x, axis, split_axis=0, concat_axis=0, tiled=True)  3.54 us
  transfers between devices with their start and end apart: 23, of which 7 were waited for; matrix products, arithmetic and copies ran while one was open for 0% of the time, Pallas kernels for 6%

profile of v3, /device:TPU:1, one launch (start us, length us, event | category | flops | bytes accessed | tf_op | source)
XLA Modules:
  0.0 117.8 jit_solution(9857256008164189249)
XLA Ops:
  1.6 2.8 %collective-permute-start = (bf16[64,256]{1,0:T(8,128)(2,1)S(1)}, bf16[64,256]{1,0:T(8,128)(2,1)S(1)}, u32[]{:S(2)}, u32[]{:S(2)}) collective-permute-start(bf16[64,256]{1,0:T(8,128)(2,1)S(1)} %get-tuple-element.60), channel_id=1, source_target_pairs={{4,8},{8,4},{12,16},{16,12},{20,24},{24,20},{28,32},{32,28},{36,40... | collective-permute-start | bytes 98312 | tf_op jit(solution)/shard_map/ppermute | solution.py:99
  4.4 2.5 %collective-permute-start.1 = (bf16[64,256]{1,0:T(8,128)(2,1)S(1)}, bf16[64,256]{1,0:T(8,128)(2,1)S(1)}, u32[]{:S(2)}, u32[]{:S(2)}) collective-permute-start(bf16[64,256]{1,0:T(8,128)(2,1)S(1)} %get-tuple-element.61), channel_id=1, source_target_pairs={{1,2},{2,1},{3,0},{0,3},{5,6},{6,5},{7,4},{4,7},{9,10},{10,9},{11,... | collective-permute-start | bytes 98312 | tf_op jit(solution)/shard_map/ppermute | solution.py:99
  6.9 7.1 %collective-permute-start.3 = (bf16[64,256]{1,0:T(8,128)(2,1)S(1)}, bf16[64,256]{1,0:T(8,128)(2,1)S(1)}, u32[]{:S(2)}, u32[]{:S(2)}) collective-permute-start(bf16[64,256]{1,0:T(8,128)(2,1)S(1)} %get-tuple-element.63), channel_id=1, source_target_pairs={{0,4},{4,0},{1,5},{5,1},{2,6},{6,2},{3,7},{7,3},{8,12},{12,8},{9,1... | collective-permute-start | bytes 98312 | tf_op jit(solution)/shard_map/ppermute | solution.py:82
  13.9 1.6 %shard_map.77 = (bf16[1024,1024]{1,0:T(8,128)(2,1)S(1)}, f32[8,1024]{1,0:T(8,128)S(1)}, f32[8,256]{1,0:T(8,128)S(1)}) custom-call(f32[1,2]{1,0:T(1,128)} %bitcast.9, bf16[1024,1024]{1,0:T(8,128)(2,1)} %bitcast.4, f32[1,256]{1,0:T(1,128)} %row_hbm.1), custom_call_target="tpu_custom_call" | custom-call | tf_op jit(solution)/shard_map/pallas_call | solution.py:77
  16.2 2.0 %shard_map.80 = (f32[272,256]{1,0:T(8,128)S(1)}, f32[272,256]{1,0:T(8,128)S(1)}, bf16[512,1024]{1,0:T(8,128)(2,1)S(1)}) custom-call(f32[16,1024]{1,0:T(8,128)S(1)} %get-tuple-element.67.load0, f32[16,1024]{1,0:T(8,128)S(1)} %get-tuple-element.68.image, bf16[160,1024]{1,0:T(8,128)(2,1)S(1)} %get-tuple-element.69.wide_in, ...), custom_call_target="tpu_custom_call" | custom-call | tf_op jit(solution)/shard_map/pallas_call | solution.py:77
  18.2 1.9 %collective-permute-start.4 = (f32[272,256]{1,0:T(8,128)S(1)}, f32[272,256]{1,0:T(8,128)S(1)}, u32[]{:S(2)}, u32[]{:S(2)}) collective-permute-start(f32[272,256]{1,0:T(8,128)S(1)} %get-tuple-element.72), channel_id=1, source_target_pairs={{0,4},{4,0},{1,5},{5,1},{2,6},{6,2},{3,7},{7,3},{8,12},{12,8},{9,1... | collective-permute-start | bytes 835592 | tf_op jit(solution)/shard_map/ppermute | solution.py:82
  21.1 2.3 %collective-permute-start.8 = (f32[16,256]{1,0:T(8,128)S(1)}, f32[16,256]{1,0:T(8,128)S(1)}, u32[]{:S(2)}, u32[]{:S(2)}) collective-permute-start(f32[16,256]{1,0:T(8,128)S(1)} %get-tuple-element.76), channel_id=1, source_target_pairs={{0,4},{4,0},{1,5},{5,1},{2,6},{6,2},{3,7},{7,3},{8,12},{12,8},{9,1... | collective-permute-start | bytes 49160 | tf_op jit(solution)/shard_map/ppermute | solution.py:82
  25.1 11.2 %all_to_all.25.got = bf16[16,24,256]{2,1,0:T(8,128)(2,1)S(1)} all-to-all(bf16[16,24,256]{2,1,0:T(8,128)(2,1)S(1)} %shard_map.82), channel_id=1, replica_groups=mesh['z'=8,'y'=4,'core'=2,'x'=4] {'y','x'}, dimensions={0} | all-to-all | bytes 393216 | tf_op jit(solution)/shard_map/all_to_all | solution.py:86
  36.3 12.7 %all_to_all.26.got = bf16[8,24,256]{2,1,0:T(8,128)(2,1)S(1)} all-to-all(bf16[8,24,256]{2,1,0:T(8,128)(2,1)S(1)} %shard_map.83), channel_id=1, replica_groups=mesh['z'=8,'y'=4,'core'=2,'x'=4] {'z'}, dimensions={0} | all-to-all | bytes 196608 | tf_op jit(solution)/shard_map/all_to_all | solution.py:86
  49.7 3.5 %all-to-all-start.2 = ((bf16[16,40,256]{2,1,0:T(8,128)(2,1)}), bf16[16,40,256]{2,1,0:T(8,128)(2,1)S(1)}, u32[]{:S(2)}, u32[]{:S(2)}) async-start(bf16[16,40,256]{2,1,0:T(8,128)(2,1)} %shard_map.84), calls=%async_computation.2 | async-start | bytes 655360 | tf_op jit(solution)/shard_map/all_to_all | solution.py:86
  53.3 3.9 %collective-permute-start.10 = (bf16[288,256]{1,0:T(8,128)(2,1)S(1)}, bf16[288,256]{1,0:T(8,128)(2,1)S(1)}, u32[]{:S(2)}, u32[]{:S(2)}) collective-permute-start(bf16[288,256]{1,0:T(8,128)(2,1)S(1)} %get-tuple-element.82), channel_id=1, source_target_pairs={{4,8},{8,4},{12,16},{16,12},{20,24},{24,20},{28,32},{32,28},{36,40... | collective-permute-start | bytes 442376 | tf_op jit(solution)/shard_map/ppermute | solution.py:99
  57.2 2.4 %collective-permute-start.11 = (bf16[288,256]{1,0:T(8,128)(2,1)S(1)}, bf16[288,256]{1,0:T(8,128)(2,1)S(1)}, u32[]{:S(2)}, u32[]{:S(2)}) collective-permute-start(bf16[288,256]{1,0:T(8,128)(2,1)S(1)} %get-tuple-element.83), channel_id=1, source_target_pairs={{1,2},{2,1},{3,0},{0,3},{5,6},{6,5},{7,4},{4,7},{9,10},{10,9},{11,... | collective-permute-start | bytes 442376 | tf_op jit(solution)/shard_map/ppermute | solution.py:99
  59.6 1.5 %all-to-all-done.2.got = bf16[16,40,256]{2,1,0:T(8,128)(2,1)S(1)} async-done(((bf16[16,40,256]{2,1,0:T(8,128)(2,1)}), bf16[16,40,256]{2,1,0:T(8,128)(2,1)S(1)}, u32[]{:S(2)}, u32[]{:S(2)}) %all-to-all-start.2) | async-done | bytes 327712 | tf_op jit(solution)/shard_map/all_to_all | solution.py:86
  61.2 5.1 %collective-permute-start.9 = (bf16[576,256]{1,0:T(8,128)(2,1)S(1)}, bf16[576,256]{1,0:T(8,128)(2,1)S(1)}, u32[]{:S(2)}, u32[]{:S(2)}) collective-permute-start(bf16[576,256]{1,0:T(8,128)(2,1)S(1)} %shard_map.85.own), channel_id=1, source_target_pairs={{0,4},{4,0},{1,5},{5,1},{2,6},{6,2},{3,7},{7,3},{8,12},{12,8},{9,1... | collective-permute-start | bytes 884744 | tf_op jit(solution)/shard_map/ppermute | solution.py:82
  66.3 3.9 %shard_map.86 = (f32[16,1024]{1,0:T(8,128)S(1)}, bf16[512,1024]{1,0:T(8,128)(2,1)}, f32[16,1024]{1,0:T(8,128)S(1)}, bf16[256,1024]{1,0:T(8,128)(2,1)S(1)}, bf16[...) custom-call(bf16[288,256]{1,0:T(8,128)(2,1)S(1)} %collective-permute-done.1, ...), custom_call_target="tpu_custom_call" | custom-call | tf_op jit(solution)/shard_map/pallas_call | solution.py:77
  71.4 1.7 %collective-permute-start.17 = (bf16[288,256]{1,0:T(8,128)(2,1)}, bf16[288,256]{1,0:T(8,128)(2,1)S(1)}, u32[]{:S(2)}, u32[]{:S(2)}) collective-permute-start(bf16[288,256]{1,0:T(8,128)(2,1)} %get-tuple-element.91), channel_id=1, source_target_pairs={{0,4},{4,0},{1,5},{5,1},{2,6},{6,2},{3,7},{7,3},{8,12},{12,8},{9,1... | collective-permute-start | bytes 442376 | tf_op jit(solution)/shard_map/ppermute | solution.py:82
  73.1 2.0 %collective-permute-done.14.n0 = bf16[288,256]{1,0:T(8,128)(2,1)S(1)} collective-permute-done((bf16[288,256]{1,0:T(8,128)(2,1)}, bf16[288,256]{1,0:T(8,128)(2,1)S(1)}, u32[]{:S(2)}, u32[]{:S(2)}) %collective-permute-start.14) | collective-permute-done | bytes 147488 | tf_op jit(solution)/shard_map/ppermute | solution.py:99
  76.7 2.5 %shard_map.88 = (f32[256,256]{1,0:T(8,128)S(1)}, bf16[256,256]{1,0:T(8,128)(2,1)S(1)}, f32[16,256]{1,0:T(8,128)S(1)}, f32[16,256]{1,0:T(8,128)S(1)}, f32[16,256]...) custom-call(f32[8,1024]{1,0:T(8,128)S(1)} %get-tuple-element.58.coef, ...), custom_call_target="tpu_custom_call" | custom-call | tf_op jit(solution)/shard_map/pallas_call | solution.py:77
  79.6 2.2 %collective-permute-start.20 = (f32[32,256]{1,0:T(8,128)S(1)}, f32[32,256]{1,0:T(8,128)S(1)}, u32[]{:S(2)}, u32[]{:S(2)}) collective-permute-start(f32[32,256]{1,0:T(8,128)S(1)} %get-tuple-element.106), channel_id=1, source_target_pairs={{0,4},{4,0},{1,5},{5,1},{2,6},{6,2},{3,7},{7,3},{8,12},{12,8},{9,1... | collective-permute-start | bytes 98312 | tf_op jit(solution)/shard_map/ppermute | solution.py:82
  83.3 1.6 %collective-permute-done.18.n0 = f32[16,256]{1,0:T(8,128)S(1)} collective-permute-done((f32[16,256]{1,0:T(8,128)S(1)}, f32[16,256]{1,0:T(8,128)S(1)}, u32[]{:S(2)}, u32[]{:S(2)}) %collective-permute-start.18) | collective-permute-done | bytes 16416 | tf_op jit(solution)/shard_map/ppermute | solution.py:82
  85.2 15.2 %all_to_all.27.got = bf16[16,40,256]{2,1,0:T(8,128)(2,1)S(1)} all-to-all(bf16[16,40,256]{2,1,0:T(8,128)(2,1)S(1)} %get-tuple-element.107), channel_id=1, replica_groups=mesh['z'=8,'y'=4,'core'=2,'x'=4] {'y','x'}, dimensions={0} | all-to-all | bytes 655360 | tf_op jit(solution)/shard_map/all_to_all | solution.py:86
  100.4 12.5 %all_to_all.28.got = bf16[8,40,256]{2,1,0:T(8,128)(2,1)S(1)} all-to-all(bf16[8,40,256]{2,1,0:T(8,128)(2,1)S(1)} %shard_map.91), channel_id=1, replica_groups=mesh['z'=8,'y'=4,'core'=2,'x'=4] {'z'}, dimensions={0} | all-to-all | bytes 327680 | tf_op jit(solution)/shard_map/all_to_all | solution.py:86
  112.9 2.2 %collective-permute-start.21 = (f32[40,256]{1,0:T(8,128)S(1)}, f32[40,256]{1,0:T(8,128)S(1)}, u32[]{:S(2)}, u32[]{:S(2)}) collective-permute-start(f32[40,256]{1,0:T(8,128)S(1)} %shard_map.92.own), channel_id=1, source_target_pairs={{0,4},{4,0},{1,5},{5,1},{2,6},{6,2},{3,7},{7,3},{8,12},{12,8},{9,1... | collective-permute-start | bytes 122888 | tf_op jit(solution)/shard_map/ppermute | solution.py:82
  116.0 1.6 %shard_map.94 = (f32[5,16,1,1,512]{4,3,2,1,0:T(1,128)}, f32[80,80]{1,0:T(8,128)}) custom-call(f32[8,1024]{1,0:T(8,128)S(1)} %get-tuple-element.58.coef, f32[40,256]{1,0:T(8,128)S(1)} %shard_map.92.own, f32[40,256]{1,0:T(8,128)S(1)} %collective-permute-done.21.got, f32[256,256]{1,0:T(8,128)S(1)} %get-tuple-element.108.coarse, ...), custom_call_target="tpu_custom_call", output_to_operand_aliasing={{0}: (11, {})} | custom-call | tf_op jit(solution)/shard_map/pallas_call | solution.py:77
  (44 shorter events, 11.1 us)
Async XLA Ops:
  1.6 14.0 %collective-permute-start = (bf16[64,256]{1,0:T(8,128)(2,1)S(1)}, bf16[64,256]{1,0:T(8,128)(2,1)S(1)}, u32[]{:S(2)}, u32[]{:S(2)}) collective-permute-start(bf16[64,256]{1,0:T(8,128)(2,1)S(1)} %get-tuple-element.60), channel_id=1, source_target_pairs={{4,8},{8,4},{12,16},{16,12},{20,24},{24,20},{28,32},{32,28},{36,40... | collective-permute-start | bytes 98312 | tf_op jit(solution)/shard_map/ppermute | solution.py:99
  4.4 11.2 %collective-permute-start.1 = (bf16[64,256]{1,0:T(8,128)(2,1)S(1)}, bf16[64,256]{1,0:T(8,128)(2,1)S(1)}, u32[]{:S(2)}, u32[]{:S(2)}) collective-permute-start(bf16[64,256]{1,0:T(8,128)(2,1)S(1)} %get-tuple-element.61), channel_id=1, source_target_pairs={{1,2},{2,1},{3,0},{0,3},{5,6},{6,5},{7,4},{4,7},{9,10},{10,9},{11,... | collective-permute-start | bytes 98312 | tf_op jit(solution)/shard_map/ppermute | solution.py:99
  6.9 8.7 %collective-permute-start.2 = (bf16[64,256]{1,0:T(8,128)(2,1)S(1)}, bf16[64,256]{1,0:T(8,128)(2,1)S(1)}, u32[]{:S(2)}, u32[]{:S(2)}) collective-permute-start(bf16[64,256]{1,0:T(8,128)(2,1)S(1)} %get-tuple-element.62), channel_id=1, source_target_pairs={{0,1},{1,0},{2,3},{3,2},{4,5},{5,4},{6,7},{7,6},{8,9},{9,8},{10,11... | collective-permute-start | bytes 98312 | tf_op jit(solution)/shard_map/ppermute | solution.py:99
  6.9 8.8 %collective-permute-start.3 = (bf16[64,256]{1,0:T(8,128)(2,1)S(1)}, bf16[64,256]{1,0:T(8,128)(2,1)S(1)}, u32[]{:S(2)}, u32[]{:S(2)}) collective-permute-start(bf16[64,256]{1,0:T(8,128)(2,1)S(1)} %get-tuple-element.63), channel_id=1, source_target_pairs={{0,4},{4,0},{1,5},{5,1},{2,6},{6,2},{3,7},{7,3},{8,12},{12,8},{9,1... | collective-permute-start | bytes 98312 | tf_op jit(solution)/shard_map/ppermute | solution.py:82
  18.2 6.8 %collective-permute-start.4 = (f32[272,256]{1,0:T(8,128)S(1)}, f32[272,256]{1,0:T(8,128)S(1)}, u32[]{:S(2)}, u32[]{:S(2)}) collective-permute-start(f32[272,256]{1,0:T(8,128)S(1)} %get-tuple-element.72), channel_id=1, source_target_pairs={{0,4},{4,0},{1,5},{5,1},{2,6},{6,2},{3,7},{7,3},{8,12},{12,8},{9,1... | collective-permute-start | bytes 835592 | tf_op jit(solution)/shard_map/ppermute | solution.py:82
  20.2 3.2 %collective-permute-start.5 = (f32[16,256]{1,0:T(8,128)S(1)}, f32[16,256]{1,0:T(8,128)S(1)}, u32[]{:S(2)}, u32[]{:S(2)}) collective-permute-start(f32[16,256]{1,0:T(8,128)S(1)} %get-tuple-element.73), channel_id=1, source_target_pairs={{4,8},{8,4},{12,16},{16,12},{20,24},{24,20},{28,32},{32,28},{36,40... | collective-permute-start | bytes 49160 | tf_op jit(solution)/shard_map/ppermute | solution.py:99
  20.2 3.8 %collective-permute-start.6 = (f32[16,256]{1,0:T(8,128)S(1)}, f32[16,256]{1,0:T(8,128)S(1)}, u32[]{:S(2)}, u32[]{:S(2)}) collective-permute-start(f32[16,256]{1,0:T(8,128)S(1)} %get-tuple-element.74), channel_id=1, source_target_pairs={{1,2},{2,1},{3,0},{0,3},{5,6},{6,5},{7,4},{4,7},{9,10},{10,9},{11,... | collective-permute-start | bytes 49160 | tf_op jit(solution)/shard_map/ppermute | solution.py:99
  21.1 2.9 %collective-permute-start.7 = (f32[16,256]{1,0:T(8,128)S(1)}, f32[16,256]{1,0:T(8,128)S(1)}, u32[]{:S(2)}, u32[]{:S(2)}) collective-permute-start(f32[16,256]{1,0:T(8,128)S(1)} %get-tuple-element.75), channel_id=1, source_target_pairs={{0,1},{1,0},{2,3},{3,2},{4,5},{5,4},{6,7},{7,6},{8,9},{9,8},{10,11... | collective-permute-start | bytes 49160 | tf_op jit(solution)/shard_map/ppermute | solution.py:99
  21.1 3.1 %collective-permute-start.8 = (f32[16,256]{1,0:T(8,128)S(1)}, f32[16,256]{1,0:T(8,128)S(1)}, u32[]{:S(2)}, u32[]{:S(2)}) collective-permute-start(f32[16,256]{1,0:T(8,128)S(1)} %get-tuple-element.76), channel_id=1, source_target_pairs={{0,4},{4,0},{1,5},{5,1},{2,6},{6,2},{3,7},{7,3},{8,12},{12,8},{9,1... | collective-permute-start | bytes 49160 | tf_op jit(solution)/shard_map/ppermute | solution.py:82
  49.7 11.4 %all-to-all-start.2 = ((bf16[16,40,256]{2,1,0:T(8,128)(2,1)}), bf16[16,40,256]{2,1,0:T(8,128)(2,1)S(1)}, u32[]{:S(2)}, u32[]{:S(2)}) async-start(bf16[16,40,256]{2,1,0:T(8,128)(2,1)} %shard_map.84), calls=%async_computation.2 | async-start | bytes 655360 | tf_op jit(solution)/shard_map/all_to_all | solution.py:86
  53.3 13.0 %collective-permute-start.10 = (bf16[288,256]{1,0:T(8,128)(2,1)S(1)}, bf16[288,256]{1,0:T(8,128)(2,1)S(1)}, u32[]{:S(2)}, u32[]{:S(2)}) collective-permute-start(bf16[288,256]{1,0:T(8,128)(2,1)S(1)} %get-tuple-element.82), channel_id=1, source_target_pairs={{4,8},{8,4},{12,16},{16,12},{20,24},{24,20},{28,32},{32,28},{36,40... | collective-permute-start | bytes 442376 | tf_op jit(solution)/shard_map/ppermute | solution.py:99
  57.2 9.0 %collective-permute-start.11 = (bf16[288,256]{1,0:T(8,128)(2,1)S(1)}, bf16[288,256]{1,0:T(8,128)(2,1)S(1)}, u32[]{:S(2)}, u32[]{:S(2)}) collective-permute-start(bf16[288,256]{1,0:T(8,128)(2,1)S(1)} %get-tuple-element.83), channel_id=1, source_target_pairs={{1,2},{2,1},{3,0},{0,3},{5,6},{6,5},{7,4},{4,7},{9,10},{10,9},{11,... | collective-permute-start | bytes 442376 | tf_op jit(solution)/shard_map/ppermute | solution.py:99
  59.6 6.6 %collective-permute-start.12 = (bf16[288,256]{1,0:T(8,128)(2,1)S(1)}, bf16[288,256]{1,0:T(8,128)(2,1)S(1)}, u32[]{:S(2)}, u32[]{:S(2)}) collective-permute-start(bf16[288,256]{1,0:T(8,128)(2,1)S(1)} %get-tuple-element.84), channel_id=1, source_target_pairs={{0,1},{1,0},{2,3},{3,2},{4,5},{5,4},{6,7},{7,6},{8,9},{9,8},{10,11... | collective-permute-start | bytes 442376 | tf_op jit(solution)/shard_map/ppermute | solution.py:99
  59.6 6.6 %collective-permute-start.13 = (bf16[288,256]{1,0:T(8,128)(2,1)S(1)}, bf16[288,256]{1,0:T(8,128)(2,1)S(1)}, u32[]{:S(2)}, u32[]{:S(2)}) collective-permute-start(bf16[288,256]{1,0:T(8,128)(2,1)S(1)} %get-tuple-element.85), channel_id=1, source_target_pairs={{0,4},{4,0},{1,5},{5,1},{2,6},{6,2},{3,7},{7,3},{8,12},{12,8},{9,1... | collective-permute-start | bytes 442376 | tf_op jit(solution)/shard_map/ppermute | solution.py:82
  61.2 15.5 %collective-permute-start.9 = (bf16[576,256]{1,0:T(8,128)(2,1)S(1)}, bf16[576,256]{1,0:T(8,128)(2,1)S(1)}, u32[]{:S(2)}, u32[]{:S(2)}) collective-permute-start(bf16[576,256]{1,0:T(8,128)(2,1)S(1)} %shard_map.85.own), channel_id=1, source_target_pairs={{0,4},{4,0},{1,5},{5,1},{2,6},{6,2},{3,7},{7,3},{8,12},{12,8},{9,1... | collective-permute-start | bytes 884744 | tf_op jit(solution)/shard_map/ppermute | solution.py:82
  70.2 4.9 %collective-permute-start.14 = (bf16[288,256]{1,0:T(8,128)(2,1)}, bf16[288,256]{1,0:T(8,128)(2,1)S(1)}, u32[]{:S(2)}, u32[]{:S(2)}) collective-permute-start(bf16[288,256]{1,0:T(8,128)(2,1)} %get-tuple-element.88), channel_id=1, source_target_pairs={{4,8},{8,4},{12,16},{16,12},{20,24},{24,20},{28,32},{32,28},{36,40... | collective-permute-start | bytes 442376 | tf_op jit(solution)/shard_map/ppermute | solution.py:99
  70.6 5.8 %collective-permute-start.15 = (bf16[288,256]{1,0:T(8,128)(2,1)}, bf16[288,256]{1,0:T(8,128)(2,1)S(1)}, u32[]{:S(2)}, u32[]{:S(2)}) collective-permute-start(bf16[288,256]{1,0:T(8,128)(2,1)} %get-tuple-element.89), channel_id=1, source_target_pairs={{1,2},{2,1},{3,0},{0,3},{5,6},{6,5},{7,4},{4,7},{9,10},{10,9},{11,... | collective-permute-start | bytes 442376 | tf_op jit(solution)/shard_map/ppermute | solution.py:99
  71.3 5.1 %collective-permute-start.16 = (bf16[288,256]{1,0:T(8,128)(2,1)}, bf16[288,256]{1,0:T(8,128)(2,1)S(1)}, u32[]{:S(2)}, u32[]{:S(2)}) collective-permute-start(bf16[288,256]{1,0:T(8,128)(2,1)} %get-tuple-element.90), channel_id=1, source_target_pairs={{0,1},{1,0},{2,3},{3,2},{4,5},{5,4},{6,7},{7,6},{8,9},{9,8},{10,11... | collective-permute-start | bytes 442376 | tf_op jit(solution)/shard_map/ppermute | solution.py:99
  71.4 5.0 %collective-permute-start.17 = (bf16[288,256]{1,0:T(8,128)(2,1)}, bf16[288,256]{1,0:T(8,128)(2,1)S(1)}, u32[]{:S(2)}, u32[]{:S(2)}) collective-permute-start(bf16[288,256]{1,0:T(8,128)(2,1)} %get-tuple-element.91), channel_id=1, source_target_pairs={{0,4},{4,0},{1,5},{5,1},{2,6},{6,2},{3,7},{7,3},{8,12},{12,8},{9,1... | collective-permute-start | bytes 442376 | tf_op jit(solution)/shard_map/ppermute | solution.py:82
  79.6 5.3 %collective-permute-start.20 = (f32[32,256]{1,0:T(8,128)S(1)}, f32[32,256]{1,0:T(8,128)S(1)}, u32[]{:S(2)}, u32[]{:S(2)}) collective-permute-start(f32[32,256]{1,0:T(8,128)S(1)} %get-tuple-element.106), channel_id=1, source_target_pairs={{0,4},{4,0},{1,5},{5,1},{2,6},{6,2},{3,7},{7,3},{8,12},{12,8},{9,1... | collective-permute-start | bytes 98312 | tf_op jit(solution)/shard_map/ppermute | solution.py:82
  81.8 3.2 %collective-permute-start.18 = (f32[16,256]{1,0:T(8,128)S(1)}, f32[16,256]{1,0:T(8,128)S(1)}, u32[]{:S(2)}, u32[]{:S(2)}) collective-permute-start(f32[16,256]{1,0:T(8,128)S(1)} %get-tuple-element.103), channel_id=1, source_target_pairs={{0,252},{4,0},{8,4},{12,8},{16,12},{20,16},{24,20},{28,24},{32,28}... | collective-permute-start | bytes 49160 | tf_op jit(solution)/shard_map/ppermute | solution.py:82
  81.9 3.1 %collective-permute-start.19 = (f32[16,256]{1,0:T(8,128)S(1)}, f32[16,256]{1,0:T(8,128)S(1)}, u32[]{:S(2)}, u32[]{:S(2)}) collective-permute-start(f32[16,256]{1,0:T(8,128)S(1)} %get-tuple-element.104), channel_id=1, source_target_pairs={{0,3},{1,0},{2,1},{3,2},{4,7},{5,4},{6,5},{7,6},{8,11},{9,8},{10,9... | collective-permute-start | bytes 49160 | tf_op jit(solution)/shard_map/ppermute | solution.py:82
  112.9 3.1 %collective-permute-start.21 = (f32[40,256]{1,0:T(8,128)S(1)}, f32[40,256]{1,0:T(8,128)S(1)}, u32[]{:S(2)}, u32[]{:S(2)}) collective-permute-start(f32[40,256]{1,0:T(8,128)S(1)} %shard_map.92.own), channel_id=1, source_target_pairs={{0,4},{4,0},{1,5},{5,1},{2,6},{6,2},{3,7},{7,3},{8,12},{12,8},{9,1... | collective-permute-start | bytes 122888 | tf_op jit(solution)/shard_map/ppermute | solution.py:82

commit v4 on v3

--- a/solution.py
+++ b/solution.py
@@ -301,16 +301,26 @@
 
 
 def join_kernel(
-    coef, load0, n0, n1, n2, n3, image, wide_in, spread, inverse, lifted_image, base1, jump0, g2, image_x, s0, s1, s2, s3
+    coef, load0, n0, n1, n2, n3, image, wide_in, spread, inverse, lifted_image, keep, got,
+    base1, jump0, image_x, s0, s1, s2, s3, out_hbm, out, sem,
 ):
     centre, inv, _ = terms_in(coef, WIDTH)
     jump = jnp.concatenate(jumped(image, (n0, n1, n2, n3)), axis=1)
+    u = dot2(jump, inverse[...])
+    g2 = dot2(dot2(u, wide_in[...], NT), spread[:, :SLOTS], NT)
+    pieces = [high_low(keep[NCO:] + got[NCO:]), high_low(g2)]
+    zero = jnp.zeros((4, NCO), F32)
+    for p in range(16):
+        rows = slice(16 * p, 16 * p + 16)
+        small = [piece[part][p : p + 1] for part in range(2) for piece in pieces]
+        out[p] = jnp.concatenate([keep[rows] + got[rows], *small, zero], axis=0).astype(BF16)
+    copy = pltpu.make_async_copy(out, out_hbm, sem)
+    copy.start()
     jump0[...] = jump
     base1[...] = (jump - centre * load0[...]) * inv
-    u = dot2(jump, inverse[...])
     image_x[...] = u
-    g2[...] = dot2(dot2(u, wide_in[...], NT), spread[:, :SLOTS], NT)
     put_chain(u, lifted_image[:NCO], (s0, s1, s2, s3))
+    copy.wait()
 
 
 def chain1_kernel(
@@ -352,15 +362,6 @@
     lift2[NCO:] = low
 
 
-def plane0_kernel(keep, got, g2, out):
-    pieces = [high_low(keep[NCO:] + got[NCO:]), high_low(g2[...])]
-    zero = jnp.zeros((4, NCO), F32)
-    for p in range(16):
-        rows = slice(16 * p, 16 * p + 16)
-        small = [piece[part][p : p + 1] for part in range(2) for piece in pieces]
-        out[p] = jnp.concatenate([keep[rows] + got[rows], *small, zero], axis=0).astype(BF16)
-
-
 def summed(got):
     total = got[0].astype(F32)
     for p in range(1, got.shape[0]):
@@ -412,8 +413,9 @@
     fetch.start()
 
     def put(first, second):
-        for half, part in ((slice(0, 128), first), (slice(128, 256), second)):
-            coarse[half] = part[320:448].astype(F32) + part[448:576].astype(F32)
+        for row, part in ((0, first), (128, second)):
+            coarse[row : row + 128] = part[320:448]
+            coarse[NCO + row : NCO + row + 128] = part[448:576]
         m0[...] = first[:NCO]
         m1[...] = second[:NCO]
         w0[...] = first[256:272].astype(F32) + first[288:304].astype(F32)
@@ -424,14 +426,14 @@
     on_core(lambda: put(own, got), lambda: put(got, own))
     centre, inv, alpha = terms_in(coef, NCO)
     w = w0[...]
-    z = hdot(w, coarse[...])
+    z = dot_halves(w, coarse[...])
     after = (g1[...] + dot2(z, m0[...]) - centre * w) * inv
     w1[...] = after
-    z1 = hdot(after, coarse[...])
+    z1 = dot_halves(after, coarse[...])
     image = (g2[...] + dot2(z, m1[...]) - centre * g1[...]) * inv
     last = alpha * (image + dot2(z1, m0[...]) - centre * after) - w
     w2[...] = last
-    z2 = hdot(last, coarse[...])
+    z2 = dot_halves(last, coarse[...])
     both = jnp.concatenate([z, z1, z2], axis=0)
     lift = lifted(both, wide_in[...], spread[:, :SLOTS])
     far = dot_halves(z, chain2[...])
@@ -533,7 +535,7 @@
     g3, packed = second[:RHS], second[RHS:]
     row = own[2 * RHS :] + got[2 * RHS :]
     row = jnp.concatenate([row[:, :128], row[:, 128:]], axis=0)
-    z3 = hdot(w3, coarse[...])
+    z3 = dot_halves(w3, coarse[...])
     lift = lifted(z3, wide_in[...], spread[:, :SLOTS])
     value = jnp.concatenate(
         [known4[:, :FACE] + alpha * lift[:, SEG[0]], known4[:, FACE:] + alpha * lift[:, SEG[2]]], axis=1
@@ -577,7 +579,6 @@
     load = ((RHS, WIDTH), F32)
     small = ((RHS, NCO), F32)
     half = ((RHS, 2 * FACE), F32)
-    square = ((NCO, NCO), F32)
     blocks = ((BLOCKS, RHS, 1, 1, 2 * FACE), F32)
     hbm = pltpu.HBM
 
@@ -611,12 +612,13 @@
     got = swapped(send)
     chain = ((2 * RHS + NCO, FACE), BF16)
     table = ((2 * NCO, WIDTH), BF16)
-    base1, jump0, g2, image_x, *sends = call(
+    base1, jump0, image_x, *sends, v = call(
         join_kernel,
-        [load, load, small, load, chain, chain, chain, chain],
-        [coef, load0, *near0, image0, wide, spread, inverse, lifted_image],
-    )
-    (v,) = call(plane0_kernel, [((16, 24, NCO), BF16)], [keep, got, g2])
+        [load, load, load, chain, chain, chain, chain, ((16, 24, NCO), BF16)],
+        [coef, load0, *near0, image0, wide, spread, inverse, lifted_image, keep, got],
+        scratch=[pltpu.VMEM((16, 24, NCO), BF16), pltpu.SemaphoreType.DMA(())],
+        out_space=[None] * 7 + [hbm],
+    )
     near1 = neighbours(sends)
     (v,) = call(depth0_kernel, [((8, 24, NCO), BF16)], [exchange(v, PLANE), own_row])
     jump1, chain1, image_x2, lifted2, *sends = call(
@@ -635,7 +637,7 @@
 
     coarse, m0, w0, w1, w2, load1, load2, load3, image3, low_sub, low_grp = call(
         march_kernel,
-        [square, ((NCO, NCO), BF16), small, small, small, load, load, load, load, face, face],
+        [((2 * NCO, NCO), BF16), ((NCO, NCO), BF16), small, small, small, load, load, load, load, face, face],
         [coef, own, swapped(own), load0, base1, jump0, jump1, jump2, chain2, spread, wide, chain1,
          local_inverse.reshape(WIDTH, WIDTH)],
         [None] * 11 + [hbm, hbm],

time: 118 us -> 119 us (level)
    pallas_call x18 -> x17, Pallas kernels: 16.7 us -> 16.8 us  [call(): return run(*args)]
where the time goes in v4:
time: 119 us; the launch traced here: 118 us
  blocking collectives  51.6 us (43%)
  starting transfers between devices  41.3 us (35%)
  Pallas kernels  16.8 us (14%)
  waiting for transfers between devices  7.43 us (6%)
    all_to_all x4, blocking collectives, exchange(): return lax.all_to_all(x, axis, split_axis=0, concat_axis=0, tiled=True)  51.6 us
    ppermute x10, starting transfers between devices, along(): return lax.ppermute(x, axis, [(i, (i + by) % count) for i in range(count)])  24 us
    pallas_call x17, Pallas kernels, call(): return run(*args)  16.8 us
    ppermute x12, starting transfers between devices, in_pairs(): return lax.ppermute(v, axis, pairs)  13.8 us
    ppermute x12, waiting for transfers between devices, in_pairs(): return lax.ppermute(v, axis, pairs)  3.9 us
    all_to_all x1, starting transfers between devices, exchange(): return lax.all_to_all(x, axis, split_axis=0, concat_axis=0, tiled=True)  3.54 us
  transfers between devices with their start and end apart: 23, of which 7 were waited for; matrix products, arithmetic and copies ran while one was open for 0% of the time, Pallas kernels for 6%

profile of v4, /device:TPU:1, one launch (start us, length us, event | category | flops | bytes accessed | tf_op | source)
XLA Modules:
  0.0 118.1 jit_solution(3411275801327780584)
XLA Ops:
  1.6 2.8 %collective-permute-start = (bf16[64,256]{1,0:T(8,128)(2,1)S(1)}, bf16[64,256]{1,0:T(8,128)(2,1)S(1)}, u32[]{:S(2)}, u32[]{:S(2)}) collective-permute-start(bf16[64,256]{1,0:T(8,128)(2,1)S(1)} %get-tuple-element.60), channel_id=1, source_target_pairs={{4,8},{8,4},{12,16},{16,12},{20,24},{24,20},{28,32},{32,28},{36,40... | collective-permute-start | bytes 98312 | tf_op jit(solution)/shard_map/ppermute | solution.py:99
  4.4 2.5 %collective-permute-start.1 = (bf16[64,256]{1,0:T(8,128)(2,1)S(1)}, bf16[64,256]{1,0:T(8,128)(2,1)S(1)}, u32[]{:S(2)}, u32[]{:S(2)}) collective-permute-start(bf16[64,256]{1,0:T(8,128)(2,1)S(1)} %get-tuple-element.61), channel_id=1, source_target_pairs={{1,2},{2,1},{3,0},{0,3},{5,6},{6,5},{7,4},{4,7},{9,10},{10,9},{11,... | collective-permute-start | bytes 98312 | tf_op jit(solution)/shard_map/ppermute | solution.py:99
  6.9 7.1 %collective-permute-start.3 = (bf16[64,256]{1,0:T(8,128)(2,1)S(1)}, bf16[64,256]{1,0:T(8,128)(2,1)S(1)}, u32[]{:S(2)}, u32[]{:S(2)}) collective-permute-start(bf16[64,256]{1,0:T(8,128)(2,1)S(1)} %get-tuple-element.63), channel_id=1, source_target_pairs={{0,4},{4,0},{1,5},{5,1},{2,6},{6,2},{3,7},{7,3},{8,12},{12,8},{9,1... | collective-permute-start | bytes 98312 | tf_op jit(solution)/shard_map/ppermute | solution.py:82
  13.9 1.6 %shard_map.77 = (bf16[1024,1024]{1,0:T(8,128)(2,1)S(1)}, f32[8,1024]{1,0:T(8,128)S(1)}, f32[8,256]{1,0:T(8,128)S(1)}) custom-call(f32[1,2]{1,0:T(1,128)} %bitcast.9, bf16[1024,1024]{1,0:T(8,128)(2,1)} %bitcast.4, f32[1,256]{1,0:T(1,128)} %row_hbm.1), custom_call_target="tpu_custom_call" | custom-call | tf_op jit(solution)/shard_map/pallas_call | solution.py:77
  16.2 2.0 %shard_map.80 = (f32[272,256]{1,0:T(8,128)S(1)}, f32[272,256]{1,0:T(8,128)S(1)}, bf16[512,1024]{1,0:T(8,128)(2,1)S(1)}) custom-call(f32[16,1024]{1,0:T(8,128)S(1)} %get-tuple-element.67.load0, f32[16,1024]{1,0:T(8,128)S(1)} %get-tuple-element.72.image, bf16[160,1024]{1,0:T(8,128)(2,1)S(1)} %get-tuple-element.73.wide_in, ...), custom_call_target="tpu_custom_call" | custom-call | tf_op jit(solution)/shard_map/pallas_call | solution.py:77
  18.2 1.9 %collective-permute-start.8 = (f32[272,256]{1,0:T(8,128)S(1)}, f32[272,256]{1,0:T(8,128)S(1)}, u32[]{:S(2)}, u32[]{:S(2)}) collective-permute-start(f32[272,256]{1,0:T(8,128)S(1)} %get-tuple-element.77), channel_id=1, source_target_pairs={{0,4},{4,0},{1,5},{5,1},{2,6},{6,2},{3,7},{7,3},{8,12},{12,8},{9,1... | collective-permute-start | bytes 835592 | tf_op jit(solution)/shard_map/ppermute | solution.py:82
  21.1 2.3 %collective-permute-start.7 = (f32[16,256]{1,0:T(8,128)S(1)}, f32[16,256]{1,0:T(8,128)S(1)}, u32[]{:S(2)}, u32[]{:S(2)}) collective-permute-start(f32[16,256]{1,0:T(8,128)S(1)} %get-tuple-element.71), channel_id=1, source_target_pairs={{0,4},{4,0},{1,5},{5,1},{2,6},{6,2},{3,7},{7,3},{8,12},{12,8},{9,1... | collective-permute-start | bytes 49160 | tf_op jit(solution)/shard_map/ppermute | solution.py:82
  24.2 1.5 %shard_map.81 = (f32[16,1024]{1,0:T(8,128)S(1)}, f32[16,1024]{1,0:T(8,128)S(1)}, f32[16,1024]{1,0:T(8,128)S(1)}, bf16[288,256]{1,0:T(8,128)(2,1)S(1)}, bf16[288,...) custom-call(f32[8,1024]{1,0:T(8,128)S(1)} %get-tuple-element.58.coef, ...), custom_call_target="tpu_custom_call" | custom-call | tf_op jit(solution)/shard_map/pallas_call | solution.py:77
  25.7 11.4 %all_to_all.25.got = bf16[16,24,256]{2,1,0:T(8,128)(2,1)S(1)} all-to-all(bf16[16,24,256]{2,1,0:T(8,128)(2,1)} %get-tuple-element.78), channel_id=1, replica_groups=mesh['z'=8,'y'=4,'core'=2,'x'=4] {'y','x'}, dimensions={0} | all-to-all | bytes 393216 | tf_op jit(solution)/shard_map/all_to_all | solution.py:86
  37.1 12.6 %all_to_all.26.got = bf16[8,24,256]{2,1,0:T(8,128)(2,1)S(1)} all-to-all(bf16[8,24,256]{2,1,0:T(8,128)(2,1)S(1)} %shard_map.82), channel_id=1, replica_groups=mesh['z'=8,'y'=4,'core'=2,'x'=4] {'z'}, dimensions={0} | all-to-all | bytes 196608 | tf_op jit(solution)/shard_map/all_to_all | solution.py:86
  50.5 3.5 %all-to-all-start.2 = ((bf16[16,40,256]{2,1,0:T(8,128)(2,1)}), bf16[16,40,256]{2,1,0:T(8,128)(2,1)S(1)}, u32[]{:S(2)}, u32[]{:S(2)}) async-start(bf16[16,40,256]{2,1,0:T(8,128)(2,1)} %shard_map.83), calls=%async_computation.2 | async-start | bytes 655360 | tf_op jit(solution)/shard_map/all_to_all | solution.py:86
  54.0 4.0 %collective-permute-start.10 = (bf16[288,256]{1,0:T(8,128)(2,1)S(1)}, bf16[288,256]{1,0:T(8,128)(2,1)S(1)}, u32[]{:S(2)}, u32[]{:S(2)}) collective-permute-start(bf16[288,256]{1,0:T(8,128)(2,1)S(1)} %get-tuple-element.82), channel_id=1, source_target_pairs={{4,8},{8,4},{12,16},{16,12},{20,24},{24,20},{28,32},{32,28},{36,40... | collective-permute-start | bytes 442376 | tf_op jit(solution)/shard_map/ppermute | solution.py:99
  58.0 2.4 %collective-permute-start.11 = (bf16[288,256]{1,0:T(8,128)(2,1)S(1)}, bf16[288,256]{1,0:T(8,128)(2,1)S(1)}, u32[]{:S(2)}, u32[]{:S(2)}) collective-permute-start(bf16[288,256]{1,0:T(8,128)(2,1)S(1)} %get-tuple-element.83), channel_id=1, source_target_pairs={{1,2},{2,1},{3,0},{0,3},{5,6},{6,5},{7,4},{4,7},{9,10},{10,9},{11,... | collective-permute-start | bytes 442376 | tf_op jit(solution)/shard_map/ppermute | solution.py:99
  60.4 1.5 %all-to-all-done.2.got = bf16[16,40,256]{2,1,0:T(8,128)(2,1)S(1)} async-done(((bf16[16,40,256]{2,1,0:T(8,128)(2,1)}), bf16[16,40,256]{2,1,0:T(8,128)(2,1)S(1)}, u32[]{:S(2)}, u32[]{:S(2)}) %all-to-all-start.2) | async-done | bytes 327712 | tf_op jit(solution)/shard_map/all_to_all | solution.py:86
  62.0 5.1 %collective-permute-start.9 = (bf16[576,256]{1,0:T(8,128)(2,1)S(1)}, bf16[576,256]{1,0:T(8,128)(2,1)S(1)}, u32[]{:S(2)}, u32[]{:S(2)}) collective-permute-start(bf16[576,256]{1,0:T(8,128)(2,1)S(1)} %shard_map.84.own), channel_id=1, source_target_pairs={{0,4},{4,0},{1,5},{5,1},{2,6},{6,2},{3,7},{7,3},{8,12},{12,8},{9,1... | collective-permute-start | bytes 884744 | tf_op jit(solution)/shard_map/ppermute | solution.py:82
  67.1 3.9 %shard_map.85 = (f32[16,1024]{1,0:T(8,128)S(1)}, bf16[512,1024]{1,0:T(8,128)(2,1)}, f32[16,1024]{1,0:T(8,128)S(1)}, bf16[256,1024]{1,0:T(8,128)(2,1)S(1)}, bf16[...) custom-call(bf16[288,256]{1,0:T(8,128)(2,1)S(1)} %collective-permute-done.1, ...), custom_call_target="tpu_custom_call" | custom-call | tf_op jit(solution)/shard_map/pallas_call | solution.py:77
  72.2 1.7 %collective-permute-start.17 = (bf16[288,256]{1,0:T(8,128)(2,1)}, bf16[288,256]{1,0:T(8,128)(2,1)S(1)}, u32[]{:S(2)}, u32[]{:S(2)}) collective-permute-start(bf16[288,256]{1,0:T(8,128)(2,1)} %get-tuple-element.91), channel_id=1, source_target_pairs={{0,4},{4,0},{1,5},{5,1},{2,6},{6,2},{3,7},{7,3},{8,12},{12,8},{9,1... | collective-permute-start | bytes 442376 | tf_op jit(solution)/shard_map/ppermute | solution.py:82
  73.9 2.0 %collective-permute-done.14.n0 = bf16[288,256]{1,0:T(8,128)(2,1)S(1)} collective-permute-done((bf16[288,256]{1,0:T(8,128)(2,1)}, bf16[288,256]{1,0:T(8,128)(2,1)S(1)}, u32[]{:S(2)}, u32[]{:S(2)}) %collective-permute-start.14) | collective-permute-done | bytes 147488 | tf_op jit(solution)/shard_map/ppermute | solution.py:99
  77.5 2.3 %shard_map.87 = (bf16[512,256]{1,0:T(8,128)(2,1)S(1)}, bf16[256,256]{1,0:T(8,128)(2,1)S(1)}, f32[16,256]{1,0:T(8,128)S(1)}, f32[16,256]{1,0:T(8,128)S(1)}, f32[1...) custom-call(f32[8,1024]{1,0:T(8,128)S(1)} %get-tuple-element.58.coef, ...), custom_call_target="tpu_custom_call" | custom-call | tf_op jit(solution)/shard_map/pallas_call | solution.py:77
  80.3 2.1 %collective-permute-start.20 = (f32[32,256]{1,0:T(8,128)S(1)}, f32[32,256]{1,0:T(8,128)S(1)}, u32[]{:S(2)}, u32[]{:S(2)}) collective-permute-start(f32[32,256]{1,0:T(8,128)S(1)} %get-tuple-element.106), channel_id=1, source_target_pairs={{0,4},{4,0},{1,5},{5,1},{2,6},{6,2},{3,7},{7,3},{8,12},{12,8},{9,1... | collective-permute-start | bytes 98312 | tf_op jit(solution)/shard_map/ppermute | solution.py:82
  84.0 1.6 %collective-permute-done.18.n0 = f32[16,256]{1,0:T(8,128)S(1)} collective-permute-done((f32[16,256]{1,0:T(8,128)S(1)}, f32[16,256]{1,0:T(8,128)S(1)}, u32[]{:S(2)}, u32[]{:S(2)}) %collective-permute-start.18) | collective-permute-done | bytes 16416 | tf_op jit(solution)/shard_map/ppermute | solution.py:82
  85.8 15.2 %all_to_all.27.got = bf16[16,40,256]{2,1,0:T(8,128)(2,1)S(1)} all-to-all(bf16[16,40,256]{2,1,0:T(8,128)(2,1)S(1)} %get-tuple-element.107), channel_id=1, replica_groups=mesh['z'=8,'y'=4,'core'=2,'x'=4] {'y','x'}, dimensions={0} | all-to-all | bytes 655360 | tf_op jit(solution)/shard_map/all_to_all | solution.py:86
  101.1 12.4 %all_to_all.28.got = bf16[8,40,256]{2,1,0:T(8,128)(2,1)S(1)} all-to-all(bf16[8,40,256]{2,1,0:T(8,128)(2,1)S(1)} %shard_map.90), channel_id=1, replica_groups=mesh['z'=8,'y'=4,'core'=2,'x'=4] {'z'}, dimensions={0} | all-to-all | bytes 327680 | tf_op jit(solution)/shard_map/all_to_all | solution.py:86
  113.5 2.3 %collective-permute-start.21 = (f32[40,256]{1,0:T(8,128)S(1)}, f32[40,256]{1,0:T(8,128)S(1)}, u32[]{:S(2)}, u32[]{:S(2)}) collective-permute-start(f32[40,256]{1,0:T(8,128)S(1)} %shard_map.91.own), channel_id=1, source_target_pairs={{0,4},{4,0},{1,5},{5,1},{2,6},{6,2},{3,7},{7,3},{8,12},{12,8},{9,1... | collective-permute-start | bytes 122888 | tf_op jit(solution)/shard_map/ppermute | solution.py:82
  (43 shorter events, 11.5 us)
Async XLA Ops:
  1.6 14.0 %collective-permute-start = (bf16[64,256]{1,0:T(8,128)(2,1)S(1)}, bf16[64,256]{1,0:T(8,128)(2,1)S(1)}, u32[]{:S(2)}, u32[]{:S(2)}) collective-permute-start(bf16[64,256]{1,0:T(8,128)(2,1)S(1)} %get-tuple-element.60), channel_id=1, source_target_pairs={{4,8},{8,4},{12,16},{16,12},{20,24},{24,20},{28,32},{32,28},{36,40... | collective-permute-start | bytes 98312 | tf_op jit(solution)/shard_map/ppermute | solution.py:99
  4.4 11.2 %collective-permute-start.1 = (bf16[64,256]{1,0:T(8,128)(2,1)S(1)}, bf16[64,256]{1,0:T(8,128)(2,1)S(1)}, u32[]{:S(2)}, u32[]{:S(2)}) collective-permute-start(bf16[64,256]{1,0:T(8,128)(2,1)S(1)} %get-tuple-element.61), channel_id=1, source_target_pairs={{1,2},{2,1},{3,0},{0,3},{5,6},{6,5},{7,4},{4,7},{9,10},{10,9},{11,... | collective-permute-start | bytes 98312 | tf_op jit(solution)/shard_map/ppermute | solution.py:99
  6.9 8.7 %collective-permute-start.2 = (bf16[64,256]{1,0:T(8,128)(2,1)S(1)}, bf16[64,256]{1,0:T(8,128)(2,1)S(1)}, u32[]{:S(2)}, u32[]{:S(2)}) collective-permute-start(bf16[64,256]{1,0:T(8,128)(2,1)S(1)} %get-tuple-element.62), channel_id=1, source_target_pairs={{0,1},{1,0},{2,3},{3,2},{4,5},{5,4},{6,7},{7,6},{8,9},{9,8},{10,11... | collective-permute-start | bytes 98312 | tf_op jit(solution)/shard_map/ppermute | solution.py:99
  6.9 8.8 %collective-permute-start.3 = (bf16[64,256]{1,0:T(8,128)(2,1)S(1)}, bf16[64,256]{1,0:T(8,128)(2,1)S(1)}, u32[]{:S(2)}, u32[]{:S(2)}) collective-permute-start(bf16[64,256]{1,0:T(8,128)(2,1)S(1)} %get-tuple-element.63), channel_id=1, source_target_pairs={{0,4},{4,0},{1,5},{5,1},{2,6},{6,2},{3,7},{7,3},{8,12},{12,8},{9,1... | collective-permute-start | bytes 98312 | tf_op jit(solution)/shard_map/ppermute | solution.py:82
  18.2 6.0 %collective-permute-start.8 = (f32[272,256]{1,0:T(8,128)S(1)}, f32[272,256]{1,0:T(8,128)S(1)}, u32[]{:S(2)}, u32[]{:S(2)}) collective-permute-start(f32[272,256]{1,0:T(8,128)S(1)} %get-tuple-element.77), channel_id=1, source_target_pairs={{0,4},{4,0},{1,5},{5,1},{2,6},{6,2},{3,7},{7,3},{8,12},{12,8},{9,1... | collective-permute-start | bytes 835592 | tf_op jit(solution)/shard_map/ppermute | solution.py:82
  20.2 3.2 %collective-permute-start.4 = (f32[16,256]{1,0:T(8,128)S(1)}, f32[16,256]{1,0:T(8,128)S(1)}, u32[]{:S(2)}, u32[]{:S(2)}) collective-permute-start(f32[16,256]{1,0:T(8,128)S(1)} %get-tuple-element.68), channel_id=1, source_target_pairs={{4,8},{8,4},{12,16},{16,12},{20,24},{24,20},{28,32},{32,28},{36,40... | collective-permute-start | bytes 49160 | tf_op jit(solution)/shard_map/ppermute | solution.py:99
  20.2 3.8 %collective-permute-start.5 = (f32[16,256]{1,0:T(8,128)S(1)}, f32[16,256]{1,0:T(8,128)S(1)}, u32[]{:S(2)}, u32[]{:S(2)}) collective-permute-start(f32[16,256]{1,0:T(8,128)S(1)} %get-tuple-element.69), channel_id=1, source_target_pairs={{1,2},{2,1},{3,0},{0,3},{5,6},{6,5},{7,4},{4,7},{9,10},{10,9},{11,... | collective-permute-start | bytes 49160 | tf_op jit(solution)/shard_map/ppermute | solution.py:99
  21.1 2.9 %collective-permute-start.6 = (f32[16,256]{1,0:T(8,128)S(1)}, f32[16,256]{1,0:T(8,128)S(1)}, u32[]{:S(2)}, u32[]{:S(2)}) collective-permute-start(f32[16,256]{1,0:T(8,128)S(1)} %get-tuple-element.70), channel_id=1, source_target_pairs={{0,1},{1,0},{2,3},{3,2},{4,5},{5,4},{6,7},{7,6},{8,9},{9,8},{10,11... | collective-permute-start | bytes 49160 | tf_op jit(solution)/shard_map/ppermute | solution.py:99
  21.1 3.1 %collective-permute-start.7 = (f32[16,256]{1,0:T(8,128)S(1)}, f32[16,256]{1,0:T(8,128)S(1)}, u32[]{:S(2)}, u32[]{:S(2)}) collective-permute-start(f32[16,256]{1,0:T(8,128)S(1)} %get-tuple-element.71), channel_id=1, source_target_pairs={{0,4},{4,0},{1,5},{5,1},{2,6},{6,2},{3,7},{7,3},{8,12},{12,8},{9,1... | collective-permute-start | bytes 49160 | tf_op jit(solution)/shard_map/ppermute | solution.py:82
  50.5 11.4 %all-to-all-start.2 = ((bf16[16,40,256]{2,1,0:T(8,128)(2,1)}), bf16[16,40,256]{2,1,0:T(8,128)(2,1)S(1)}, u32[]{:S(2)}, u32[]{:S(2)}) async-start(bf16[16,40,256]{2,1,0:T(8,128)(2,1)} %shard_map.83), calls=%async_computation.2 | async-start | bytes 655360 | tf_op jit(solution)/shard_map/all_to_all | solution.py:86
  54.0 13.0 %collective-permute-start.10 = (bf16[288,256]{1,0:T(8,128)(2,1)S(1)}, bf16[288,256]{1,0:T(8,128)(2,1)S(1)}, u32[]{:S(2)}, u32[]{:S(2)}) collective-permute-start(bf16[288,256]{1,0:T(8,128)(2,1)S(1)} %get-tuple-element.82), channel_id=1, source_target_pairs={{4,8},{8,4},{12,16},{16,12},{20,24},{24,20},{28,32},{32,28},{36,40... | collective-permute-start | bytes 442376 | tf_op jit(solution)/shard_map/ppermute | solution.py:99
  58.0 9.0 %collective-permute-start.11 = (bf16[288,256]{1,0:T(8,128)(2,1)S(1)}, bf16[288,256]{1,0:T(8,128)(2,1)S(1)}, u32[]{:S(2)}, u32[]{:S(2)}) collective-permute-start(bf16[288,256]{1,0:T(8,128)(2,1)S(1)} %get-tuple-element.83), channel_id=1, source_target_pairs={{1,2},{2,1},{3,0},{0,3},{5,6},{6,5},{7,4},{4,7},{9,10},{10,9},{11,... | collective-permute-start | bytes 442376 | tf_op jit(solution)/shard_map/ppermute | solution.py:99
  60.4 6.6 %collective-permute-start.12 = (bf16[288,256]{1,0:T(8,128)(2,1)S(1)}, bf16[288,256]{1,0:T(8,128)(2,1)S(1)}, u32[]{:S(2)}, u32[]{:S(2)}) collective-permute-start(bf16[288,256]{1,0:T(8,128)(2,1)S(1)} %get-tuple-element.84), channel_id=1, source_target_pairs={{0,1},{1,0},{2,3},{3,2},{4,5},{5,4},{6,7},{7,6},{8,9},{9,8},{10,11... | collective-permute-start | bytes 442376 | tf_op jit(solution)/shard_map/ppermute | solution.py:99
  60.4 6.6 %collective-permute-start.13 = (bf16[288,256]{1,0:T(8,128)(2,1)S(1)}, bf16[288,256]{1,0:T(8,128)(2,1)S(1)}, u32[]{:S(2)}, u32[]{:S(2)}) collective-permute-start(bf16[288,256]{1,0:T(8,128)(2,1)S(1)} %get-tuple-element.85), channel_id=1, source_target_pairs={{0,4},{4,0},{1,5},{5,1},{2,6},{6,2},{3,7},{7,3},{8,12},{12,8},{9,1... | collective-permute-start | bytes 442376 | tf_op jit(solution)/shard_map/ppermute | solution.py:82
  62.0 15.5 %collective-permute-start.9 = (bf16[576,256]{1,0:T(8,128)(2,1)S(1)}, bf16[576,256]{1,0:T(8,128)(2,1)S(1)}, u32[]{:S(2)}, u32[]{:S(2)}) collective-permute-start(bf16[576,256]{1,0:T(8,128)(2,1)S(1)} %shard_map.84.own), channel_id=1, source_target_pairs={{0,4},{4,0},{1,5},{5,1},{2,6},{6,2},{3,7},{7,3},{8,12},{12,8},{9,1... | collective-permute-start | bytes 884744 | tf_op jit(solution)/shard_map/ppermute | solution.py:82
  71.0 4.9 %collective-permute-start.14 = (bf16[288,256]{1,0:T(8,128)(2,1)}, bf16[288,256]{1,0:T(8,128)(2,1)S(1)}, u32[]{:S(2)}, u32[]{:S(2)}) collective-permute-start(bf16[288,256]{1,0:T(8,128)(2,1)} %get-tuple-element.88), channel_id=1, source_target_pairs={{4,8},{8,4},{12,16},{16,12},{20,24},{24,20},{28,32},{32,28},{36,40... | collective-permute-start | bytes 442376 | tf_op jit(solution)/shard_map/ppermute | solution.py:99
  71.4 5.8 %collective-permute-start.15 = (bf16[288,256]{1,0:T(8,128)(2,1)}, bf16[288,256]{1,0:T(8,128)(2,1)S(1)}, u32[]{:S(2)}, u32[]{:S(2)}) collective-permute-start(bf16[288,256]{1,0:T(8,128)(2,1)} %get-tuple-element.89), channel_id=1, source_target_pairs={{1,2},{2,1},{3,0},{0,3},{5,6},{6,5},{7,4},{4,7},{9,10},{10,9},{11,... | collective-permute-start | bytes 442376 | tf_op jit(solution)/shard_map/ppermute | solution.py:99
  72.1 5.1 %collective-permute-start.16 = (bf16[288,256]{1,0:T(8,128)(2,1)}, bf16[288,256]{1,0:T(8,128)(2,1)S(1)}, u32[]{:S(2)}, u32[]{:S(2)}) collective-permute-start(bf16[288,256]{1,0:T(8,128)(2,1)} %get-tuple-element.90), channel_id=1, source_target_pairs={{0,1},{1,0},{2,3},{3,2},{4,5},{5,4},{6,7},{7,6},{8,9},{9,8},{10,11... | collective-permute-start | bytes 442376 | tf_op jit(solution)/shard_map/ppermute | solution.py:99
  72.2 5.0 %collective-permute-start.17 = (bf16[288,256]{1,0:T(8,128)(2,1)}, bf16[288,256]{1,0:T(8,128)(2,1)S(1)}, u32[]{:S(2)}, u32[]{:S(2)}) collective-permute-start(bf16[288,256]{1,0:T(8,128)(2,1)} %get-tuple-element.91), channel_id=1, source_target_pairs={{0,4},{4,0},{1,5},{5,1},{2,6},{6,2},{3,7},{7,3},{8,12},{12,8},{9,1... | collective-permute-start | bytes 442376 | tf_op jit(solution)/shard_map/ppermute | solution.py:82
  80.3 5.3 %collective-permute-start.20 = (f32[32,256]{1,0:T(8,128)S(1)}, f32[32,256]{1,0:T(8,128)S(1)}, u32[]{:S(2)}, u32[]{:S(2)}) collective-permute-start(f32[32,256]{1,0:T(8,128)S(1)} %get-tuple-element.106), channel_id=1, source_target_pairs={{0,4},{4,0},{1,5},{5,1},{2,6},{6,2},{3,7},{7,3},{8,12},{12,8},{9,1... | collective-permute-start | bytes 98312 | tf_op jit(solution)/shard_map/ppermute | solution.py:82
  82.4 3.2 %collective-permute-start.18 = (f32[16,256]{1,0:T(8,128)S(1)}, f32[16,256]{1,0:T(8,128)S(1)}, u32[]{:S(2)}, u32[]{:S(2)}) collective-permute-start(f32[16,256]{1,0:T(8,128)S(1)} %get-tuple-element.103), channel_id=1, source_target_pairs={{0,252},{4,0},{8,4},{12,8},{16,12},{20,16},{24,20},{28,24},{32,28}... | collective-permute-start | bytes 49160 | tf_op jit(solution)/shard_map/ppermute | solution.py:82
  82.5 3.1 %collective-permute-start.19 = (f32[16,256]{1,0:T(8,128)S(1)}, f32[16,256]{1,0:T(8,128)S(1)}, u32[]{:S(2)}, u32[]{:S(2)}) collective-permute-start(f32[16,256]{1,0:T(8,128)S(1)} %get-tuple-element.104), channel_id=1, source_target_pairs={{0,3},{1,0},{2,1},{3,2},{4,7},{5,4},{6,5},{7,6},{8,11},{9,8},{10,9... | collective-permute-start | bytes 49160 | tf_op jit(solution)/shard_map/ppermute | solution.py:82
  113.5 3.1 %collective-permute-start.21 = (f32[40,256]{1,0:T(8,128)S(1)}, f32[40,256]{1,0:T(8,128)S(1)}, u32[]{:S(2)}, u32[]{:S(2)}) collective-permute-start(f32[40,256]{1,0:T(8,128)S(1)} %shard_map.91.own), channel_id=1, source_target_pairs={{0,4},{4,0},{1,5},{5,1},{2,6},{6,2},{3,7},{7,3},{8,12},{12,8},{9,1... | collective-permute-start | bytes 122888 | tf_op jit(solution)/shard_map/ppermute | solution.py:82

commit v5 on v4

--- a/solution.py
+++ b/solution.py
@@ -262,7 +262,7 @@
     pairs0 = bdot(wide, wide, NT) * 0.5
     wide_image = bdot(wide, inverse[...])
     top, low = halves_of(wide_image)
-    top, low = halves_of(bdot(spread_t, top) + bdot(spread_t, low))
+    top, low = halves_of(bdot(spread_t, top))
     lifted_image[:NCO] = top
     lifted_image[NCO:] = low
     pairs1 = dot2(wide_image, wide, NT)
@@ -403,14 +403,21 @@
     return coef[0:1, :width], coef[1:2, :width], coef[2:3, :width]
 
 
+def fetch2_kernel(after, chain1_hbm, inverse_hbm, chain1, inverse, sems):
+    copies = [
+        pltpu.make_async_copy(chain1_hbm, chain1, sems.at[0]),
+        pltpu.make_async_copy(inverse_hbm, inverse, sems.at[1]),
+    ]
+    for copy in copies:
+        copy.start()
+    for copy in copies:
+        copy.wait()
+
+
 def march_kernel(
-    coef, own, got, load0, base1, jump0, jump1, jump2, chain2, spread, wide_in, chain1_hbm, inverse_hbm,
-    coarse, m0, w0, w1, w2, load1, load2, load3, image3, low_sub, low_grp, m1, g1, g2, chain1, inverse, sems,
+    coef, own, got, load0, base1, jump0, jump1, jump2, chain2, spread, wide_in, chain1, inverse,
+    coarse, m0, w0, w1, w2, load1, load2, load3, image3, low_sub, low_grp, m1, g1, g2,
 ):
-    table = pltpu.make_async_copy(chain1_hbm, chain1, sems.at[0])
-    table.start()
-    fetch = pltpu.make_async_copy(inverse_hbm, inverse, sems.at[1])
-    fetch.start()
 
     def put(first, second):
         for row, part in ((0, first), (128, second)):
@@ -437,7 +444,6 @@
     both = jnp.concatenate([z, z1, z2], axis=0)
     lift = lifted(both, wide_in[...], spread[:, :SLOTS])
     far = dot_halves(z, chain2[...])
-    table.wait()
     near = dot_halves(both[: 2 * RHS], chain1[...])
     centre, inv, alpha = terms_in(coef, WIDTH)
     x1 = base1[...] + inv * lift[:RHS]
@@ -449,7 +455,6 @@
     j2 = alpha * (jj1 + near[RHS:] - centre * j1) - jump0[...]
     x3 = alpha * (j2 + lift[2 * RHS :] - centre * x2) - x1
     load3[...] = x3
-    fetch.wait()
     u = bdot(x3.astype(BF16), inverse[...])
     image3[...] = u
     low_sub[...] = u[:, SEG[1]]
@@ -633,16 +638,21 @@
     near2 = neighbours(sends)
     (v,) = call(spread0_kernel, [((16, 40, NCO), BF16)], [exchange(v, "z")])
     (own,) = call(collect0_kernel, [((576, NCO), BF16)], [exchange(v, PLANE)])
+    got = swapped(own)
+    chain1, inverse = call(
+        fetch2_kernel,
+        [table, ((WIDTH, WIDTH), BF16)],
+        [own, chain1, local_inverse.reshape(WIDTH, WIDTH)],
+        [None, hbm, hbm],
+        [pltpu.SemaphoreType.DMA((2,))],
+    )
     jump2, chain2 = call(chain2_kernel, [load, table], [*near2, image_x2, lifted2])
 
     coarse, m0, w0, w1, w2, load1, load2, load3, image3, low_sub, low_grp = call(
         march_kernel,
         [((2 * NCO, NCO), BF16), ((NCO, NCO), BF16), small, small, small, load, load, load, load, face, face],
-        [coef, own, swapped(own), load0, base1, jump0, jump1, jump2, chain2, spread, wide, chain1,
-         local_inverse.reshape(WIDTH, WIDTH)],
-        [None] * 11 + [hbm, hbm],
-        [pltpu.VMEM((NCO, NCO), BF16), pltpu.VMEM((RHS, NCO), F32), pltpu.VMEM((RHS, NCO), F32),
-         pltpu.VMEM((2 * NCO, WIDTH), BF16), pltpu.VMEM((WIDTH, WIDTH), BF16), pltpu.SemaphoreType.DMA((2,))],
+        [coef, own, got, load0, base1, jump0, jump1, jump2, chain2, spread, wide, chain1, inverse],
+        scratch=[pltpu.VMEM((NCO, NCO), BF16), pltpu.VMEM((RHS, NCO), F32), pltpu.VMEM((RHS, NCO), F32)],
     )
     n0 = along(low_sub, SUB, -1)
     n2 = along(low_grp, "x", -1)

time: 119 us -> 119 us (level)
  Pallas kernels: 16.8 us -> 18.1 us
    pallas_call x17 -> x18, Pallas kernels: 16.8 us -> 18.1 us  [call(): return run(*args)]
  transfers between devices with their start and end apart: 23 -> 23, of which waited for: 7 -> 8; matrix products, arithmetic and copies ran while one was open for 0% -> 0% of each run, Pallas kernels for 6% -> 7%
where the time goes in v5:
time: 119 us
  blocking collectives  50.7 us (43%)
  starting transfers between devices  41.7 us (35%)
  Pallas kernels  18.1 us (15%)
  waiting for transfers between devices  7.42 us (6%)
    all_to_all x4, blocking collectives, exchange(): return lax.all_to_all(x, axis, split_axis=0, concat_axis=0, tiled=True)  50.7 us
    ppermute x10, starting transfers between devices, along(): return lax.ppermute(x, axis, [(i, (i + by) % count) for i in range(count)])  24.2 us
    pallas_call x18, Pallas kernels, call(): return run(*args)  18.1 us
    ppermute x12, starting transfers between devices, in_pairs(): return lax.ppermute(v, axis, pairs)  14 us
    ppermute x12, waiting for transfers between devices, in_pairs(): return lax.ppermute(v, axis, pairs)  4 us
    all_to_all x1, starting transfers between devices, exchange(): return lax.all_to_all(x, axis, split_axis=0, concat_axis=0, tiled=True)  3.54 us
  transfers between devices with their start and end apart: 23, of which 8 were waited for; matrix products, arithmetic and copies ran while one was open for 0% of the time, Pallas kernels for 7%

profile of v5, /device:TPU:1, one launch (start us, length us, event | category | flops | bytes accessed | tf_op | source)
XLA Modules:
  0.0 118.9 jit_solution(12487431503530570615)
XLA Ops:
  1.6 2.8 %collective-permute-start = (bf16[64,256]{1,0:T(8,128)(2,1)S(1)}, bf16[64,256]{1,0:T(8,128)(2,1)S(1)}, u32[]{:S(2)}, u32[]{:S(2)}) collective-permute-start(bf16[64,256]{1,0:T(8,128)(2,1)S(1)} %get-tuple-element.62), channel_id=1, source_target_pairs={{4,8},{8,4},{12,16},{16,12},{20,24},{24,20},{28,32},{32,28},{36,40... | collective-permute-start | bytes 98312 | tf_op jit(solution)/shard_map/ppermute | solution.py:99
  4.4 2.5 %collective-permute-start.1 = (bf16[64,256]{1,0:T(8,128)(2,1)S(1)}, bf16[64,256]{1,0:T(8,128)(2,1)S(1)}, u32[]{:S(2)}, u32[]{:S(2)}) collective-permute-start(bf16[64,256]{1,0:T(8,128)(2,1)S(1)} %get-tuple-element.63), channel_id=1, source_target_pairs={{1,2},{2,1},{3,0},{0,3},{5,6},{6,5},{7,4},{4,7},{9,10},{10,9},{11,... | collective-permute-start | bytes 98312 | tf_op jit(solution)/shard_map/ppermute | solution.py:99
  6.9 7.1 %collective-permute-start.3 = (bf16[64,256]{1,0:T(8,128)(2,1)S(1)}, bf16[64,256]{1,0:T(8,128)(2,1)S(1)}, u32[]{:S(2)}, u32[]{:S(2)}) collective-permute-start(bf16[64,256]{1,0:T(8,128)(2,1)S(1)} %get-tuple-element.65), channel_id=1, source_target_pairs={{0,4},{4,0},{1,5},{5,1},{2,6},{6,2},{3,7},{7,3},{8,12},{12,8},{9,1... | collective-permute-start | bytes 98312 | tf_op jit(solution)/shard_map/ppermute | solution.py:82
  13.9 1.6 %shard_map.77 = (bf16[1024,1024]{1,0:T(8,128)(2,1)S(1)}, f32[8,1024]{1,0:T(8,128)S(1)}, f32[8,256]{1,0:T(8,128)S(1)}) custom-call(f32[1,2]{1,0:T(1,128)} %bitcast.9, bf16[1024,1024]{1,0:T(8,128)(2,1)} %bitcast.4, f32[1,256]{1,0:T(1,128)} %row_hbm.1), custom_call_target="tpu_custom_call" | custom-call | tf_op jit(solution)/shard_map/pallas_call | solution.py:77
  16.2 1.7 %shard_map.80 = (f32[272,256]{1,0:T(8,128)S(1)}, f32[272,256]{1,0:T(8,128)S(1)}, bf16[512,1024]{1,0:T(8,128)(2,1)S(1)}) custom-call(f32[16,1024]{1,0:T(8,128)S(1)} %get-tuple-element.69.load0, f32[16,1024]{1,0:T(8,128)S(1)} %get-tuple-element.74.image, bf16[160,1024]{1,0:T(8,128)(2,1)S(1)} %get-tuple-element.75.wide_in, ...), custom_call_target="tpu_custom_call" | custom-call | tf_op jit(solution)/shard_map/pallas_call | solution.py:77
  17.9 2.1 %collective-permute-start.8 = (f32[272,256]{1,0:T(8,128)S(1)}, f32[272,256]{1,0:T(8,128)S(1)}, u32[]{:S(2)}, u32[]{:S(2)}) collective-permute-start(f32[272,256]{1,0:T(8,128)S(1)} %get-tuple-element.79), channel_id=1, source_target_pairs={{0,4},{4,0},{1,5},{5,1},{2,6},{6,2},{3,7},{7,3},{8,12},{12,8},{9,1... | collective-permute-start | bytes 835592 | tf_op jit(solution)/shard_map/ppermute | solution.py:82
  20.9 2.2 %collective-permute-start.7 = (f32[16,256]{1,0:T(8,128)S(1)}, f32[16,256]{1,0:T(8,128)S(1)}, u32[]{:S(2)}, u32[]{:S(2)}) collective-permute-start(f32[16,256]{1,0:T(8,128)S(1)} %get-tuple-element.73), channel_id=1, source_target_pairs={{0,4},{4,0},{1,5},{5,1},{2,6},{6,2},{3,7},{7,3},{8,12},{12,8},{9,1... | collective-permute-start | bytes 49160 | tf_op jit(solution)/shard_map/ppermute | solution.py:82
  25.4 11.5 %all_to_all.25.got = bf16[16,24,256]{2,1,0:T(8,128)(2,1)S(1)} all-to-all(bf16[16,24,256]{2,1,0:T(8,128)(2,1)} %get-tuple-element.80), channel_id=1, replica_groups=mesh['z'=8,'y'=4,'core'=2,'x'=4] {'y','x'}, dimensions={0} | all-to-all | bytes 393216 | tf_op jit(solution)/shard_map/all_to_all | solution.py:86
  36.9 12.6 %all_to_all.26.got = bf16[8,24,256]{2,1,0:T(8,128)(2,1)S(1)} all-to-all(bf16[8,24,256]{2,1,0:T(8,128)(2,1)S(1)} %shard_map.82), channel_id=1, replica_groups=mesh['z'=8,'y'=4,'core'=2,'x'=4] {'z'}, dimensions={0} | all-to-all | bytes 196608 | tf_op jit(solution)/shard_map/all_to_all | solution.py:86
  50.3 3.5 %all-to-all-start.2 = ((bf16[16,40,256]{2,1,0:T(8,128)(2,1)}), bf16[16,40,256]{2,1,0:T(8,128)(2,1)S(1)}, u32[]{:S(2)}, u32[]{:S(2)}) async-start(bf16[16,40,256]{2,1,0:T(8,128)(2,1)} %shard_map.83), calls=%async_computation.2 | async-start | bytes 655360 | tf_op jit(solution)/shard_map/all_to_all | solution.py:86
  53.9 4.0 %collective-permute-start.10 = (bf16[288,256]{1,0:T(8,128)(2,1)S(1)}, bf16[288,256]{1,0:T(8,128)(2,1)S(1)}, u32[]{:S(2)}, u32[]{:S(2)}) collective-permute-start(bf16[288,256]{1,0:T(8,128)(2,1)S(1)} %get-tuple-element.84), channel_id=1, source_target_pairs={{4,8},{8,4},{12,16},{16,12},{20,24},{24,20},{28,32},{32,28},{36,40... | collective-permute-start | bytes 442376 | tf_op jit(solution)/shard_map/ppermute | solution.py:99
  57.8 2.4 %collective-permute-start.11 = (bf16[288,256]{1,0:T(8,128)(2,1)S(1)}, bf16[288,256]{1,0:T(8,128)(2,1)S(1)}, u32[]{:S(2)}, u32[]{:S(2)}) collective-permute-start(bf16[288,256]{1,0:T(8,128)(2,1)S(1)} %get-tuple-element.85), channel_id=1, source_target_pairs={{1,2},{2,1},{3,0},{0,3},{5,6},{6,5},{7,4},{4,7},{9,10},{10,9},{11,... | collective-permute-start | bytes 442376 | tf_op jit(solution)/shard_map/ppermute | solution.py:99
  61.8 4.9 %collective-permute-start.9 = (bf16[576,256]{1,0:T(8,128)(2,1)S(1)}, bf16[576,256]{1,0:T(8,128)(2,1)S(1)}, u32[]{:S(2)}, u32[]{:S(2)}) collective-permute-start(bf16[576,256]{1,0:T(8,128)(2,1)S(1)} %shard_map.84.after.own), channel_id=1, source_target_pairs={{0,4},{4,0},{1,5},{5,1},{2,6},{6,2},{3,7},{7,3},{8,12},{12,8},{9,1... | collective-permute-start | bytes 884744 | tf_op jit(solution)/shard_map/ppermute | solution.py:82
  66.7 4.1 %shard_map.85 = (f32[16,1024]{1,0:T(8,128)S(1)}, bf16[512,1024]{1,0:T(8,128)(2,1)}, f32[16,1024]{1,0:T(8,128)S(1)}, bf16[256,1024]{1,0:T(8,128)(2,1)S(1)}, bf16[...) custom-call(bf16[288,256]{1,0:T(8,128)(2,1)S(1)} %collective-permute-done.1, ...), custom_call_target="tpu_custom_call" | custom-call | tf_op jit(solution)/shard_map/pallas_call | solution.py:77
  72.3 1.7 %collective-permute-start.17 = (bf16[288,256]{1,0:T(8,128)(2,1)}, bf16[288,256]{1,0:T(8,128)(2,1)S(1)}, u32[]{:S(2)}, u32[]{:S(2)}) collective-permute-start(bf16[288,256]{1,0:T(8,128)(2,1)} %get-tuple-element.93), channel_id=1, source_target_pairs={{0,4},{4,0},{1,5},{5,1},{2,6},{6,2},{3,7},{7,3},{8,12},{12,8},{9,1... | collective-permute-start | bytes 442376 | tf_op jit(solution)/shard_map/ppermute | solution.py:82
  73.9 1.8 %collective-permute-done.14.n0 = bf16[288,256]{1,0:T(8,128)(2,1)S(1)} collective-permute-done((bf16[288,256]{1,0:T(8,128)(2,1)}, bf16[288,256]{1,0:T(8,128)(2,1)S(1)}, u32[]{:S(2)}, u32[]{:S(2)}) %collective-permute-start.14) | collective-permute-done | bytes 147488 | tf_op jit(solution)/shard_map/ppermute | solution.py:99
  75.7 1.5 %collective-permute-done.15.n1 = bf16[288,256]{1,0:T(8,128)(2,1)S(1)} collective-permute-done((bf16[288,256]{1,0:T(8,128)(2,1)}, bf16[288,256]{1,0:T(8,128)(2,1)S(1)}, u32[]{:S(2)}, u32[]{:S(2)}) %collective-permute-start.15) | collective-permute-done | bytes 147488 | tf_op jit(solution)/shard_map/ppermute | solution.py:99
  77.5 1.9 %shard_map.87 = (bf16[512,1024]{1,0:T(8,128)(2,1)S(1)}, bf16[1024,1024]{1,0:T(8,128)(2,1)S(1)}) custom-call(bf16[576,256]{1,0:T(8,128)(2,1)S(1)} %shard_map.84.after.own, bf16[512,1024]{1,0:T(8,128)(2,1)} %get-tuple-element.98.chain1_hbm, bf16[1024,1024]{1,0:T(8,128)(2,1)} %bitcast.6), custom_call_target="tpu_custom_call" | custom-call | tf_op jit(solution)/shard_map/pallas_call | solution.py:77
  79.5 1.8 %shard_map.88 = (bf16[512,256]{1,0:T(8,128)(2,1)S(1)}, bf16[256,256]{1,0:T(8,128)(2,1)S(1)}, f32[16,256]{1,0:T(8,128)S(1)}, f32[16,256]{1,0:T(8,128)S(1)}, f32[1...) custom-call(f32[8,1024]{1,0:T(8,128)S(1)} %get-tuple-element.60.coef, ...), custom_call_target="tpu_custom_call" | custom-call | tf_op jit(solution)/shard_map/pallas_call | solution.py:77
  81.7 2.2 %collective-permute-start.20 = (f32[32,256]{1,0:T(8,128)S(1)}, f32[32,256]{1,0:T(8,128)S(1)}, u32[]{:S(2)}, u32[]{:S(2)}) collective-permute-start(f32[32,256]{1,0:T(8,128)S(1)} %get-tuple-element.110), channel_id=1, source_target_pairs={{0,4},{4,0},{1,5},{5,1},{2,6},{6,2},{3,7},{7,3},{8,12},{12,8},{9,1... | collective-permute-start | bytes 98312 | tf_op jit(solution)/shard_map/ppermute | solution.py:82
  85.4 1.6 %collective-permute-done.18.n0 = f32[16,256]{1,0:T(8,128)S(1)} collective-permute-done((f32[16,256]{1,0:T(8,128)S(1)}, f32[16,256]{1,0:T(8,128)S(1)}, u32[]{:S(2)}, u32[]{:S(2)}) %collective-permute-start.18) | collective-permute-done | bytes 16416 | tf_op jit(solution)/shard_map/ppermute | solution.py:82
  87.2 14.8 %all_to_all.27.got = bf16[16,40,256]{2,1,0:T(8,128)(2,1)S(1)} all-to-all(bf16[16,40,256]{2,1,0:T(8,128)(2,1)S(1)} %get-tuple-element.111), channel_id=1, replica_groups=mesh['z'=8,'y'=4,'core'=2,'x'=4] {'y','x'}, dimensions={0} | all-to-all | bytes 655360 | tf_op jit(solution)/shard_map/all_to_all | solution.py:86
  102.1 11.8 %all_to_all.28.got = bf16[8,40,256]{2,1,0:T(8,128)(2,1)S(1)} all-to-all(bf16[8,40,256]{2,1,0:T(8,128)(2,1)S(1)} %shard_map.91), channel_id=1, replica_groups=mesh['z'=8,'y'=4,'core'=2,'x'=4] {'z'}, dimensions={0} | all-to-all | bytes 327680 | tf_op jit(solution)/shard_map/all_to_all | solution.py:86
  113.9 2.7 %collective-permute-start.21 = (f32[40,256]{1,0:T(8,128)S(1)}, f32[40,256]{1,0:T(8,128)S(1)}, u32[]{:S(2)}, u32[]{:S(2)}) collective-permute-start(f32[40,256]{1,0:T(8,128)S(1)} %shard_map.92.own), channel_id=1, source_target_pairs={{0,4},{4,0},{1,5},{5,1},{2,6},{6,2},{3,7},{7,3},{8,12},{12,8},{9,1... | collective-permute-start | bytes 122888 | tf_op jit(solution)/shard_map/ppermute | solution.py:82
  (44 shorter events, 13.4 us)
Async XLA Ops:
  1.6 14.0 %collective-permute-start = (bf16[64,256]{1,0:T(8,128)(2,1)S(1)}, bf16[64,256]{1,0:T(8,128)(2,1)S(1)}, u32[]{:S(2)}, u32[]{:S(2)}) collective-permute-start(bf16[64,256]{1,0:T(8,128)(2,1)S(1)} %get-tuple-element.62), channel_id=1, source_target_pairs={{4,8},{8,4},{12,16},{16,12},{20,24},{24,20},{28,32},{32,28},{36,40... | collective-permute-start | bytes 98312 | tf_op jit(solution)/shard_map/ppermute | solution.py:99
  4.4 11.2 %collective-permute-start.1 = (bf16[64,256]{1,0:T(8,128)(2,1)S(1)}, bf16[64,256]{1,0:T(8,128)(2,1)S(1)}, u32[]{:S(2)}, u32[]{:S(2)}) collective-permute-start(bf16[64,256]{1,0:T(8,128)(2,1)S(1)} %get-tuple-element.63), channel_id=1, source_target_pairs={{1,2},{2,1},{3,0},{0,3},{5,6},{6,5},{7,4},{4,7},{9,10},{10,9},{11,... | collective-permute-start | bytes 98312 | tf_op jit(solution)/shard_map/ppermute | solution.py:99
  6.9 8.7 %collective-permute-start.2 = (bf16[64,256]{1,0:T(8,128)(2,1)S(1)}, bf16[64,256]{1,0:T(8,128)(2,1)S(1)}, u32[]{:S(2)}, u32[]{:S(2)}) collective-permute-start(bf16[64,256]{1,0:T(8,128)(2,1)S(1)} %get-tuple-element.64), channel_id=1, source_target_pairs={{0,1},{1,0},{2,3},{3,2},{4,5},{5,4},{6,7},{7,6},{8,9},{9,8},{10,11... | collective-permute-start | bytes 98312 | tf_op jit(solution)/shard_map/ppermute | solution.py:99
  6.9 8.8 %collective-permute-start.3 = (bf16[64,256]{1,0:T(8,128)(2,1)S(1)}, bf16[64,256]{1,0:T(8,128)(2,1)S(1)}, u32[]{:S(2)}, u32[]{:S(2)}) collective-permute-start(bf16[64,256]{1,0:T(8,128)(2,1)S(1)} %get-tuple-element.65), channel_id=1, source_target_pairs={{0,4},{4,0},{1,5},{5,1},{2,6},{6,2},{3,7},{7,3},{8,12},{12,8},{9,1... | collective-permute-start | bytes 98312 | tf_op jit(solution)/shard_map/ppermute | solution.py:82
  17.9 6.0 %collective-permute-start.8 = (f32[272,256]{1,0:T(8,128)S(1)}, f32[272,256]{1,0:T(8,128)S(1)}, u32[]{:S(2)}, u32[]{:S(2)}) collective-permute-start(f32[272,256]{1,0:T(8,128)S(1)} %get-tuple-element.79), channel_id=1, source_target_pairs={{0,4},{4,0},{1,5},{5,1},{2,6},{6,2},{3,7},{7,3},{8,12},{12,8},{9,1... | collective-permute-start | bytes 835592 | tf_op jit(solution)/shard_map/ppermute | solution.py:82
  20.0 3.2 %collective-permute-start.4 = (f32[16,256]{1,0:T(8,128)S(1)}, f32[16,256]{1,0:T(8,128)S(1)}, u32[]{:S(2)}, u32[]{:S(2)}) collective-permute-start(f32[16,256]{1,0:T(8,128)S(1)} %get-tuple-element.70), channel_id=1, source_target_pairs={{4,8},{8,4},{12,16},{16,12},{20,24},{24,20},{28,32},{32,28},{36,40... | collective-permute-start | bytes 49160 | tf_op jit(solution)/shard_map/ppermute | solution.py:99
  20.0 3.8 %collective-permute-start.5 = (f32[16,256]{1,0:T(8,128)S(1)}, f32[16,256]{1,0:T(8,128)S(1)}, u32[]{:S(2)}, u32[]{:S(2)}) collective-permute-start(f32[16,256]{1,0:T(8,128)S(1)} %get-tuple-element.71), channel_id=1, source_target_pairs={{1,2},{2,1},{3,0},{0,3},{5,6},{6,5},{7,4},{4,7},{9,10},{10,9},{11,... | collective-permute-start | bytes 49160 | tf_op jit(solution)/shard_map/ppermute | solution.py:99
  20.9 2.9 %collective-permute-start.6 = (f32[16,256]{1,0:T(8,128)S(1)}, f32[16,256]{1,0:T(8,128)S(1)}, u32[]{:S(2)}, u32[]{:S(2)}) collective-permute-start(f32[16,256]{1,0:T(8,128)S(1)} %get-tuple-element.72), channel_id=1, source_target_pairs={{0,1},{1,0},{2,3},{3,2},{4,5},{5,4},{6,7},{7,6},{8,9},{9,8},{10,11... | collective-permute-start | bytes 49160 | tf_op jit(solution)/shard_map/ppermute | solution.py:99
  20.9 3.0 %collective-permute-start.7 = (f32[16,256]{1,0:T(8,128)S(1)}, f32[16,256]{1,0:T(8,128)S(1)}, u32[]{:S(2)}, u32[]{:S(2)}) collective-permute-start(f32[16,256]{1,0:T(8,128)S(1)} %get-tuple-element.73), channel_id=1, source_target_pairs={{0,4},{4,0},{1,5},{5,1},{2,6},{6,2},{3,7},{7,3},{8,12},{12,8},{9,1... | collective-permute-start | bytes 49160 | tf_op jit(solution)/shard_map/ppermute | solution.py:82
  50.3 11.4 %all-to-all-start.2 = ((bf16[16,40,256]{2,1,0:T(8,128)(2,1)}), bf16[16,40,256]{2,1,0:T(8,128)(2,1)S(1)}, u32[]{:S(2)}, u32[]{:S(2)}) async-start(bf16[16,40,256]{2,1,0:T(8,128)(2,1)} %shard_map.83), calls=%async_computation.2 | async-start | bytes 655360 | tf_op jit(solution)/shard_map/all_to_all | solution.py:86
  53.9 12.8 %collective-permute-start.10 = (bf16[288,256]{1,0:T(8,128)(2,1)S(1)}, bf16[288,256]{1,0:T(8,128)(2,1)S(1)}, u32[]{:S(2)}, u32[]{:S(2)}) collective-permute-start(bf16[288,256]{1,0:T(8,128)(2,1)S(1)} %get-tuple-element.84), channel_id=1, source_target_pairs={{4,8},{8,4},{12,16},{16,12},{20,24},{24,20},{28,32},{32,28},{36,40... | collective-permute-start | bytes 442376 | tf_op jit(solution)/shard_map/ppermute | solution.py:99
  57.8 8.9 %collective-permute-start.11 = (bf16[288,256]{1,0:T(8,128)(2,1)S(1)}, bf16[288,256]{1,0:T(8,128)(2,1)S(1)}, u32[]{:S(2)}, u32[]{:S(2)}) collective-permute-start(bf16[288,256]{1,0:T(8,128)(2,1)S(1)} %get-tuple-element.85), channel_id=1, source_target_pairs={{1,2},{2,1},{3,0},{0,3},{5,6},{6,5},{7,4},{4,7},{9,10},{10,9},{11,... | collective-permute-start | bytes 442376 | tf_op jit(solution)/shard_map/ppermute | solution.py:99
  60.3 6.5 %collective-permute-start.12 = (bf16[288,256]{1,0:T(8,128)(2,1)S(1)}, bf16[288,256]{1,0:T(8,128)(2,1)S(1)}, u32[]{:S(2)}, u32[]{:S(2)}) collective-permute-start(bf16[288,256]{1,0:T(8,128)(2,1)S(1)} %get-tuple-element.86), channel_id=1, source_target_pairs={{0,1},{1,0},{2,3},{3,2},{4,5},{5,4},{6,7},{7,6},{8,9},{9,8},{10,11... | collective-permute-start | bytes 442376 | tf_op jit(solution)/shard_map/ppermute | solution.py:99
  60.3 6.5 %collective-permute-start.13 = (bf16[288,256]{1,0:T(8,128)(2,1)S(1)}, bf16[288,256]{1,0:T(8,128)(2,1)S(1)}, u32[]{:S(2)}, u32[]{:S(2)}) collective-permute-start(bf16[288,256]{1,0:T(8,128)(2,1)S(1)} %get-tuple-element.87), channel_id=1, source_target_pairs={{0,4},{4,0},{1,5},{5,1},{2,6},{6,2},{3,7},{7,3},{8,12},{12,8},{9,1... | collective-permute-start | bytes 442376 | tf_op jit(solution)/shard_map/ppermute | solution.py:82
  61.8 17.7 %collective-permute-start.9 = (bf16[576,256]{1,0:T(8,128)(2,1)S(1)}, bf16[576,256]{1,0:T(8,128)(2,1)S(1)}, u32[]{:S(2)}, u32[]{:S(2)}) collective-permute-start(bf16[576,256]{1,0:T(8,128)(2,1)S(1)} %shard_map.84.after.own), channel_id=1, source_target_pairs={{0,4},{4,0},{1,5},{5,1},{2,6},{6,2},{3,7},{7,3},{8,12},{12,8},{9,1... | collective-permute-start | bytes 884744 | tf_op jit(solution)/shard_map/ppermute | solution.py:82
  70.8 4.9 %collective-permute-start.14 = (bf16[288,256]{1,0:T(8,128)(2,1)}, bf16[288,256]{1,0:T(8,128)(2,1)S(1)}, u32[]{:S(2)}, u32[]{:S(2)}) collective-permute-start(bf16[288,256]{1,0:T(8,128)(2,1)} %get-tuple-element.90), channel_id=1, source_target_pairs={{4,8},{8,4},{12,16},{16,12},{20,24},{24,20},{28,32},{32,28},{36,40... | collective-permute-start | bytes 442376 | tf_op jit(solution)/shard_map/ppermute | solution.py:99
  71.4 5.8 %collective-permute-start.15 = (bf16[288,256]{1,0:T(8,128)(2,1)}, bf16[288,256]{1,0:T(8,128)(2,1)S(1)}, u32[]{:S(2)}, u32[]{:S(2)}) collective-permute-start(bf16[288,256]{1,0:T(8,128)(2,1)} %get-tuple-element.91), channel_id=1, source_target_pairs={{1,2},{2,1},{3,0},{0,3},{5,6},{6,5},{7,4},{4,7},{9,10},{10,9},{11,... | collective-permute-start | bytes 442376 | tf_op jit(solution)/shard_map/ppermute | solution.py:99
  72.1 5.1 %collective-permute-start.16 = (bf16[288,256]{1,0:T(8,128)(2,1)}, bf16[288,256]{1,0:T(8,128)(2,1)S(1)}, u32[]{:S(2)}, u32[]{:S(2)}) collective-permute-start(bf16[288,256]{1,0:T(8,128)(2,1)} %get-tuple-element.92), channel_id=1, source_target_pairs={{0,1},{1,0},{2,3},{3,2},{4,5},{5,4},{6,7},{7,6},{8,9},{9,8},{10,11... | collective-permute-start | bytes 442376 | tf_op jit(solution)/shard_map/ppermute | solution.py:99
  72.3 5.0 %collective-permute-start.17 = (bf16[288,256]{1,0:T(8,128)(2,1)}, bf16[288,256]{1,0:T(8,128)(2,1)S(1)}, u32[]{:S(2)}, u32[]{:S(2)}) collective-permute-start(bf16[288,256]{1,0:T(8,128)(2,1)} %get-tuple-element.93), channel_id=1, source_target_pairs={{0,4},{4,0},{1,5},{5,1},{2,6},{6,2},{3,7},{7,3},{8,12},{12,8},{9,1... | collective-permute-start | bytes 442376 | tf_op jit(solution)/shard_map/ppermute | solution.py:82
  81.7 5.3 %collective-permute-start.20 = (f32[32,256]{1,0:T(8,128)S(1)}, f32[32,256]{1,0:T(8,128)S(1)}, u32[]{:S(2)}, u32[]{:S(2)}) collective-permute-start(f32[32,256]{1,0:T(8,128)S(1)} %get-tuple-element.110), channel_id=1, source_target_pairs={{0,4},{4,0},{1,5},{5,1},{2,6},{6,2},{3,7},{7,3},{8,12},{12,8},{9,1... | collective-permute-start | bytes 98312 | tf_op jit(solution)/shard_map/ppermute | solution.py:82
  83.8 3.2 %collective-permute-start.18 = (f32[16,256]{1,0:T(8,128)S(1)}, f32[16,256]{1,0:T(8,128)S(1)}, u32[]{:S(2)}, u32[]{:S(2)}) collective-permute-start(f32[16,256]{1,0:T(8,128)S(1)} %get-tuple-element.107), channel_id=1, source_target_pairs={{0,252},{4,0},{8,4},{12,8},{16,12},{20,16},{24,20},{28,24},{32,28}... | collective-permute-start | bytes 49160 | tf_op jit(solution)/shard_map/ppermute | solution.py:82
  83.9 3.1 %collective-permute-start.19 = (f32[16,256]{1,0:T(8,128)S(1)}, f32[16,256]{1,0:T(8,128)S(1)}, u32[]{:S(2)}, u32[]{:S(2)}) collective-permute-start(f32[16,256]{1,0:T(8,128)S(1)} %get-tuple-element.108), channel_id=1, source_target_pairs={{0,3},{1,0},{2,1},{3,2},{4,7},{5,4},{6,5},{7,6},{8,11},{9,8},{10,9... | collective-permute-start | bytes 49160 | tf_op jit(solution)/shard_map/ppermute | solution.py:82
  113.9 3.5 %collective-permute-start.21 = (f32[40,256]{1,0:T(8,128)S(1)}, f32[40,256]{1,0:T(8,128)S(1)}, u32[]{:S(2)}, u32[]{:S(2)}) collective-permute-start(f32[40,256]{1,0:T(8,128)S(1)} %shard_map.92.own), channel_id=1, source_target_pairs={{0,4},{4,0},{1,5},{5,1},{2,6},{6,2},{3,7},{7,3},{8,12},{12,8},{9,1... | collective-permute-start | bytes 122888 | tf_op jit(solution)/shard_map/ppermute | solution.py:82
